TPU v7x, 32 devices: a whole 2x2x4 slice. The times are simulated.
32 devices in a mesh: gx: 2 (over core), gy: 4 (over z), gz: 4 (over y, x).
Axes of the slice: x: 2, y: 2, z: 4, core: 2. Of those that a mesh axis runs over, the one named last changes fastest.
Arguments:
- source: float32 [16, 64, 512], P('gx', 'gy', 'gz'), may hold values from -18 to 18
- pressure_old: float32 [16, 64, 512], P('gx', 'gy', 'gz'), may hold values from -6 to 6
- strain_prev: float32 [16, 64, 512], P('gx', 'gy', 'gz'), may hold values from -6 to 6
- motion_old: float32 [3, 16, 64, 512], P(None, 'gx', 'gy', 'gz'), may hold values from -6 to 6
- body_force: float32 [3, 16, 64, 512], P(None, 'gx', 'gy', 'gz'), may hold values from -6 to 6
- zone_ids: int32 [16, 64, 512], P('gx', 'gy', 'gz'), may hold values from 0 to 7
- drained: int32 [16, 64, 512], P('gx', 'gy', 'gz'), may hold values 0 or 1
- perm_table: float32 [8], replicated, may hold values from 0.1 to 3
- lame_table: float32 [8], replicated, may hold values from 0.5 to 4
- shear_table: float32 [8], replicated, may hold values from 0.3 to 2
Outputs:
- pressure: float32 [16, 64, 512], P('gx', 'gy', 'gz')
- motion: float32 [3, 16, 64, 512], P(None, 'gx', 'gy', 'gz')
- strain: float32 [16, 64, 512], P('gx', 'gy', 'gz')
All inputs are finite; a program needn't handle non-finite values. No bound on the sum of `drained` on one device may be relied on, other than what follows from the above.
Results may differ from a plain program's by a relative error of at most 0.0001.
Values sent between devices are 32-bit elements; how exact they have to be, the bound alone decides.
No kernel may reach another device: no remote copies, remote signals or barrier semaphores. Data moves between devices by JAX's collectives and lax.ppermute only.
A program may use at most 64 MiB of HBM per device.

v0:
```python
import jax
import jax.numpy as jnp
from jax import lax
from jax.sharding import PartitionSpec as P

ITERS = 2
ZONES = 8


storage = 0.2
biot_coef = 0.8
time_step = 1.0
leakage = 2.0
support = 1.0


def extended(shard, sides, width):
    for axis, dim in sides:
        peers, length = (lax.axis_size(axis), shard.shape[dim])
        up = [(i, (i + 1) % peers) for i in range(peers - 1)]
        down = [(j, i) for i, j in up]
        last = lax.slice_in_dim(shard, length - width, length, axis=dim)
        initial = lax.slice_in_dim(shard, 0, width, axis=dim)
        before = lax.ppermute(last, axis, up)
        after = lax.ppermute(initial, axis, down)
        shard = jnp.concatenate([before, shard, after], axis=dim)
    return shard


def lookup(zone_ids, lookup_table):
    result = jnp.zeros(zone_ids.shape, jnp.float32)
    for zone_index in range(ZONES):
        result = result + jnp.where(zone_ids == zone_index, lookup_table[zone_index], 0.0)
    return result


def interior(padded):
    return padded[..., 1:-1, 1:-1, 1:-1]


def neighbours(padded):
    return [
        padded[..., 2:, 1:-1, 1:-1],
        padded[..., :-2, 1:-1, 1:-1],
        padded[..., 1:-1, 2:, 1:-1],
        padded[..., 1:-1, :-2, 1:-1],
        padded[..., 1:-1, 1:-1, 2:],
        padded[..., 1:-1, 1:-1, :-2],
    ]


def harmonic(own_value, beside):
    return 2.0 * own_value * beside / (own_value + beside)


def central_div(motion_pad):
    return 0.5 * (
        motion_pad[0, 2:, 1:-1, 1:-1]
        - motion_pad[0, :-2, 1:-1, 1:-1]
        + (motion_pad[1, 1:-1, 2:, 1:-1] - motion_pad[1, 1:-1, :-2, 1:-1])
        + (motion_pad[2, 1:-1, 1:-1, 2:] - motion_pad[2, 1:-1, 1:-1, :-2])
    )


def central_grad(press_pad):
    sided = neighbours(press_pad)
    return jnp.stack(
        [0.5 * (sided[0] - sided[1]), 0.5 * (sided[2] - sided[3]), 0.5 * (sided[4] - sided[5])]
    )


def pressure_faces(values):
    return extended(values, (("gx", 0), ("gy", 1), ("gz", 2)), 1)


def motion_faces(values):
    return extended(values, (("gx", 1), ("gy", 2), ("gz", 3)), 1)


def products(residual, precond, image):
    return lax.psum((jnp.sum(residual * precond), jnp.sum(precond * image)), ("gx", "gy", "gz"))


def conjugate(start_pad, rhs, diag, apply_padded, faces):
    iterate = interior(start_pad)
    tracked = start_pad
    residual = rhs - apply_padded(start_pad)
    precond = residual / diag
    precond_pad = faces(precond)
    image = apply_padded(precond_pad)
    gamma_now, curvature = products(residual, precond, image)
    step_len = gamma_now / curvature
    direction = precond
    direction_pad = precond_pad
    along = image
    for iteration in range(ITERS):
        iterate = iterate + step_len * direction
        residual = residual - step_len * along
        tracked = tracked + step_len * direction_pad
        if iteration + 1 < ITERS:
            precond = residual / diag
            precond_pad = faces(precond)
            image = apply_padded(precond_pad)
            gamma_new, curvature = products(residual, precond, image)
            momentum = gamma_new / gamma_now
            step_len = gamma_new / (curvature - momentum * gamma_new / step_len)
            direction = precond + momentum * direction
            along = image + momentum * along
            direction_pad = precond_pad + momentum * direction_pad
            gamma_now = gamma_new
    return (iterate, tracked)


def shards(
    source,
    pressure_old,
    strain_prev,
    motion_old,
    body_force,
    zone_ids,
    drained,
    perm_table,
    lame_table,
    shear_table,
):
    permeability = lookup(zone_ids, perm_table)
    lame_first = lookup(zone_ids, lame_table)
    shear_mod = lookup(zone_ids, shear_table)
    fixed_term = biot_coef * biot_coef / (lame_first + 2.0 * shear_mod / 3.0)
    stacked = jnp.concatenate(
        [jnp.stack([permeability, lame_first + shear_mod, shear_mod, pressure_old]), motion_old], 0
    )
    padded = extended(stacked, (("gx", 1), ("gy", 2), ("gz", 3)), 1)
    perm_pad = padded[0]
    heft_pad = padded[1]
    shear_pad = padded[2]
    press_pad = padded[3]
    motion_pad = padded[4:7]
    transmit = [harmonic(permeability, beside) for beside in neighbours(perm_pad)]
    reaction = storage + fixed_term + leakage * drained.astype(jnp.float32)
    pdiag = reaction + time_step * sum(transmit)

    def apply_pressure(field_pad):
        center = interior(field_pad)
        flux = sum(
            (factor * (center - beside) for factor, beside in zip(transmit, neighbours(field_pad)))
        )
        return reaction * center + time_step * flux

    prhs = (
        source
        + (storage + fixed_term) * pressure_old
        - biot_coef * (central_div(motion_pad) - strain_prev)
    )
    pressure, pressure_kept = conjugate(press_pad, prhs, pdiag, apply_pressure, pressure_faces)
    heft = interior(heft_pad)
    shear_faces = [harmonic(shear_mod, beside) for beside in neighbours(shear_pad)]
    heft_sides = neighbours(heft_pad)
    base_diag = support + sum(shear_faces) + heft
    ediag = jnp.stack(
        [base_diag + heft_sides[1], base_diag + heft_sides[3], base_diag + heft_sides[5]]
    )

    def apply_motion(field_pad):
        center = interior(field_pad)
        spread = sum(
            (
                factor * (center - beside)
                for factor, beside in zip(shear_faces, neighbours(field_pad))
            )
        )
        diverg = (
            field_pad[0, 1:, :-1, :-1]
            - field_pad[0, :-1, :-1, :-1]
            + (field_pad[1, :-1, 1:, :-1] - field_pad[1, :-1, :-1, :-1])
            + (field_pad[2, :-1, :-1, 1:] - field_pad[2, :-1, :-1, :-1])
        )
        scaled = heft_pad[:-1, :-1, :-1] * diverg
        own_part = scaled[1:, 1:, 1:]
        push = jnp.stack(
            [
                scaled[:-1, 1:, 1:] - own_part,
                scaled[1:, :-1, 1:] - own_part,
                scaled[1:, 1:, :-1] - own_part,
            ]
        )
        return support * center + spread + push

    erhs = body_force - biot_coef * central_grad(pressure_kept)
    motion, motion_kept = conjugate(motion_pad, erhs, ediag, apply_motion, motion_faces)
    strain = central_div(motion_kept)
    return (pressure, motion, strain)


def solution(mesh):
    placed = (
        P("gx", "gy", "gz"),
        P("gx", "gy", "gz"),
        P("gx", "gy", "gz"),
        P(None, "gx", "gy", "gz"),
        P(None, "gx", "gy", "gz"),
        P("gx", "gy", "gz"),
        P("gx", "gy", "gz"),
        P(),
        P(),
        P(),
    )
    return jax.shard_map(
        shards,
        mesh=mesh,
        in_specs=placed,
        out_specs=(P("gx", "gy", "gz"), P(None, "gx", "gy", "gz"), P("gx", "gy", "gz")),
        check_vma=False,
    )
```

profile of v0, /device:TPU:0, one launch (start us, length us, event | category | flops | bytes accessed | tf_op | source)
XLA Modules:
  0.0 354.0 jit_solution(5678843765989169779)
XLA Ops:
  0.6 1.6 fusion.174
  3.6 6.7 %bitcast_dynamic-update-slice_fusion.3 = (f32[7,8,16,128]{3,2,1,0:T(8,128)S(1)}, f32[8,16,128]{2,1,0:T(8,128)}, pred[8,16,128]{2,1,0:T(8,128)(4,1)S(1)}, pred[8,...) fusion(f32[]{:T(128)} %bitcast.7, f32[]{:T(128)} %bitcast.6, ...), kind=kLoop, calls=%fused_computation.308 | loop fusion | flops 376831 | bytes 327712
  10.3 10.7 %bitcast_dynamic-update-slice_fusion.2 = (f32[7,8,16,128]{3,2,1,0:T(8,128)S(1)}, f32[8,16,128]{2,1,0:T(8,128)S(1)}, f32[8,16,128]{2,1,0:T(8,128)}) fusion(f32[7,8,16,128]{3,2,1,0:T(8,128)S(1)} %get-tuple-element.51, pred[8,16,128]{2,1,0:T(8,128)(4,1)S(1)} %get-tuple-element.60, f32[]{:T(128)} %bitcast.24, pred[8,16,128]{2,1,0:T(8,128)(4,1)S(1)} %get-tuple-element.59, ...), kind=kLoop, calls=%fused_computation.307 | loop fusion | flops 507904 | bytes 327744
  22.0 2.4 collective-permute-start
  24.4 1.3 collective-permute-start.1
  25.7 1.8 collective-permute-done.1
  27.6 4.3 %collective-permute-start.2 = (f32[7,10,1,128]{3,2,1,0:T(1,128)S(1)}, f32[7,10,1,128]{3,2,1,0:T(1,128)S(1)}, u32[]{:S(2)}, u32[]{:S(2)}) collective-permute-start(f32[7,10,1,128]{3,2,1,0:T(1,128)S(1)} %get-tuple-element.67), channel_id=1, source_target_pairs={{0,4},{4,8},{8,12},{1,5},{5,9},{9,13},{2,6},{6,10},{10,14},{3,7},{... | collective-permute-start | bytes 107528 | tf_op jit(solution)/shard_map/ppermute | solution.py:24
  31.9 1.3 collective-permute-start.3
  33.5 4.2 %collective-permute-done.3 = f32[7,10,1,128]{3,2,1,0:T(1,128)S(1)} collective-permute-done((f32[7,10,1,128]{3,2,1,0:T(1,128)S(1)}, f32[7,10,1,128]{3,2,1,0:T(1,128)S(1)}, u32[]{:S(2)}, u32[]{:S(2)}) %collective-permute-start.3) | collective-permute-done | bytes 35872 | tf_op jit(solution)/shard_map/ppermute | solution.py:25
  38.7 3.4 collective-permute-start.4
  44.4 4.0 %collective-permute-done.5 = f32[7,10,18,1]{2,3,1,0:T(1,128)S(1)} collective-permute-done((f32[7,10,18,1]{2,3,1,0:T(1,128)S(1)}, f32[7,10,18,1]{2,3,1,0:T(1,128)S(1)}, u32[]{:S(2)}, u32[]{:S(2)}) %collective-permute-start.5) | collective-permute-done | bytes 5072 | tf_op jit(solution)/shard_map/ppermute | solution.py:25
  52.3 1.3 collective-permute-start.6
  53.7 1.8 collective-permute-done.6
  55.4 3.5 collective-permute-start.9
  58.9 1.3 collective-permute-start.8
  60.6 3.8 %collective-permute-done.8 = f32[10,1,128]{2,1,0:T(1,128)S(1)} collective-permute-done((f32[10,1,128]{2,1,0:T(1,128)S(1)}, f32[10,1,128]{2,1,0:T(1,128)S(1)}, u32[]{:S(2)}, u32[]{:S(2)}) %collective-permute-start.8) | collective-permute-done | bytes 5152 | tf_op jit(solution)/shard_map/ppermute | solution.py:25
  65.9 4.9 %collective-permute-start.11 = (f32[10,18,1]{2,1,0:T(8,128)S(1)}, f32[10,18,1]{2,1,0:T(8,128)S(1)}, u32[]{:S(2)}, u32[]{:S(2)}) collective-permute-start(f32[10,18,1]{2,1,0:T(8,128)S(1)} %get-tuple-element.102), channel_id=1, source_target_pairs={{0,1},{1,2},{2,3},{4,5},{5,6},{6,7},{8,9},{9,10},{10,11},{12,13},{... | collective-permute-start | bytes 2168 | tf_op jit(solution)/shard_map/ppermute | solution.py:24
  73.3 1.4 multiply_reduce_fusion.4
  74.7 42.3 %all-reduce.3 = (f32[]{:T(128)}, f32[]{:T(128)}) all-reduce(f32[]{:T(128)} %get-tuple-element.15, f32[]{:T(128)} %get-tuple-element.14), channel_id=1, replica_groups=mesh['gx'=2,'gy'=4,'gz'=4] {'gx','gy','gz'}, use_global_device_ids=true, to_apply=%region_1.2 | all-reduce | flops 2 | bytes 16 | tf_op jit(solution)/shard_map/psum | solution.py:81
  118.3 1.6 fusion.155
  124.3 2.3 collective-permute-start.15
  126.5 1.3 collective-permute-start.14
  128.6 3.5 collective-permute-done.14
  132.2 1.3 collective-permute-start.16
  133.6 5.4 %collective-permute-start.17 = (f32[10,18,1]{2,1,0:T(8,128)S(1)}, f32[10,18,1]{2,1,0:T(8,128)S(1)}, u32[]{:S(2)}, u32[]{:S(2)}) collective-permute-start(f32[10,18,1]{2,1,0:T(8,128)S(1)} %get-tuple-element.100), channel_id=1, source_target_pairs={{0,1},{1,2},{2,3},{4,5},{5,6},{6,7},{8,9},{9,10},{10,11},{12,13},{... | collective-permute-start | bytes 2168 | tf_op jit(solution)/shard_map/ppermute | solution.py:24
  139.8 1.6 collective-permute-done.17
  142.2 41.6 %all-reduce.2 = (f32[]{:T(128)}, f32[]{:T(128)}) all-reduce(f32[]{:T(128)} %get-tuple-element.98, f32[]{:T(128)} %fusion.102), channel_id=1, replica_groups=mesh['gx'=2,'gy'=4,'gz'=4] {'gx','gy','gz'}, use_global_device_ids=true, to_apply=%region_5.6 | all-reduce | flops 2 | bytes 16 | tf_op jit(solution)/shard_map/psum | solution.py:81
  188.2 1.5 fusion.4
  193.9 1.8 collective-permute-done.18
  195.7 3.0 collective-permute-start.21
  198.7 1.3 collective-permute-start.20
  200.2 4.2 %collective-permute-done.20 = f32[3,10,1,128]{3,2,1,0:T(1,128)S(1)} collective-permute-done((f32[3,10,1,128]{3,2,1,0:T(1,128)S(1)}, f32[3,10,1,128]{3,2,1,0:T(1,128)S(1)}, u32[]{:S(2)}, u32[]{:S(2)}) %collective-permute-start.20) | collective-permute-done | bytes 15392 | tf_op jit(solution)/shard_map/ppermute | solution.py:25
  204.6 4.6 %collective-permute-start.23 = (f32[3,10,18,1]{3,2,1,0:T(8,128)S(1)}, f32[3,10,18,1]{3,2,1,0:T(8,128)S(1)}, u32[]{:S(2)}, u32[]{:S(2)}) collective-permute-start(f32[3,10,18,1]{3,2,1,0:T(8,128)S(1)} %get-tuple-element.74), channel_id=1, source_target_pairs={{0,1},{1,2},{2,3},{4,5},{5,6},{6,7},{8,9},{9,10},{10,11},{12,13},{... | collective-permute-start | bytes 6488 | tf_op jit(solution)/shard_map/ppermute | solution.py:24
  210.5 5.4 %collective-permute-done.23 = f32[3,10,18,1]{3,2,1,0:T(8,128)S(1)} collective-permute-done((f32[3,10,18,1]{3,2,1,0:T(8,128)S(1)}, f32[3,10,18,1]{3,2,1,0:T(8,128)S(1)}, u32[]{:S(2)}, u32[]{:S(2)}) %collective-permute-start.23) | collective-permute-done | bytes 2192 | tf_op jit(solution)/shard_map/ppermute | solution.py:24
  217.1 8.7 %collective-permute-done.22 = f32[3,10,18,1]{3,2,1,0:T(8,128)S(1)} collective-permute-done((f32[3,10,18,1]{3,2,1,0:T(8,128)S(1)}, f32[3,10,18,1]{3,2,1,0:T(8,128)S(1)}, u32[]{:S(2)}, u32[]{:S(2)}) %collective-permute-start.22) | collective-permute-done | bytes 2192 | tf_op jit(solution)/shard_map/ppermute | solution.py:25
  227.5 38.8 %all-reduce.1 = (f32[]{:T(128)}, f32[]{:T(128)}) all-reduce(f32[]{:T(128)} %get-tuple-element.13, f32[]{:T(128)} %get-tuple-element.12), channel_id=1, replica_groups=mesh['gx'=2,'gy'=4,'gz'=4] {'gx','gy','gz'}, use_global_device_ids=true, to_apply=%region_9.10 | all-reduce | flops 2 | bytes 16 | tf_op jit(solution)/shard_map/psum | solution.py:81
  267.5 1.7 multiply_reduce_fusion
  270.5 1.3 collective-permute-start.24
  271.8 1.8 collective-permute-done.24
  273.6 3.1 collective-permute-start.27
  278.1 4.2 %collective-permute-done.26 = f32[3,10,1,128]{3,2,1,0:T(1,128)S(1)} collective-permute-done((f32[3,10,1,128]{3,2,1,0:T(1,128)S(1)}, f32[3,10,1,128]{3,2,1,0:T(1,128)S(1)}, u32[]{:S(2)}, u32[]{:S(2)}) %collective-permute-start.26) | collective-permute-done | bytes 15392 | tf_op jit(solution)/shard_map/ppermute | solution.py:25
  282.6 4.5 %collective-permute-start.29 = (f32[3,10,18,1]{3,2,1,0:T(8,128)S(1)}, f32[3,10,18,1]{3,2,1,0:T(8,128)S(1)}, u32[]{:S(2)}, u32[]{:S(2)}) collective-permute-start(f32[3,10,18,1]{3,2,1,0:T(8,128)S(1)} %get-tuple-element.72), channel_id=1, source_target_pairs={{0,1},{1,2},{2,3},{4,5},{5,6},{6,7},{8,9},{9,10},{10,11},{12,13},{... | collective-permute-start | bytes 6488 | tf_op jit(solution)/shard_map/ppermute | solution.py:24
  287.9 1.5 collective-permute-start.28
  289.3 4.5 %collective-permute-done.29 = f32[3,10,18,1]{3,2,1,0:T(8,128)S(1)} collective-permute-done((f32[3,10,18,1]{3,2,1,0:T(8,128)S(1)}, f32[3,10,18,1]{3,2,1,0:T(8,128)S(1)}, u32[]{:S(2)}, u32[]{:S(2)}) %collective-permute-start.29) | collective-permute-done | bytes 2192 | tf_op jit(solution)/shard_map/ppermute | solution.py:24
  295.0 8.7 %collective-permute-done.28 = f32[3,10,18,1]{3,2,1,0:T(8,128)S(1)} collective-permute-done((f32[3,10,18,1]{3,2,1,0:T(8,128)S(1)}, f32[3,10,18,1]{3,2,1,0:T(8,128)S(1)}, u32[]{:S(2)}, u32[]{:S(2)}) %collective-permute-start.28) | collective-permute-done | bytes 2192 | tf_op jit(solution)/shard_map/ppermute | solution.py:25
  305.6 38.8 %all-reduce = (f32[]{:T(128)}, f32[]{:T(128)}) all-reduce(f32[]{:T(128)} %get-tuple-element.24, f32[]{:T(128)} %fusion.23), channel_id=1, replica_groups=mesh['gx'=2,'gy'=4,'gz'=4] {'gx','gy','gz'}, use_global_device_ids=true, to_apply=%region_13.14 | all-reduce | flops 2 | bytes 16 | tf_op jit(solution)/shard_map/psum | solution.py:81
  348.9 1.8 multiply_add_fusion
  350.8 2.4 fusion.1
  (246 shorter events, 36.8 us)
Async XLA Ops:
  22.0 3.7 %collective-permute-start = (f32[7,1,16,128]{3,2,1,0:T(8,128)S(1)}, f32[7,1,16,128]{3,2,1,0:T(8,128)S(1)}, u32[]{:S(2)}, u32[]{:S(2)}) collective-permute-start(f32[7,1,16,128]{3,2,1,0:T(8,128)S(1)} %get-tuple-element.69), channel_id=1, source_target_pairs={{0,16},{1,17},{2,18},{3,19},{4,20},{5,21},{6,22},{7,23},{8,24},{9,... | collective-permute-start | bytes 172040 | tf_op jit(solution)/shard_map/ppermute | solution.py:24
  24.4 3.1 collective-permute-start.1
  27.6 5.9 %collective-permute-start.2 = (f32[7,10,1,128]{3,2,1,0:T(1,128)S(1)}, f32[7,10,1,128]{3,2,1,0:T(1,128)S(1)}, u32[]{:S(2)}, u32[]{:S(2)}) collective-permute-start(f32[7,10,1,128]{3,2,1,0:T(1,128)S(1)} %get-tuple-element.67), channel_id=1, source_target_pairs={{0,4},{4,8},{8,12},{1,5},{5,9},{9,13},{2,6},{6,10},{10,14},{3,7},{... | collective-permute-start | bytes 107528 | tf_op jit(solution)/shard_map/ppermute | solution.py:24
  31.9 5.8 %collective-permute-start.3 = (f32[7,10,1,128]{3,2,1,0:T(1,128)S(1)}, f32[7,10,1,128]{3,2,1,0:T(1,128)S(1)}, u32[]{:S(2)}, u32[]{:S(2)}) collective-permute-start(f32[7,10,1,128]{3,2,1,0:T(1,128)S(1)} %get-tuple-element.68), channel_id=1, source_target_pairs={{4,0},{8,4},{12,8},{5,1},{9,5},{13,9},{6,2},{10,6},{14,10},{7,3},{... | collective-permute-start | bytes 107528 | tf_op jit(solution)/shard_map/ppermute | solution.py:25
  33.5 156.5 %copy-start.4 = (f32[7,10,1,128]{3,2,1,0:T(1,128)}, f32[7,10,1,128]{3,2,1,0:T(1,128)S(1)}, u32[]{:S(2)}) copy-start(f32[7,10,1,128]{3,2,1,0:T(1,128)S(1)} %collective-permute-done.2) | copy-start | bytes 107524
  37.7 152.3 %copy-start.6 = (f32[7,10,1,128]{3,2,1,0:T(1,128)}, f32[7,10,1,128]{3,2,1,0:T(1,128)S(1)}, u32[]{:S(2)}) copy-start(f32[7,10,1,128]{3,2,1,0:T(1,128)S(1)} %collective-permute-done.3) | copy-start | bytes 107524
  38.7 5.2 %collective-permute-start.4 = (f32[7,10,18,1]{2,3,1,0:T(1,128)S(1)}, f32[7,10,18,1]{2,3,1,0:T(1,128)S(1)}, u32[]{:S(2)}, u32[]{:S(2)}) collective-permute-start(f32[7,10,18,1]{2,3,1,0:T(1,128)S(1)} %copy.333), channel_id=1, source_target_pairs={{0,1},{1,2},{2,3},{4,5},{5,6},{6,7},{8,9},{9,10},{10,11},{12,13},{... | collective-permute-start | bytes 15128 | tf_op jit(solution)/shard_map/ppermute | solution.py:24
  42.6 5.8 %collective-permute-start.5 = (f32[7,10,18,1]{2,3,1,0:T(1,128)S(1)}, f32[7,10,18,1]{2,3,1,0:T(1,128)S(1)}, u32[]{:S(2)}, u32[]{:S(2)}) collective-permute-start(f32[7,10,18,1]{2,3,1,0:T(1,128)S(1)} %copy.334), channel_id=1, source_target_pairs={{1,0},{2,1},{3,2},{5,4},{6,5},{7,6},{9,8},{10,9},{11,10},{13,12},{... | collective-permute-start | bytes 15128 | tf_op jit(solution)/shard_map/ppermute | solution.py:25
  51.0 22.2 %copy-start.13 = (f32[8,16,128]{2,1,0:T(8,128)}, f32[8,16,128]{2,1,0:T(8,128)S(1)}, u32[]{:S(2)}) copy-start(f32[8,16,128]{2,1,0:T(8,128)S(1)} %get-tuple-element.40) | copy-start | bytes 196612
  51.0 22.2 %copy-start.40 = (f32[8,16,128]{2,1,0:T(8,128)}, f32[8,16,128]{2,1,0:T(8,128)S(1)}, u32[]{:S(2)}) copy-start(f32[8,16,128]{2,1,0:T(8,128)S(1)} %get-tuple-element.41) | copy-start | bytes 196612
  51.0 22.2 %copy-start.42 = (f32[8,16,128]{2,1,0:T(8,128)}, f32[8,16,128]{2,1,0:T(8,128)S(1)}, u32[]{:S(2)}) copy-start(f32[8,16,128]{2,1,0:T(8,128)S(1)} %get-tuple-element.42) | copy-start | bytes 196612
  51.0 22.2 %copy-start.44 = (f32[8,16,128]{2,1,0:T(8,128)}, f32[8,16,128]{2,1,0:T(8,128)S(1)}, u32[]{:S(2)}) copy-start(f32[8,16,128]{2,1,0:T(8,128)S(1)} %get-tuple-element.43) | copy-start | bytes 196612
  51.0 22.2 %copy-start.46 = (f32[8,16,128]{2,1,0:T(8,128)}, f32[8,16,128]{2,1,0:T(8,128)S(1)}, u32[]{:S(2)}) copy-start(f32[8,16,128]{2,1,0:T(8,128)S(1)} %get-tuple-element.44) | copy-start | bytes 196612
  51.0 22.2 %copy-start.48 = (f32[8,16,128]{2,1,0:T(8,128)}, f32[8,16,128]{2,1,0:T(8,128)S(1)}, u32[]{:S(2)}) copy-start(f32[8,16,128]{2,1,0:T(8,128)S(1)} %get-tuple-element.45) | copy-start | bytes 196612
  51.0 22.2 %copy-start.50 = (f32[8,16,128]{2,1,0:T(8,128)}, f32[8,16,128]{2,1,0:T(8,128)S(1)}, u32[]{:S(2)}) copy-start(f32[8,16,128]{2,1,0:T(8,128)S(1)} %get-tuple-element.46) | copy-start | bytes 196612
  51.0 22.2 %copy-start.52 = (f32[8,16,128]{2,1,0:T(8,128)}, f32[8,16,128]{2,1,0:T(8,128)S(1)}, u32[]{:S(2)}) copy-start(f32[8,16,128]{2,1,0:T(8,128)S(1)} %get-tuple-element.47) | copy-start | bytes 196612
  51.0 2.6 collective-permute-start.7
  52.3 3.1 collective-permute-start.6
  55.4 5.1 %collective-permute-start.9 = (f32[10,1,128]{2,1,0:T(1,128)S(1)}, f32[10,1,128]{2,1,0:T(1,128)S(1)}, u32[]{:S(2)}, u32[]{:S(2)}) collective-permute-start(f32[10,1,128]{2,1,0:T(1,128)S(1)} %get-tuple-element.105), channel_id=1, source_target_pairs={{0,4},{4,8},{8,12},{1,5},{5,9},{9,13},{2,6},{6,10},{10,14},{3,7},{... | collective-permute-start | bytes 15368 | tf_op jit(solution)/shard_map/ppermute | solution.py:24
  58.9 5.5 %collective-permute-start.8 = (f32[10,1,128]{2,1,0:T(1,128)S(1)}, f32[10,1,128]{2,1,0:T(1,128)S(1)}, u32[]{:S(2)}, u32[]{:S(2)}) collective-permute-start(f32[10,1,128]{2,1,0:T(1,128)S(1)} %get-tuple-element.106), channel_id=1, source_target_pairs={{4,0},{8,4},{12,8},{5,1},{9,5},{13,9},{6,2},{10,6},{14,10},{7,3},{... | collective-permute-start | bytes 15368 | tf_op jit(solution)/shard_map/ppermute | solution.py:25
  64.6 7.5 %collective-permute-start.10 = (f32[10,18,1]{2,1,0:T(8,128)S(1)}, f32[10,18,1]{2,1,0:T(8,128)S(1)}, u32[]{:S(2)}, u32[]{:S(2)}) collective-permute-start(f32[10,18,1]{2,1,0:T(8,128)S(1)} %get-tuple-element.101), channel_id=1, source_target_pairs={{1,0},{2,1},{3,2},{5,4},{6,5},{7,6},{9,8},{10,9},{11,10},{13,12},{... | collective-permute-start | bytes 2168 | tf_op jit(solution)/shard_map/ppermute | solution.py:25
  65.9 7.4 %collective-permute-start.11 = (f32[10,18,1]{2,1,0:T(8,128)S(1)}, f32[10,18,1]{2,1,0:T(8,128)S(1)}, u32[]{:S(2)}, u32[]{:S(2)}) collective-permute-start(f32[10,18,1]{2,1,0:T(8,128)S(1)} %get-tuple-element.102), channel_id=1, source_target_pairs={{0,1},{1,2},{2,3},{4,5},{5,6},{6,7},{8,9},{9,10},{10,11},{12,13},{... | collective-permute-start | bytes 2168 | tf_op jit(solution)/shard_map/ppermute | solution.py:24
  119.9 3.5 collective-permute-start.13
  121.2 3.1 collective-permute-start.12
  124.3 4.3 %collective-permute-start.15 = (f32[10,1,128]{2,1,0:T(1,128)S(1)}, f32[10,1,128]{2,1,0:T(1,128)S(1)}, u32[]{:S(2)}, u32[]{:S(2)}) collective-permute-start(f32[10,1,128]{2,1,0:T(1,128)S(1)} %get-tuple-element.103), channel_id=1, source_target_pairs={{0,4},{4,8},{8,12},{1,5},{5,9},{9,13},{2,6},{6,10},{10,14},{3,7},{... | collective-permute-start | bytes 15368 | tf_op jit(solution)/shard_map/ppermute | solution.py:24
  126.5 5.5 %collective-permute-start.14 = (f32[10,1,128]{2,1,0:T(1,128)S(1)}, f32[10,1,128]{2,1,0:T(1,128)S(1)}, u32[]{:S(2)}, u32[]{:S(2)}) collective-permute-start(f32[10,1,128]{2,1,0:T(1,128)S(1)} %get-tuple-element.104), channel_id=1, source_target_pairs={{4,0},{8,4},{12,8},{5,1},{9,5},{13,9},{6,2},{10,6},{14,10},{7,3},{... | collective-permute-start | bytes 15368 | tf_op jit(solution)/shard_map/ppermute | solution.py:25
  132.2 7.6 %collective-permute-start.16 = (f32[10,18,1]{2,1,0:T(8,128)S(1)}, f32[10,18,1]{2,1,0:T(8,128)S(1)}, u32[]{:S(2)}, u32[]{:S(2)}) collective-permute-start(f32[10,18,1]{2,1,0:T(8,128)S(1)} %get-tuple-element.99), channel_id=1, source_target_pairs={{1,0},{2,1},{3,2},{5,4},{6,5},{7,6},{9,8},{10,9},{11,10},{13,12},{... | collective-permute-start | bytes 2168 | tf_op jit(solution)/shard_map/ppermute | solution.py:25
  133.6 7.8 %collective-permute-start.17 = (f32[10,18,1]{2,1,0:T(8,128)S(1)}, f32[10,18,1]{2,1,0:T(8,128)S(1)}, u32[]{:S(2)}, u32[]{:S(2)}) collective-permute-start(f32[10,18,1]{2,1,0:T(8,128)S(1)} %get-tuple-element.100), channel_id=1, source_target_pairs={{0,1},{1,2},{2,3},{4,5},{5,6},{6,7},{8,9},{9,10},{10,11},{12,13},{... | collective-permute-start | bytes 2168 | tf_op jit(solution)/shard_map/ppermute | solution.py:24
  191.2 34.7 %copy-start.3 = (f32[3,8,16,128]{3,2,1,0:T(8,128)}, f32[3,8,16,128]{3,2,1,0:T(8,128)S(1)}, u32[]{:S(2)}) copy-start(f32[3,8,16,128]{3,2,1,0:T(8,128)S(1)} %get-tuple-element.28) | copy-start | bytes 589828
  191.3 2.6 collective-permute-start.19
  192.6 3.1 collective-permute-start.18
  193.9 32.1 %copy-start.27 = (f32[3,1,16,128]{3,2,1,0:T(8,128)}, f32[3,1,16,128]{3,2,1,0:T(8,128)S(1)}, u32[]{:S(2)}) copy-start(f32[3,1,16,128]{3,2,1,0:T(8,128)S(1)} %collective-permute-done.19) | copy-start | bytes 73732
  195.7 30.3 %copy-start.29 = (f32[3,1,16,128]{3,2,1,0:T(8,128)}, f32[3,1,16,128]{3,2,1,0:T(8,128)S(1)}, u32[]{:S(2)}) copy-start(f32[3,1,16,128]{3,2,1,0:T(8,128)S(1)} %collective-permute-done.18) | copy-start | bytes 73732
  195.7 4.5 %collective-permute-start.21 = (f32[3,10,1,128]{3,2,1,0:T(1,128)S(1)}, f32[3,10,1,128]{3,2,1,0:T(1,128)S(1)}, u32[]{:S(2)}, u32[]{:S(2)}) collective-permute-start(f32[3,10,1,128]{3,2,1,0:T(1,128)S(1)} %get-tuple-element.79), channel_id=1, source_target_pairs={{0,4},{4,8},{8,12},{1,5},{5,9},{9,13},{2,6},{6,10},{10,14},{3,7},{... | collective-permute-start | bytes 46088 | tf_op jit(solution)/shard_map/ppermute | solution.py:24
  198.7 5.6 %collective-permute-start.20 = (f32[3,10,1,128]{3,2,1,0:T(1,128)S(1)}, f32[3,10,1,128]{3,2,1,0:T(1,128)S(1)}, u32[]{:S(2)}, u32[]{:S(2)}) collective-permute-start(f32[3,10,1,128]{3,2,1,0:T(1,128)S(1)} %get-tuple-element.80), channel_id=1, source_target_pairs={{4,0},{8,4},{12,8},{5,1},{9,5},{13,9},{6,2},{10,6},{14,10},{7,3},{... | collective-permute-start | bytes 46088 | tf_op jit(solution)/shard_map/ppermute | solution.py:25
  200.2 25.9 %copy-start.63 = (f32[3,10,1,128]{3,2,1,0:T(1,128)}, f32[3,10,1,128]{3,2,1,0:T(1,128)S(1)}, u32[]{:S(2)}) copy-start(f32[3,10,1,128]{3,2,1,0:T(1,128)S(1)} %collective-permute-done.21) | copy-start | bytes 46084
  204.6 11.3 %collective-permute-start.23 = (f32[3,10,18,1]{3,2,1,0:T(8,128)S(1)}, f32[3,10,18,1]{3,2,1,0:T(8,128)S(1)}, u32[]{:S(2)}, u32[]{:S(2)}) collective-permute-start(f32[3,10,18,1]{3,2,1,0:T(8,128)S(1)} %get-tuple-element.74), channel_id=1, source_target_pairs={{0,1},{1,2},{2,3},{4,5},{5,6},{6,7},{8,9},{9,10},{10,11},{12,13},{... | collective-permute-start | bytes 6488 | tf_op jit(solution)/shard_map/ppermute | solution.py:24
  209.2 16.5 %collective-permute-start.22 = (f32[3,10,18,1]{3,2,1,0:T(8,128)S(1)}, f32[3,10,18,1]{3,2,1,0:T(8,128)S(1)}, u32[]{:S(2)}, u32[]{:S(2)}) collective-permute-start(f32[3,10,18,1]{3,2,1,0:T(8,128)S(1)} %get-tuple-element.73), channel_id=1, source_target_pairs={{1,0},{2,1},{3,2},{5,4},{6,5},{7,6},{9,8},{10,9},{11,10},{13,12},{... | collective-permute-start | bytes 6488 | tf_op jit(solution)/shard_map/ppermute | solution.py:25
  226.5 41.0 %copy-start.36 = (f32[1,8,16,128]{3,2,1,0:T(8,128)S(1)}, f32[1,8,16,128]{3,2,1,0:T(8,128)}, u32[]{:S(2)}) copy-start(f32[1,8,16,128]{3,2,1,0:T(8,128)} %get-tuple-element.29) | copy-start | bytes 196612
  269.2 2.6 collective-permute-start.25
  270.5 3.1 collective-permute-start.24
  271.8 32.1 %copy-start.31 = (f32[3,1,16,128]{3,2,1,0:T(8,128)}, f32[3,1,16,128]{3,2,1,0:T(8,128)S(1)}, u32[]{:S(2)}) copy-start(f32[3,1,16,128]{3,2,1,0:T(8,128)S(1)} %collective-permute-done.25) | copy-start | bytes 73732
  273.6 30.3 %copy-start.33 = (f32[3,1,16,128]{3,2,1,0:T(8,128)}, f32[3,1,16,128]{3,2,1,0:T(8,128)S(1)}, u32[]{:S(2)}) copy-start(f32[3,1,16,128]{3,2,1,0:T(8,128)S(1)} %collective-permute-done.24) | copy-start | bytes 73732
  273.6 4.5 %collective-permute-start.27 = (f32[3,10,1,128]{3,2,1,0:T(1,128)S(1)}, f32[3,10,1,128]{3,2,1,0:T(1,128)S(1)}, u32[]{:S(2)}, u32[]{:S(2)}) collective-permute-start(f32[3,10,1,128]{3,2,1,0:T(1,128)S(1)} %get-tuple-element.77), channel_id=1, source_target_pairs={{0,4},{4,8},{8,12},{1,5},{5,9},{9,13},{2,6},{6,10},{10,14},{3,7},{... | collective-permute-start | bytes 46088 | tf_op jit(solution)/shard_map/ppermute | solution.py:24
  276.7 5.6 %collective-permute-start.26 = (f32[3,10,1,128]{3,2,1,0:T(1,128)S(1)}, f32[3,10,1,128]{3,2,1,0:T(1,128)S(1)}, u32[]{:S(2)}, u32[]{:S(2)}) collective-permute-start(f32[3,10,1,128]{3,2,1,0:T(1,128)S(1)} %get-tuple-element.78), channel_id=1, source_target_pairs={{4,0},{8,4},{12,8},{5,1},{9,5},{13,9},{6,2},{10,6},{14,10},{7,3},{... | collective-permute-start | bytes 46088 | tf_op jit(solution)/shard_map/ppermute | solution.py:25
  278.1 25.8 %copy-start.59 = (f32[3,10,1,128]{3,2,1,0:T(1,128)}, f32[3,10,1,128]{3,2,1,0:T(1,128)S(1)}, u32[]{:S(2)}) copy-start(f32[3,10,1,128]{3,2,1,0:T(1,128)S(1)} %collective-permute-done.27) | copy-start | bytes 46084
  282.6 11.2 %collective-permute-start.29 = (f32[3,10,18,1]{3,2,1,0:T(8,128)S(1)}, f32[3,10,18,1]{3,2,1,0:T(8,128)S(1)}, u32[]{:S(2)}, u32[]{:S(2)}) collective-permute-start(f32[3,10,18,1]{3,2,1,0:T(8,128)S(1)} %get-tuple-element.72), channel_id=1, source_target_pairs={{0,1},{1,2},{2,3},{4,5},{5,6},{6,7},{8,9},{9,10},{10,11},{12,13},{... | collective-permute-start | bytes 6488 | tf_op jit(solution)/shard_map/ppermute | solution.py:24
  287.9 15.8 %collective-permute-start.28 = (f32[3,10,18,1]{3,2,1,0:T(8,128)S(1)}, f32[3,10,18,1]{3,2,1,0:T(8,128)S(1)}, u32[]{:S(2)}, u32[]{:S(2)}) collective-permute-start(f32[3,10,18,1]{3,2,1,0:T(8,128)S(1)} %get-tuple-element.71), channel_id=1, source_target_pairs={{1,0},{2,1},{3,2},{5,4},{6,5},{7,6},{9,8},{10,9},{11,10},{13,12},{... | collective-permute-start | bytes 6488 | tf_op jit(solution)/shard_map/ppermute | solution.py:25
  (68 other events, 233.1 us)
where the time goes:
time: 356 us; the launch traced here: 354 us
  blocking collectives  161 us (45%)
  starting transfers between devices  66 us (19%)
  waiting for transfers between devices  62.5 us (18%)
  other arithmetic  39.3 us (11%)
  between operations  13.4 us (4%)
  local copies, waits for them, and re-layouts  11.4 us (3%)
    psum x4, blocking collectives, products(): lax.psum((jnp.sum(residual * precond), jnp.sum(precond * image)), ('gx',...  161 us
    ppermute x15, waiting for transfers between devices, extended(): after = lax.ppermute(initial, axis, down)  49.3 us
    ppermute x15, starting transfers between devices, extended(): before = lax.ppermute(last, axis, up)  46.5 us
    ppermute x15, starting transfers between devices, extended(): after = lax.ppermute(initial, axis, down)  19.5 us
    unnamed x2, other arithmetic  17.4 us
    ppermute x15, waiting for transfers between devices, extended(): before = lax.ppermute(last, axis, up)  13.3 us
  transfers between devices with their start and end apart: 30, of which 20 were waited for; matrix products, arithmetic and copies ran while one was open for 2% of the time, Pallas kernels for 0%

commit v1 on v0

v1 whole, which is shorter than its diff:
```python
import jax
import jax.numpy as jnp
from jax import lax
from jax.experimental import pallas as pl
from jax.experimental.pallas import tpu as pltpu
from jax.sharding import PartitionSpec as P

ZONES = 8

storage = 0.2
biot_coef = 0.8
leakage = 2.0
support = 1.0

AXES = ("gx", "gy", "gz")
LANES = 128
TILE = 8

ZONE, PRESS, MOTION, SOURCE, DRAIN, BODY = 0, 1, 2, 5, 6, 7
WIDTHS = (5, 5, 5, 5, 5, 4, 4, 2, 2, 2)
NF = len(WIDTHS)
W = max(WIDTHS)
OFFSETS = tuple(sum(WIDTHS[:f]) for f in range(NF))
SLOT = 8
PAIRS = tuple((j, k) for j in range(3) for k in range(j, 3))
SUMS = 4 + 4 * len(PAIRS)


def up_to(value, multiple):
    return -(-value // multiple) * multiple


MSG_ROWS = up_to(sum(WIDTHS), TILE)


def lane_iota(shape):
    return lax.broadcasted_iota(jnp.int32, shape, len(shape) - 1)


def pack_rows(source, pressure, strain, motion, body, zones, drained, fields, upward, downward):
    nx, ny, _ = source.shape
    for x in range(nx):
        values = [
            zones[x].astype(jnp.float32) + 1.0,
            pressure[x],
            motion[0, x],
            motion[1, x],
            motion[2, x],
            source[x] + biot_coef * strain[x],
            drained[x].astype(jnp.float32),
            body[0, x],
            body[1, x],
            body[2, x],
        ]
        for f, value in enumerate(values):
            fields[f, x] = value
            width, offset = WIDTHS[f], OFFSETS[f]
            upward[x, offset : offset + width, :] = value[ny - width :, :]
            downward[x, offset : offset + width, :] = value[:width, :]
        rest = MSG_ROWS - sum(WIDTHS)
        if rest:
            empty = jnp.zeros((rest, source.shape[2]), jnp.float32)
            upward[x, MSG_ROWS - rest :, :] = empty
            downward[x, MSG_ROWS - rest :, :] = empty


def pack_lanes(last_y, fields, low, high, tall, rightward, leftward):
    _, nx, ny, nz = fields.shape
    rows = tall.shape[2]
    parts = LANES // (SLOT * nx)
    height = rows // parts
    at_y = lax.axis_index("gy")
    keep_low = jnp.where(at_y > 0, 1.0, 0.0)
    keep_high = jnp.where(at_y < last_y, 1.0, 0.0)
    for f in range(NF):
        width, offset = WIDTHS[f], OFFSETS[f]

        def fill(x, _, f=f, width=width, offset=offset):
            tall[f, x, :ny, :] = fields[f, x]
            tall[f, x, ny:, :] = jnp.zeros((rows - ny, nz), jnp.float32)
            tall[f, x, ny : ny + width, :] = high[x, offset : offset + width, :] * keep_high
            tall[f, x, rows - width :, :] = low[x, offset : offset + width, :] * keep_low
            return 0

        lax.fori_loop(0, nx, fill, 0)
        lane = lane_iota((height, LANES))
        to_right = jnp.zeros((height, LANES), jnp.float32)
        to_left = jnp.zeros((height, LANES), jnp.float32)
        for x in range(nx):
            for part in range(parts):
                piece = tall[f, x, part * height : (part + 1) * height, :]
                start = part * SLOT * nx + SLOT * x
                mine = (lane >= start) & (lane < start + width)
                ending = piece[:, nz - LANES :]
                to_right = jnp.where(
                    mine, pltpu.roll(ending, (start + width) % LANES, 1), to_right
                )
                to_left = jnp.where(mine, pltpu.roll(piece[:, :LANES], start, 1), to_left)
        rightward[f] = to_right
        leftward[f] = to_left


def harmonic(a, b):
    return 2.0 * a * b / jnp.maximum(a + b, 1e-30)


def main_kernel(
    peers,
    tables,
    tall,
    below,
    above,
    left,
    right,
    left_below,
    right_below,
    left_above,
    right_above,
    basis,
    partial,
    ext,
    perm,
    heft,
    shear,
    fixed,
    tx,
    ty,
    tz,
    mx,
    my,
    mz,
    react,
    pdiag,
    pinv,
    z0,
    p0,
    ediag,
    einv,
    push,
    zs,
    ps,
    acc,
):
    _, nx, rows, nz = tall.shape
    ny = basis.shape[2]
    lanes = ext.shape[3]
    parts = LANES // (SLOT * nx)
    height = rows // parts
    at = [lax.axis_index(a) for a in AXES]
    has_below = (at[0] > 0).astype(jnp.int32)
    has_above = (at[0] < peers[0] - 1).astype(jnp.int32)
    keep_left = jnp.where(at[2] > 0, 1.0, 0.0)
    keep_right = jnp.where(at[2] < peers[2] - 1, 1.0, 0.0)

    def first(halo):
        return W - halo * has_below

    def end(halo):
        return W + nx + halo * has_above

    def yp(v):
        return pltpu.roll(v, v.shape[0] - 1, 0)

    def ym(v):
        return pltpu.roll(v, 1, 0)

    def zp(v):
        return pltpu.roll(v, v.shape[1] - 1, 1)

    def zm(v):
        return pltpu.roll(v, 1, 1)

    def layers(start, stop, body):
        def step(l, carry):
            body(l)
            return carry

        lax.fori_loop(start, stop, step, 0)

    empty = jnp.zeros((rows, lanes), jnp.float32)
    for l in (W - 1, W + nx):
        for ref in (perm, heft, shear, z0, p0):
            ref[l] = empty
        for f in range(NF):
            ext[f, l] = empty
        for i in range(9):
            zs[i, l] = empty
            ps[i, l] = empty

    def assemble(l, x, source, low, high):
        lane = lane_iota((height, LANES))
        for f in range(NF):
            width = WIDTHS[f]
            ext[f, l, :, :nz] = source[f, x]
            for part in range(parts):
                start = part * SLOT * nx + SLOT * x
                after = pltpu.roll(high[f], LANES - start, 1) * keep_right
                before = pltpu.roll(low[f], LANES - width - start, 1) * keep_left
                side = jnp.where(
                    lane < width, after, jnp.where(lane >= LANES - width, before, 0.0)
                )
                ext[f, l, part * height : (part + 1) * height, nz:] = side
        zone = ext[ZONE, l]
        picked = [jnp.zeros((rows, lanes), jnp.float32)] * 3
        for index in range(ZONES):
            here = zone == float(index + 1)
            picked = [
                jnp.where(here, tables[t, index], value) for t, value in enumerate(picked)
            ]
        perm[l] = picked[0]
        heft[l] = picked[1] + picked[2]
        shear[l] = picked[2]
        fixed[l] = jnp.where(
            zone > 0.0,
            biot_coef * biot_coef / jnp.maximum(picked[1] + 2.0 * picked[2] / 3.0, 1e-30),
            0.0,
        )

    layers(
        first(W), W, lambda l: assemble(l, l + nx - W, below, left_below, right_below)
    )
    layers(W, W + nx, lambda l: assemble(l, l - W, tall, left, right))
    layers(
        W + nx, end(W), lambda l: assemble(l, l - W - nx, above, left_above, right_above)
    )

    def press_faces(l):
        own = perm[l]
        tx[l] = harmonic(own, perm[l + 1])
        ty[l] = harmonic(own, yp(own))
        tz[l] = harmonic(own, zp(own))

    layers(first(4) - 1, end(4), press_faces)

    def press_flux(read, l):
        own = read(l)
        along_y = ty[l] * (own - yp(own))
        along_z = tz[l] * (own - zp(own))
        return (
            tx[l] * (own - read(l + 1))
            + tx[l - 1] * (own - read(l - 1))
            + (along_y - ym(along_y))
            + (along_z - zm(along_z))
        )

    def central(read, l):
        a, b = read(1, l), read(2, l)
        return 0.5 * (
            read(0, l + 1) - read(0, l - 1) + (yp(a) - ym(a)) + (zp(b) - zm(b))
        )

    def old_press(l):
        return ext[PRESS, l]

    def old_motion(c, l):
        return ext[MOTION + c, l]

    def press_start(l):
        along_y, along_z = ty[l], tz[l]
        leak = leakage * ext[DRAIN, l]
        reaction = storage + fixed[l] + leak
        diag = (
            reaction
            + tx[l]
            + tx[l - 1]
            + (along_y + ym(along_y))
            + (along_z + zm(along_z))
        )
        inverse = jnp.where(ext[ZONE, l] > 0.0, 1.0 / diag, 0.0)
        residual = (
            ext[SOURCE, l]
            - biot_coef * central(old_motion, l)
            - leak * ext[PRESS, l]
            - press_flux(old_press, l)
        )
        react[l] = reaction
        pdiag[l] = diag
        pinv[l] = inverse
        z0[l] = residual * inverse

    layers(first(4), end(4), press_start)

    def press_next(l):
        own = z0[l]
        p0[l] = (react[l] * own + press_flux(lambda i: z0[i], l)) * pinv[l]

    layers(first(3), end(3), press_next)

    def motion_faces(l):
        own = shear[l]
        mx[l] = harmonic(own, shear[l + 1])
        my[l] = harmonic(own, yp(own))
        mz[l] = harmonic(own, zp(own))

    layers(first(2) - 1, end(2), motion_faces)

    def scaled_div(read, l):
        a, b, c = read(0, l), read(1, l), read(2, l)
        return heft[l] * ((read(0, l + 1) - a) + (yp(b) - b) + (zp(c) - c))

    def elastic(read, l, pushed, pushed_before):
        back = (pushed_before, ym(pushed), zm(pushed))
        out = []
        for c in range(3):
            own = read(c, l)
            along_y = my[l] * (own - yp(own))
            along_z = mz[l] * (own - zp(own))
            out.append(
                support * own
                + (
                    mx[l] * (own - read(c, l + 1))
                    + mx[l - 1] * (own - read(c, l - 1))
                    + (along_y - ym(along_y))
                    + (along_z - zm(along_z))
                )
                + (back[c] - pushed)
            )
        return out

    def gradient(read, l):
        own = read(l)
        return (
            0.5 * (read(l + 1) - read(l - 1)),
            0.5 * (yp(own) - ym(own)),
            0.5 * (zp(own) - zm(own)),
        )

    def motion_start(l):
        weight = heft[l]
        along_y, along_z = my[l], mz[l]
        base = (
            support
            + mx[l]
            + mx[l - 1]
            + (along_y + ym(along_y))
            + (along_z + zm(along_z))
            + weight
        )
        inside = ext[ZONE, l] > 0.0
        for c, beside in enumerate((heft[l - 1], ym(weight), zm(weight))):
            diag = base + beside
            ediag[c, l] = diag
            einv[c, l] = jnp.where(inside, 1.0 / diag, 0.0)
        pushed = scaled_div(old_motion, l)
        push[0, l] = pushed
        image = elastic(old_motion, l, pushed, push[0, l - 1])
        grads = [
            gradient(old_press, l),
            gradient(lambda i: z0[i], l),
            gradient(lambda i: p0[i], l),
        ]
        for c in range(3):
            inverse = einv[c, l]
            zs[c, l] = (ext[BODY + c, l] - biot_coef * grads[0][c] - image[c]) * inverse
            zs[3 + c, l] = -biot_coef * grads[1][c] * inverse
            zs[6 + c, l] = -biot_coef * grads[2][c] * inverse

    push[0, first(2) - 1] = scaled_div(old_motion, first(2) - 1)
    layers(first(2), end(2), motion_start)

    for j in range(3):

        def basis_field(c, l, j=j):
            return zs[3 * j + c, l]

        def motion_next(l, j=j, read=basis_field):
            pushed = scaled_div(read, l)
            push[j, l] = pushed
            image = elastic(read, l, pushed, push[j, l - 1])
            for c in range(3):
                ps[3 * j + c, l] = image[c] * einv[c, l]

        push[j, first(1) - 1] = scaled_div(basis_field, first(1) - 1)
        layers(first(1), end(1), motion_next)

    acc[...] = jnp.zeros(acc.shape, jnp.float32)

    def own_part(v):
        return v[:ny, :nz]

    def finish(l):
        x = l - W

        def add(index, value):
            total = value[:TILE]
            for start in range(TILE, ny, TILE):
                total = total + value[start : start + TILE]
            folded = total[:, :LANES]
            for start in range(LANES, nz, LANES):
                folded = folded + total[:, start : start + LANES]
            acc[index] = acc[index] + folded

        field, image = z0[l], p0[l]
        a, b = own_part(field), own_part(image)
        basis[0, x] = a
        basis[1, x] = b
        diag = own_part(pdiag[l])
        add(0, diag * a * a)
        add(1, diag * a * b)
        add(2, diag * b * b)
        dx = own_part(p0[l + 1]) - b
        dy = own_part(yp(image)) - b
        dz = own_part(zp(image)) - b
        add(
            3,
            own_part(react[l]) * b * b
            + own_part(tx[l]) * dx * dx
            + own_part(ty[l]) * dy * dy
            + own_part(tz[l]) * dz * dz,
        )
        basis[20, x] = own_part(central(old_motion, l))
        za, pa, steps, divs = [], [], [], []
        for j in range(3):
            za.append([own_part(zs[3 * j + c, l]) for c in range(3)])
            pa.append([own_part(ps[3 * j + c, l]) for c in range(3)])
            for c in range(3):
                basis[2 + 3 * j + c, x] = za[j][c]
                basis[11 + 3 * j + c, x] = pa[j][c]
            basis[21 + j, x] = own_part(central(lambda c, i, j=j: zs[3 * j + c, i], l))
            basis[24 + j, x] = own_part(central(lambda c, i, j=j: ps[3 * j + c, i], l))
            moved = []
            for c in range(3):
                own = ps[3 * j + c, l]
                moved.append(
                    (
                        own_part(ps[3 * j + c, l + 1]) - pa[j][c],
                        own_part(yp(own)) - pa[j][c],
                        own_part(zp(own)) - pa[j][c],
                    )
                )
            steps.append(moved)
            divs.append(moved[0][0] + moved[1][1] + moved[2][2])
        diags = [own_part(ediag[c, l]) for c in range(3)]
        faces = [own_part(ref[l]) for ref in (mx, my, mz)]
        weight = own_part(heft[l])
        for i, (j, k) in enumerate(PAIRS):
            add(4 + i, sum(diags[c] * za[j][c] * za[k][c] for c in range(3)))
            add(10 + i, sum(diags[c] * za[j][c] * pa[k][c] for c in range(3)))
            add(16 + i, sum(diags[c] * pa[j][c] * pa[k][c] for c in range(3)))
            energy = support * sum(pa[j][c] * pa[k][c] for c in range(3))
            for d in range(3):
                energy = energy + faces[d] * sum(
                    steps[j][c][d] * steps[k][c][d] for c in range(3)
                )
            add(22 + i, energy + weight * divs[j] * divs[k])

    layers(W, W + nx, finish)

    sums = jnp.concatenate(
        [jnp.sum(acc[i], axis=0, keepdims=True) for i in range(acc.shape[0])], axis=0
    )
    totals = jnp.sum(sums, axis=1, keepdims=True)
    row = lax.broadcasted_iota(jnp.int32, sums.shape, 0)
    spread = jnp.where(row == lane_iota(sums.shape), totals, 0.0)
    line = jnp.sum(spread, axis=0, keepdims=True)
    partial[...] = jnp.broadcast_to(line, partial.shape)


def step_sizes(gamma, delta, cross, energy):
    first = gamma / delta
    gamma_new = gamma - 2.0 * first * delta + first * first * cross
    curved = delta - 2.0 * first * cross + first * first * energy
    ratio = gamma_new / gamma
    second = gamma_new / (curved - ratio * gamma_new / first)
    return first + second * (1.0 + ratio), -first * second


def combine(sums, basis, pressure_old, motion_old, pressure, motion, strain):
    line = jnp.sum(sums[...], axis=0, keepdims=True)
    lane = lane_iota(line.shape)

    def value(index):
        return jnp.sum(jnp.where(lane == index, line, 0.0), axis=1, keepdims=True)

    c1, c2 = step_sizes(*[value(i) for i in range(4)])
    weights = (jnp.ones_like(c1), c1, c2)

    def form(start):
        total = 0.0
        for i, (j, k) in enumerate(PAIRS):
            scale = 1.0 if j == k else 2.0
            total = total + scale * weights[j] * weights[k] * value(start + i)
        return total

    d1, d2 = step_sizes(form(4), form(10), form(16), form(22))
    on_z = [d1 * w for w in weights]
    on_p = [d2 * w for w in weights]
    for x in range(pressure.shape[0]):
        pressure[x] = pressure_old[x] + c1 * basis[0, x] + c2 * basis[1, x]
        for c in range(3):
            total = motion_old[c, x]
            for j in range(3):
                total = total + on_z[j] * basis[2 + 3 * j + c, x]
                total = total + on_p[j] * basis[11 + 3 * j + c, x]
            motion[c, x] = total
        total = basis[20, x]
        for j in range(3):
            total = total + on_z[j] * basis[21 + j, x]
            total = total + on_p[j] * basis[24 + j, x]
        strain[x] = total


def f32(*shape):
    return jax.ShapeDtypeStruct(shape, jnp.float32)


def call(kernel, outs, *args, smem=(), scratch=(), limit=None):
    specs = [
        pl.BlockSpec(memory_space=pltpu.SMEM if i in smem else pltpu.VMEM)
        for i in range(len(args))
    ]
    return pl.pallas_call(
        kernel,
        out_shape=outs,
        in_specs=specs,
        scratch_shapes=scratch,
        compiler_params=pltpu.CompilerParams(vmem_limit_bytes=limit),
    )(*args)


def ring(value, axis, step):
    peers = lax.axis_size(axis)
    return lax.ppermute(value, axis, [(i, (i + step) % peers) for i in range(peers)])


def x_neighbours(value):
    peers = lax.axis_size("gx")
    above = ring(value, "gx", -1)
    below = above if peers == 2 else ring(value, "gx", 1)
    return below, above


def shards(
    source,
    pressure_old,
    strain_prev,
    motion_old,
    body_force,
    zone_ids,
    drained,
    perm_table,
    lame_table,
    shear_table,
):
    nx, ny, nz = source.shape
    peers = [lax.axis_size(a) for a in AXES]
    count = peers[0] * peers[1] * peers[2]
    rows = up_to(ny + 2 * W, 2 * TILE)
    parts = LANES // (SLOT * nx)
    height = rows // parts
    fields, upward, downward = call(
        pack_rows,
        [f32(NF, nx, ny, nz), f32(nx, MSG_ROWS, nz), f32(nx, MSG_ROWS, nz)],
        source,
        pressure_old,
        strain_prev,
        motion_old,
        body_force,
        zone_ids,
        drained,
    )
    low = ring(upward, "gy", 1)
    high = ring(downward, "gy", -1)

    def lanes_kernel(*refs):
        pack_lanes(peers[1] - 1, *refs)

    tall, rightward, leftward = call(
        lanes_kernel,
        [f32(NF, nx, rows, nz), f32(NF, height, LANES), f32(NF, height, LANES)],
        fields,
        low,
        high,
    )
    below, above = x_neighbours(tall)
    left = ring(rightward, "gz", 1)
    right = ring(leftward, "gz", -1)
    left_below, left_above = x_neighbours(left)
    right_below, right_above = x_neighbours(right)
    tables = jnp.stack([perm_table, lame_table, shear_table])

    depth, lanes = nx + 2 * W, nz + LANES

    def layer(*lead):
        return pltpu.VMEM((*lead, depth, rows, lanes), jnp.float32)

    def kernel(*refs):
        main_kernel(peers, *refs)

    basis, partial = call(
        kernel,
        [f32(27, nx, ny, nz), f32(count, LANES)],
        tables,
        tall,
        below,
        above,
        left,
        right,
        left_below,
        right_below,
        left_above,
        right_above,
        smem=(0,),
        scratch=[layer(NF)]
        + [layer() for _ in range(15)]
        + [layer(3), layer(3), layer(3), layer(9), layer(9)]
        + [pltpu.VMEM((up_to(SUMS, TILE), TILE, LANES), jnp.float32)],
        limit=50 * 2**20,
    )
    sums = lax.all_to_all(partial, AXES, 0, 0, tiled=True)
    return tuple(
        call(
            combine,
            [f32(nx, ny, nz), f32(3, nx, ny, nz), f32(nx, ny, nz)],
            sums,
            basis,
            pressure_old,
            motion_old,
        )
    )


def solution(mesh):
    placed = (
        P("gx", "gy", "gz"),
        P("gx", "gy", "gz"),
        P("gx", "gy", "gz"),
        P(None, "gx", "gy", "gz"),
        P(None, "gx", "gy", "gz"),
        P("gx", "gy", "gz"),
        P("gx", "gy", "gz"),
        P(),
        P(),
        P(),
    )
    return jax.shard_map(
        shards,
        mesh=mesh,
        in_specs=placed,
        out_specs=(P("gx", "gy", "gz"), P(None, "gx", "gy", "gz"), P("gx", "gy", "gz")),
        check_vma=False,
    )
```

time: 356 us -> 62.6 us (0.18)
  blocking collectives: 161 us -> 10.6 us
  starting transfers between devices: 66 us -> 8.01 us
  waiting for transfers between devices: 62.5 us -> 13.4 us
  other arithmetic: 39.3 us -> 0.01 us
  Pallas kernels: 0 us -> 27.6 us
  between operations: 13.4 us -> 0.69 us
  local copies, waits for them, and re-layouts: 11.4 us -> 1.99 us
    psum x4 -> x0, blocking collectives: 161 us -> none  [products(): lax.psum((jnp.sum(residual * precond), jnp.sum(precond * image)), ('gx',...]
    ppermute x30 -> x7, starting transfers between devices: 66 us -> 8.01 us  [ring(): lax.ppermute(value, axis, [(i, (i + step) % peers) for i in range(peers)])]
    ppermute x30 -> x7, waiting for transfers between devices: 62.5 us -> 13.4 us  [ring(): lax.ppermute(value, axis, [(i, (i + step) % peers) for i in range(peers)])]
    pallas_call x0 -> x4, Pallas kernels: none -> 27.6 us  [call(): pl.pallas_call(kernel, out_shape=outs, in_specs=specs, scratch_shapes=scr...]
    unnamed x2 -> x0, other arithmetic: 17.4 us -> none
    all_to_all x0 -> x1, blocking collectives: none -> 10.6 us  [shards(): sums = lax.all_to_all(partial, AXES, 0, 0, tiled=True)]
    add x4 -> x0, other arithmetic: 6.41 us -> none  [the longest x2 3.93 us: conjugate(): tracked = tracked + step_len * direction_pad]
    reduce_sum x5 -> x0, other arithmetic: 5.73 us -> none  [the longest x4 4.03 us: products(): jnp.sum(precond * image)]
  transfers between devices with their start and end apart: 30 -> 7, of which waited for: 20 -> 5; matrix products, arithmetic and copies ran while one was open for 2% -> 0% of each run, Pallas kernels for 0% -> 0%
where the time goes in v1:
time: 62.6 us; the launch traced here: 62.3 us
  Pallas kernels  27.6 us (44%)
  waiting for transfers between devices  13.4 us (21%)
  blocking collectives  10.6 us (17%)
  starting transfers between devices  8.01 us (13%)
  local copies, waits for them, and re-layouts  1.99 us (3%)
  between operations  0.69 us (1%)
    pallas_call x4, Pallas kernels, call(): pl.pallas_call(kernel, out_shape=outs, in_specs=specs, scratch_shapes=scr...  27.6 us
    ppermute x7, waiting for transfers between devices, ring(): lax.ppermute(value, axis, [(i, (i + step) % peers) for i in range(peers)])  13.4 us
    all_to_all x1, blocking collectives, shards(): sums = lax.all_to_all(partial, AXES, 0, 0, tiled=True)  10.6 us
    ppermute x7, starting transfers between devices, ring(): lax.ppermute(value, axis, [(i, (i + step) % peers) for i in range(peers)])  8.01 us
    unnamed x12, local copies, waits for them, and re-layouts  1.99 us
  transfers between devices with their start and end apart: 7, of which 5 were waited for; matrix products, arithmetic and copies ran while one was open for 0% of the time, Pallas kernels for 0%

profile of v1, /device:TPU:0, one launch (start us, length us, event | category | flops | bytes accessed | tf_op | source)
XLA Modules:
  0.0 62.3 jit_solution(1427740248285523624)
XLA Ops:
  0.6 0.0 copy-start.3
  0.6 0.0 copy-start.4
  0.7 0.0 copy-start.5
  0.7 2.2 %shard_map.121 = (f32[10,8,16,128]{3,2,1,0:T(8,128)}, f32[8,40,128]{2,1,0:T(8,128)}, f32[8,40,128]{2,1,0:T(8,128)}) custom-call(f32[8,16,128]{2,1,0:T(8,128)} %source.1, f32[8,16,128]{2,1,0:T(8,128)} %pressure_old.1, f32[8,16,128]{2,1,0:T(8,128)} %strain.1, f32[3,8,16,128]{3,2,1,0:T(8,128)} %motion_old.1, f32[3,8,16,128]{3,2,1,0:T(8,128)} %body.1, ...), custom_call_target="tpu_custom_call" | custom-call | tf_op jit(solution)/shard_map/pallas_call | solution.py:512
  2.8 3.1 %collective-permute-start = (f32[8,40,128]{2,1,0:T(8,128)}, f32[8,40,128]{2,1,0:T(8,128)S(1)}, u32[]{:S(2)}, u32[]{:S(2)}) collective-permute-start(f32[8,40,128]{2,1,0:T(8,128)} %get-tuple-element.12), channel_id=1, source_target_pairs={{0,4},{4,8},{8,12},{12,0},{1,5},{5,9},{9,13},{13,1},{2,6},{6,10},{... | collective-permute-start | bytes 491528 | tf_op jit(solution)/shard_map/ppermute | solution.py:523
  5.9 2.0 %collective-permute-start.1 = (f32[8,40,128]{2,1,0:T(8,128)}, f32[8,40,128]{2,1,0:T(8,128)S(1)}, u32[]{:S(2)}, u32[]{:S(2)}) collective-permute-start(f32[8,40,128]{2,1,0:T(8,128)} %get-tuple-element.13), channel_id=1, source_target_pairs={{0,12},{4,0},{8,4},{12,8},{1,13},{5,1},{9,5},{13,9},{2,14},{6,2},{... | collective-permute-start | bytes 491528 | tf_op jit(solution)/shard_map/ppermute | solution.py:523
  7.9 5.3 %collective-permute-done.refs_1_ = f32[8,40,128]{2,1,0:T(8,128)S(1)} collective-permute-done((f32[8,40,128]{2,1,0:T(8,128)}, f32[8,40,128]{2,1,0:T(8,128)S(1)}, u32[]{:S(2)}, u32[]{:S(2)}) %collective-permute-start) | collective-permute-done | bytes 163872 | tf_op jit(solution)/shard_map/ppermute | solution.py:523
  13.2 0.0 copy-start.1
  13.2 2.0 %collective-permute-done.1.refs_2_ = f32[8,40,128]{2,1,0:T(8,128)S(1)} collective-permute-done((f32[8,40,128]{2,1,0:T(8,128)}, f32[8,40,128]{2,1,0:T(8,128)S(1)}, u32[]{:S(2)}, u32[]{:S(2)}) %collective-permute-start.1) | collective-permute-done | bytes 163872 | tf_op jit(solution)/shard_map/ppermute | solution.py:523
  15.3 0.0 copy-start.2
  15.3 0.0 copy-done.1
  15.3 0.7 %copy-done.2 = f32[8,40,128]{2,1,0:T(8,128)} copy-done((f32[8,40,128]{2,1,0:T(8,128)}, f32[8,40,128]{2,1,0:T(8,128)S(1)}, u32[]{:S(2)}) %copy-start.2) | copy-done | bytes 163864
  15.9 4.0 %shard_map.122 = (f32[10,8,32,128]{3,2,1,0:T(8,128)}, f32[10,16,128]{2,1,0:T(8,128)}, f32[10,16,128]{2,1,0:T(8,128)}) custom-call(f32[10,8,16,128]{3,2,1,0:T(8,128)} %get-tuple-element.11.refs_0_, f32[8,40,128]{2,1,0:T(8,128)} %copy-done.1, f32[8,40,128]{2,1,0:T(8,128)} %copy-done.2), custom_call_target="tpu_custom_call" | custom-call | tf_op jit(solution)/shard_map/pallas_call | solution.py:512
  19.9 0.0 collective-permute-start.2
  19.9 1.5 %collective-permute-start.3 = (f32[10,16,128]{2,1,0:T(8,128)}, f32[10,16,128]{2,1,0:T(8,128)S(1)}, u32[]{:S(2)}, u32[]{:S(2)}) collective-permute-start(f32[10,16,128]{2,1,0:T(8,128)} %get-tuple-element.15), channel_id=1, source_target_pairs={{0,1},{1,2},{2,3},{3,0},{4,5},{5,6},{6,7},{7,4},{8,9},{9,10},{10,1... | collective-permute-start | bytes 245768 | tf_op jit(solution)/shard_map/ppermute | solution.py:523
  21.4 1.4 %collective-permute-start.4 = (f32[10,16,128]{2,1,0:T(8,128)}, f32[10,16,128]{2,1,0:T(8,128)S(1)}, u32[]{:S(2)}, u32[]{:S(2)}) collective-permute-start(f32[10,16,128]{2,1,0:T(8,128)} %get-tuple-element.16), channel_id=1, source_target_pairs={{0,3},{1,0},{2,1},{3,2},{4,7},{5,4},{6,5},{7,6},{8,11},{9,8},{10,9... | collective-permute-start | bytes 245768 | tf_op jit(solution)/shard_map/ppermute | solution.py:523
  22.8 3.5 %collective-permute-done.3.refs_4_ = f32[10,16,128]{2,1,0:T(8,128)S(1)} collective-permute-done((f32[10,16,128]{2,1,0:T(8,128)}, f32[10,16,128]{2,1,0:T(8,128)S(1)}, u32[]{:S(2)}, u32[]{:S(2)}) %collective-permute-start.3) | collective-permute-done | bytes 81952 | tf_op jit(solution)/shard_map/ppermute | solution.py:523
  26.3 0.0 collective-permute-start.5
  26.3 1.3 %collective-permute-done.4.refs_5_ = f32[10,16,128]{2,1,0:T(8,128)S(1)} collective-permute-done((f32[10,16,128]{2,1,0:T(8,128)}, f32[10,16,128]{2,1,0:T(8,128)S(1)}, u32[]{:S(2)}, u32[]{:S(2)}) %collective-permute-start.4) | collective-permute-done | bytes 81952 | tf_op jit(solution)/shard_map/ppermute | solution.py:523
  27.7 0.0 collective-permute-start.6
  27.7 0.0 copy-done.3
  27.7 0.0 copy-done.4
  27.7 0.0 copy-done.5
  27.7 0.0 collective-permute-done.5.refs_6_.refs_8_
  27.7 1.2 %collective-permute-done.6.refs_7_.refs_9_ = f32[10,16,128]{2,1,0:T(8,128)S(1)} collective-permute-done((f32[10,16,128]{2,1,0:T(8,128)S(1)}, f32[10,16,128]{2,1,0:T(8,128)S(1)}, u32[]{:S(2)}, u32[]{:S(2)}) %collective-permute-start.6) | collective-permute-done | bytes 81952 | tf_op jit(solution)/shard_map/ppermute | solution.py:523
  28.9 0.0 collective-permute-done.2.refs_2_.refs_3_
  28.9 0.0 copy-start
  29.0 1.3 %copy-done = f32[10,8,32,128]{3,2,1,0:T(8,128)S(1)} copy-done((f32[10,8,32,128]{3,2,1,0:T(8,128)S(1)}, f32[10,8,32,128]{3,2,1,0:T(8,128)}, u32[]{:S(2)}) %copy-start) | copy-done | bytes 1310744
  30.3 19.1 %shard_map.123 = (f32[27,8,16,128]{3,2,1,0:T(8,128)}, f32[32,128]{1,0:T(8,128)S(1)}) custom-call(f32[3,8]{1,0:T(4,128)S(1)} %pad_maximum_fusion.refs_0_, f32[10,8,32,128]{3,2,1,0:T(8,128)S(1)} %copy-done, f32[10,8,32,128]{3,2,1,0:T(8,128)S(1)} %collective-permute-done.2.refs_2_.refs_3_, f32[10,8,32,128]{3,2,1,0:T(8,128)S(1)} %collective-permute-done.2.refs_2_.refs_3_, ...), custom_call_target="tpu_custom_call" | custom-call | tf_op jit(solution)/shard_map/pallas_call | solution.py:512
  49.3 10.6 %all_to_all.11 = f32[32,1,128]{2,1,0:T(1,128)} all-to-all(f32[32,1,128]{2,1,0:T(1,128)S(1)} %bitcast.7), channel_id=1, replica_groups=mesh['gx'=2,'gy'=4,'gz'=4] {'gx','gy','gz'}, dimensions={0} | all-to-all | bytes 32768 | tf_op jit(solution)/shard_map/all_to_all | solution.py:610
  59.9 2.4 %shard_map.124 = (f32[8,16,128]{2,1,0:T(8,128)}, f32[3,8,16,128]{3,2,1,0:T(8,128)}, f32[8,16,128]{2,1,0:T(8,128)}) custom-call(f32[32,128]{1,0:T(8,128)} %bitcast.8, f32[27,8,16,128]{3,2,1,0:T(8,128)} %get-tuple-element.18.basis, f32[8,16,128]{2,1,0:T(8,128)} %pressure_old.1, f32[3,8,16,128]{3,2,1,0:T(8,128)} %motion_old.1), custom_call_target="tpu_custom_call" | custom-call | tf_op jit(solution)/shard_map/pallas_call | solution.py:512
  (1 shorter events, 0.0 us)
Async XLA Ops:
  0.6 27.0 %copy-start.3 = (f32[8]{0:T(128)S(1)}, f32[8]{0:T(128)}, u32[]{:S(2)}) copy-start(f32[8]{0:T(128)} %param.19) | copy-start | bytes 100
  0.6 27.0 %copy-start.4 = (f32[8]{0:T(128)S(1)}, f32[8]{0:T(128)}, u32[]{:S(2)}) copy-start(f32[8]{0:T(128)} %param.18) | copy-start | bytes 100
  0.7 27.0 %copy-start.5 = (f32[8]{0:T(128)S(1)}, f32[8]{0:T(128)}, u32[]{:S(2)}) copy-start(f32[8]{0:T(128)} %param.17) | copy-start | bytes 100
  2.8 10.4 %collective-permute-start = (f32[8,40,128]{2,1,0:T(8,128)}, f32[8,40,128]{2,1,0:T(8,128)S(1)}, u32[]{:S(2)}, u32[]{:S(2)}) collective-permute-start(f32[8,40,128]{2,1,0:T(8,128)} %get-tuple-element.12), channel_id=1, source_target_pairs={{0,4},{4,8},{8,12},{12,0},{1,5},{5,9},{9,13},{13,1},{2,6},{6,10},{... | collective-permute-start | bytes 491528 | tf_op jit(solution)/shard_map/ppermute | solution.py:523
  5.9 9.4 %collective-permute-start.1 = (f32[8,40,128]{2,1,0:T(8,128)}, f32[8,40,128]{2,1,0:T(8,128)S(1)}, u32[]{:S(2)}, u32[]{:S(2)}) collective-permute-start(f32[8,40,128]{2,1,0:T(8,128)} %get-tuple-element.13), channel_id=1, source_target_pairs={{0,12},{4,0},{8,4},{12,8},{1,13},{5,1},{9,5},{13,9},{2,14},{6,2},{... | collective-permute-start | bytes 491528 | tf_op jit(solution)/shard_map/ppermute | solution.py:523
  13.2 2.1 %copy-start.1 = (f32[8,40,128]{2,1,0:T(8,128)}, f32[8,40,128]{2,1,0:T(8,128)S(1)}, u32[]{:S(2)}) copy-start(f32[8,40,128]{2,1,0:T(8,128)S(1)} %collective-permute-done.refs_1_) | copy-start | bytes 491524
  15.3 0.7 %copy-start.2 = (f32[8,40,128]{2,1,0:T(8,128)}, f32[8,40,128]{2,1,0:T(8,128)S(1)}, u32[]{:S(2)}) copy-start(f32[8,40,128]{2,1,0:T(8,128)S(1)} %collective-permute-done.1.refs_2_) | copy-start | bytes 491524
  19.9 9.1 %collective-permute-start.2 = (f32[10,8,32,128]{3,2,1,0:T(8,128)}, f32[10,8,32,128]{3,2,1,0:T(8,128)S(1)}, u32[]{:S(2)}, u32[]{:S(2)}) collective-permute-start(f32[10,8,32,128]{3,2,1,0:T(8,128)} %get-tuple-element.14.refs_1_), channel_id=1, source_target_pairs={{0,16},{16,0},{1,17},{17,1},{2,18},{18,2},{3,19},{19,3},{4,20},{20... | collective-permute-start | bytes 3932168 | tf_op jit(solution)/shard_map/ppermute | solution.py:523
  19.9 6.4 %collective-permute-start.3 = (f32[10,16,128]{2,1,0:T(8,128)}, f32[10,16,128]{2,1,0:T(8,128)S(1)}, u32[]{:S(2)}, u32[]{:S(2)}) collective-permute-start(f32[10,16,128]{2,1,0:T(8,128)} %get-tuple-element.15), channel_id=1, source_target_pairs={{0,1},{1,2},{2,3},{3,0},{4,5},{5,6},{6,7},{7,4},{8,9},{9,10},{10,1... | collective-permute-start | bytes 245768 | tf_op jit(solution)/shard_map/ppermute | solution.py:523
  21.4 6.3 %collective-permute-start.4 = (f32[10,16,128]{2,1,0:T(8,128)}, f32[10,16,128]{2,1,0:T(8,128)S(1)}, u32[]{:S(2)}, u32[]{:S(2)}) collective-permute-start(f32[10,16,128]{2,1,0:T(8,128)} %get-tuple-element.16), channel_id=1, source_target_pairs={{0,3},{1,0},{2,1},{3,2},{4,7},{5,4},{6,5},{7,6},{8,11},{9,8},{10,9... | collective-permute-start | bytes 245768 | tf_op jit(solution)/shard_map/ppermute | solution.py:523
  26.3 1.4 %collective-permute-start.5 = (f32[10,16,128]{2,1,0:T(8,128)S(1)}, f32[10,16,128]{2,1,0:T(8,128)S(1)}, u32[]{:S(2)}, u32[]{:S(2)}) collective-permute-start(f32[10,16,128]{2,1,0:T(8,128)S(1)} %collective-permute-done.3.refs_4_), channel_id=1, source_target_pairs={{0,16},{16,0},{1,17},{17,1},{2,18},{18,2},{3,19},{19,3},{4,20},{20... | collective-permute-start | bytes 245768 | tf_op jit(solution)/shard_map/ppermute | solution.py:523
  27.7 1.3 %collective-permute-start.6 = (f32[10,16,128]{2,1,0:T(8,128)S(1)}, f32[10,16,128]{2,1,0:T(8,128)S(1)}, u32[]{:S(2)}, u32[]{:S(2)}) collective-permute-start(f32[10,16,128]{2,1,0:T(8,128)S(1)} %collective-permute-done.4.refs_5_), channel_id=1, source_target_pairs={{0,16},{16,0},{1,17},{17,1},{2,18},{18,2},{3,19},{19,3},{4,20},{20... | collective-permute-start | bytes 245768 | tf_op jit(solution)/shard_map/ppermute | solution.py:523
  28.9 1.3 %copy-start = (f32[10,8,32,128]{3,2,1,0:T(8,128)S(1)}, f32[10,8,32,128]{3,2,1,0:T(8,128)}, u32[]{:S(2)}) copy-start(f32[10,8,32,128]{3,2,1,0:T(8,128)} %get-tuple-element.14.refs_1_) | copy-start | bytes 3932164

commit v2 on v0

v2 whole, which is shorter than its diff:
```python
import jax
import jax.numpy as jnp
from jax import lax
from jax.experimental import pallas as pl
from jax.experimental.pallas import tpu as pltpu
from jax.sharding import PartitionSpec as P

ZONES = 8

storage = 0.2
biot_coef = 0.8
leakage = 2.0
support = 1.0

AXES = ("gx", "gy", "gz")
LANES = 128
TILE = 8
MIB = 2**20

ZONE, PRESS, MOTION, SOURCE, DRAIN, BODY = 0, 1, 2, 5, 6, 7
WIDTHS = (5, 5, 5, 5, 5, 4, 4, 2, 2, 2)
NF = len(WIDTHS)
WIDE = 5
W = max(WIDTHS)
OFFSETS = tuple(sum(WIDTHS[:f]) for f in range(NF))
PAIRS = tuple((j, k) for j in range(3) for k in range(j, 3))
SUMS = 4 + 4 * len(PAIRS)
BASIS = 27
SEG = 16
ENDS = 2 * SEG
UNROLL = 4
PACK_LIMIT = 62


def up_to(value, multiple):
    return -(-value // multiple) * multiple


MSG_ROWS = up_to(sum(WIDTHS), TILE)


def iota(shape, dim):
    return lax.broadcasted_iota(jnp.int32, shape, dim)


def pack_rows(*refs):
    sources, (fields, first, second), rest = refs[:7], refs[7:10], refs[10:]
    held, arrived = rest[:7], rest[7]
    copies = [
        pltpu.make_async_copy(source, copy, arrived.at[i])
        for i, (source, copy) in enumerate(zip(sources, held))
    ]
    for copy in copies:
        copy.start()
    for copy in copies:
        copy.wait()
    source, pressure, strain, motion, body, zones, drained = held
    nx, ny, nz = source.shape
    spare = MSG_ROWS - sum(WIDTHS)
    for x in range(nx):
        values = [
            zones[x].astype(jnp.float32) + 1.0,
            pressure[x],
            motion[0, x],
            motion[1, x],
            motion[2, x],
            source[x] + biot_coef * strain[x],
            drained[x].astype(jnp.float32),
            body[0, x],
            body[1, x],
            body[2, x],
        ]
        for f, value in enumerate(values):
            fields[f, x] = value
        if spare:
            empty = jnp.zeros((spare, nz), jnp.float32)
            first[x, MSG_ROWS - spare :, :] = empty
            second[x, MSG_ROWS - spare :, :] = empty

    def messages(upward, downward):
        for x in range(nx):
            for f in range(NF):
                width, offset = WIDTHS[f], OFFSETS[f]
                upward[x, offset : offset + width, :] = fields[f, x, ny - width :, :]
                downward[x, offset : offset + width, :] = fields[f, x, :width, :]

    even = lax.axis_index("gy") % 2 == 0
    pl.when(even)(lambda: messages(first, second))
    pl.when(jnp.logical_not(even))(lambda: messages(second, first))


class Rows:
    def __init__(self, first, second, peers):
        self.refs = first, second
        self.even = lax.axis_index("gy") % 2 == 0
        self.keep = keeps("gy", peers[1])

    def read(self, f, x):
        width, offset = WIDTHS[f], OFFSETS[f]
        a, b = [ref[x, offset : offset + width, :] for ref in self.refs]
        low, high = jnp.where(self.even, b, a), jnp.where(self.even, a, b)
        return low * self.keep[0], high * self.keep[1]


def keeps(axis, peers):
    at = lax.axis_index(axis)
    return jnp.where(at > 0, 1.0, 0.0), jnp.where(at < peers - 1, 1.0, 0.0)


def pack_ends(peers, fields, first, second, ends, rightward, leftward, stage):
    _, nx, ny, nz = fields.shape
    tall = ny + 2 * TILE
    pack = LANES // tall
    rows = Rows(first, second, peers)
    gap = jnp.zeros((TILE, nz), jnp.float32)
    inner = SEG - W
    spare = MSG_ROWS - sum(WIDTHS)
    for g in range(nx // pack):
        if spare:
            empty = jnp.zeros((spare, LANES), jnp.float32)
            rightward[g, MSG_ROWS - spare :, :] = empty
            leftward[g, MSG_ROWS - spare :, :] = empty
        for f in range(NF):
            width, offset = WIDTHS[f], OFFSETS[f]
            slot = g * NF + f
            for i in range(pack):
                x = g * pack + i
                top = i * tall
                stage[slot, top : top + TILE, :] = gap
                stage[slot, top + TILE + ny : top + tall, :] = gap
                stage[slot, top + TILE : top + TILE + ny, :] = fields[f, x]
                low, high = rows.read(f, x)
                stage[slot, top + TILE - width : top + TILE, :] = low
                stage[slot, top + TILE + ny : top + TILE + ny + width, :] = high
            begin = stage[slot, :, :LANES].T
            finish = begin if nz == LANES else stage[slot, :, nz - LANES :].T
            rightward[g, offset : offset + width, :] = finish[LANES - width :]
            leftward[g, offset : offset + width, :] = begin[:width]
            ends[f, g, :TILE, :] = jnp.zeros((TILE, LANES), jnp.float32)
            ends[f, g, ENDS - TILE :, :] = jnp.zeros((TILE, LANES), jnp.float32)
            ends[f, g, W:SEG, :] = begin[:inner]
            ends[f, g, SEG : ENDS - W, :] = finish[LANES - inner :]


def harmonic(a, b):
    return 2.0 * a * b / jnp.maximum(a + b, 1e-30)


def lookup(zone, tables):
    picked = [jnp.zeros(zone.shape, jnp.float32) for _ in tables]
    for index in range(ZONES):
        here = zone == float(index + 1)
        picked = [
            jnp.where(here, table[row, index], value)
            for (table, row), value in zip(tables, picked)
        ]
    return picked


def fixed_term(zone, lame, shear):
    scale = jnp.maximum(lame + 2.0 * shear / 3.0, 1e-30)
    return jnp.where(zone > 0.0, biot_coef * biot_coef / scale, 0.0)


KEPT = ("motion", "z0", "p0", "zs", "ps")
ARRAYS = (
    ("zone", 0),
    ("press", 0),
    ("motion", 3),
    ("load", 0),
    ("drain", 0),
    ("body", 3),
    ("perm", 0),
    ("heft", 0),
    ("shear", 0),
    ("fixed", 0),
    ("tx", 0),
    ("ty", 0),
    ("tz", 0),
    ("mx", 0),
    ("my", 0),
    ("mz", 0),
    ("react", 0),
    ("pdiag", 0),
    ("pinv", 0),
    ("z0", 0),
    ("p0", 0),
    ("ediag", 3),
    ("einv", 3),
    ("push", 3),
    ("zs", 9),
    ("ps", 9),
)


class Domain:
    def __init__(self, arrays):
        self.__dict__.update(arrays)

    def press_faces(self, l):
        own = self.perm[l]
        self.tx[l] = harmonic(own, self.nxt(self.perm, l))
        self.ty[l] = harmonic(own, self.yp(own))
        self.tz[l] = harmonic(own, self.zp(own))

    def motion_faces(self, l):
        own = self.shear[l]
        self.mx[l] = harmonic(own, self.nxt(self.shear, l))
        self.my[l] = harmonic(own, self.yp(own))
        self.mz[l] = harmonic(own, self.zp(own))

    def steps(self, ref, l):
        own = ref[l]
        return self.nxt(ref, l) - own, self.yp(own) - own, self.zp(own) - own

    def back_y(self, value):
        return self.ym(value) - value

    def back_z(self, value):
        return self.zm(value) - value

    def press_flux(self, ref, l, along_y=True):
        dx, dy, dz = self.steps(ref, l)
        total = self.back_x(self.tx, dx, ref, l) + self.back_z(self.tz[l] * dz)
        return total + self.back_y(self.ty[l] * dy) if along_y else total

    def y_terms(self, l):
        face = self.ty[l]
        own, middle = self.press[l], self.motion[1, l]
        return (
            face + self.ym(face),
            self.back_y(face * (self.yp(own) - own))
            + (0.5 * biot_coef) * (self.yp(middle) - self.ym(middle)),
        )

    def press_start(self, l):
        face_sum, y_part = self.y_terms(l)
        face = self.tz[l]
        leak = leakage * self.drain[l]
        reaction = storage + self.fixed[l] + leak
        diag = (
            reaction
            + self.tx[l]
            + self.prv(self.tx, l)
            + face_sum
            + (face + self.zm(face))
        )
        inverse = jnp.where(self.zone[l] > 0.0, 1.0 / diag, 0.0)
        along_x, along_z = self.motion.at[0], self.motion[2, l]
        change = (self.nxt(along_x, l) - self.prv(along_x, l)) + (
            self.zp(along_z) - self.zm(along_z)
        )
        residual = (
            self.load[l]
            - (0.5 * biot_coef) * change
            - leak * self.press[l]
            - self.press_flux(self.press, l, False)
            - y_part
        )
        self.react[l] = reaction
        self.pdiag[l] = diag
        self.pinv[l] = inverse
        self.z0[l] = residual * inverse

    def press_next(self, l):
        image = self.react[l] * self.z0[l] + self.press_flux(self.z0, l)
        self.p0[l] = image * self.pinv[l]

    @staticmethod
    def parts(ref, j):
        return [ref.at[3 * j + c] for c in range(3)]

    def elastic(self, refs, l, j):
        steps = [self.steps(ref, l) for ref in refs]
        pushed = self.heft[l] * (steps[0][0] + steps[1][1] + steps[2][2])
        self.keep_push(j, l, pushed)
        out = []
        for c in range(3):
            dx, dy, dz = steps[c]
            step_y, step_z = self.my[l] * dy, self.mz[l] * dz
            if c == 1:
                step_y = step_y + pushed
            if c == 2:
                step_z = step_z + pushed
            push = (j, pushed) if c == 0 else None
            out.append(
                support * refs[c][l]
                + self.back_x(self.mx, dx, refs[c], l, push)
                + self.back_y(step_y)
                + self.back_z(step_z)
            )
        return out

    def gradient(self, ref, l):
        own = ref[l]
        return (
            0.5 * (self.nxt(ref, l) - self.prv(ref, l)),
            0.5 * (self.yp(own) - self.ym(own)),
            0.5 * (self.zp(own) - self.zm(own)),
        )

    def motion_start(self, l):
        weight = self.heft[l]
        along_y, along_z = self.my[l], self.mz[l]
        base = (
            support
            + self.mx[l]
            + self.prv(self.mx, l)
            + (along_y + self.ym(along_y))
            + (along_z + self.zm(along_z))
            + weight
        )
        inside = self.zone[l] > 0.0
        beside = (self.prv(self.heft, l), self.ym(weight), self.zm(weight))
        image = self.elastic(self.parts(self.motion, 0), l, 0)
        grads = [self.gradient(ref, l) for ref in (self.press, self.z0, self.p0)]
        for c in range(3):
            diag = base + beside[c]
            inverse = jnp.where(inside, 1.0 / diag, 0.0)
            self.ediag[c, l] = diag
            self.einv[c, l] = inverse
            start = self.body[c, l] - biot_coef * grads[0][c] - image[c]
            self.zs[c, l] = start * inverse
            scale = -biot_coef * inverse
            self.zs[3 + c, l] = grads[1][c] * scale
            self.zs[6 + c, l] = grads[2][c] * scale

    def motion_next(self, l, j):
        image = self.elastic(self.parts(self.zs, j), l, j)
        for c in range(3):
            self.ps[3 * j + c, l] = image[c] * self.einv[c, l]

    def stages(self):
        self.run(4, self.press_faces, 1)
        self.run(4, self.press_start)
        self.run(3, self.press_next)
        self.run(2, self.motion_faces, 1)
        self.lead(2, lambda l: self.first_push(self.parts(self.motion, 0), l, 0))
        self.run(2, self.motion_start)
        for j in range(3):
            self.lead(1, lambda l: self.first_push(self.parts(self.zs, j), l, j))
            self.run(1, lambda l: self.motion_next(l, j))

    def finish(self, l, acc, mask):
        own = self.own

        def add(index, value):
            acc[index] = acc[index] + self.fold(value, mask)

        def total(pairs):
            out = None
            for a, b in pairs:
                out = a * b if out is None else out + a * b
            return out

        a, b = own(self.z0[l]), own(self.p0[l])
        diag = own(self.pdiag[l])
        scaled = diag * b
        add(0, diag * a * a)
        add(1, scaled * a)
        add(2, scaled * b)
        energy = own(self.react[l]) * b * b
        for face, step in zip((self.tx, self.ty, self.tz), self.steps(self.p0, l)):
            step = own(step)
            energy = energy + own(face[l]) * step * step
        add(3, energy)
        diags = [own(self.ediag[c, l]) for c in range(3)]
        faces = [own(ref[l]) for ref in (self.mx, self.my, self.mz)]
        weight = own(self.heft[l])
        za, pa, dz, dp, steps, heavy = [], [], [], [], [], []
        for j in range(3):
            zj, pj = self.parts(self.zs, j), self.parts(self.ps, j)
            za.append([own(ref[l]) for ref in zj])
            pa.append([own(ref[l]) for ref in pj])
            dz.append([d * v for d, v in zip(diags, za[j])])
            dp.append([d * v for d, v in zip(diags, pa[j])])
            moved = [[own(v) for v in self.steps(ref, l)] for ref in pj]
            div = moved[0][0] + moved[1][1] + moved[2][2]
            flat = [(faces[d], moved[c][d]) for c in range(3) for d in range(3)]
            steps.append([v for _, v in flat] + [div] + pa[j])
            heavy.append([f * v for f, v in flat] + [weight * div])
            heavy[j] = heavy[j] + [support * v for v in pa[j]]
        for i, (j, k) in enumerate(PAIRS):
            add(4 + i, total(zip(dz[j], za[k])))
            add(10 + i, total(zip(dp[k], za[j])))
            add(16 + i, total(zip(dp[j], pa[k])))
            add(22 + i, total(zip(heavy[j], steps[k])))

    @staticmethod
    def loop(start, count, body, unroll=UNROLL):
        if not isinstance(count, int):
            unroll = 1
        chunks = count // unroll

        def step(i, carry):
            for u in range(unroll):
                body(start + i * unroll + u)
            return carry

        if isinstance(chunks, int) and chunks == 1:
            step(0, 0)
        else:
            lax.fori_loop(0, chunks, step, 0)
        if isinstance(count, int):
            for u in range(chunks * unroll, count):
                body(start + u)


class Brick(Domain):
    def nxt(self, ref, l):
        return ref[l + 1]

    def prv(self, ref, l):
        return ref[l - 1]

    def yp(self, v):
        return pltpu.roll(v, v.shape[0] - 1, 0)

    def ym(self, v):
        return pltpu.roll(v, 1, 0)

    def zp(self, v):
        return pltpu.roll(v, v.shape[1] - 1, 1)

    def zm(self, v):
        return pltpu.roll(v, 1, 1)

    def back_x(self, faces, step, ref, l, push=None):
        out = faces[l - 1] * (ref[l] - ref[l - 1]) - faces[l] * step
        if push:
            out = out + (self.push[push[0], l - 1] - push[1])
        return out

    def keep_push(self, j, l, value):
        self.push[j, l] = value

    def first_push(self, refs, l, j):
        dx, dy, dz = [self.steps(ref, l)[i] for i, ref in enumerate(refs)]
        self.push[j, l] = self.heft[l] * (dx + dy + dz)

    def own(self, v):
        return v[: self.ny]

    def fold(self, value, mask):
        total = value[:TILE]
        for start in range(TILE, value.shape[0], TILE):
            total = total + value[start : start + TILE]
        total = jnp.where(mask, total, 0.0)
        folded = total[:, :LANES]
        for start in range(LANES, value.shape[1], LANES):
            folded = folded + total[:, start : start + LANES]
        return folded

    def first(self, halo):
        return W - halo * self.has_below

    def reach(self, halo):
        if self.pair:
            return halo
        return halo * (self.has_below + self.has_above)

    def run(self, halo, body, before=0):
        self.loop(self.first(halo) - before, self.nx + self.reach(halo) + before, body)

    def lead(self, halo, body):
        body(self.first(halo) - 1)

    def narrow(self, v):
        ny = self.ny
        upper, lower = v[ny : ny + TILE], v[ny + TILE :]
        both = jnp.where(iota(upper.shape, 0) < TILE // 2, upper, lower)
        return jnp.concatenate([v[:ny], both], axis=0)

    def press_faces(self, l):
        own = self.perm[l]
        self.tx[l] = harmonic(own, self.nxt(self.perm, l))
        tall = self.perm_tall[l]
        face = harmonic(tall, self.yp(tall))
        self.ty_tall[l] = face
        self.ty[l] = self.narrow(face)
        self.tz[l] = harmonic(own, self.zp(own))

    def y_terms(self, l):
        face = self.ty_tall[l]
        own, middle = self.tall[PRESS, l], self.tall[MOTION + 1, l]
        return (
            self.narrow(face + self.ym(face)),
            self.narrow(
                self.back_y(face * (self.yp(own) - own))
                + (0.5 * biot_coef) * (self.yp(middle) - self.ym(middle))
            ),
        )

    def assemble(self, l, x, fields, beside, tables):
        ny = self.ny
        rows = ny + 2 * TILE
        gap = jnp.zeros((2 * TILE, fields.shape[3]), jnp.float32)
        narrow_rows = ny + TILE
        slim = (self.load, self.drain) + tuple(self.body.at[c] for c in range(3))
        for f in range(NF):
            width = WIDTHS[f]
            below, above = beside.read(f, x)
            if f < WIDE:
                self.tall[f, l, :ny, :] = fields[f, x]
                self.tall[f, l, ny:, :] = gap
                self.tall[f, l, ny : ny + width, :] = above
                self.tall[f, l, rows - width :, :] = below
            else:
                ref = slim[f - WIDE]
                ref[l, :ny, :] = fields[f, x]
                ref[l, ny:, :] = gap[:TILE]
                ref[l, ny : ny + width, :] = above
                ref[l, narrow_rows - width :, :] = below
        tall_zone = self.tall[ZONE, l]
        (perm,) = lookup(tall_zone, tables[:1])
        self.perm_tall[l] = perm
        self.perm[l] = self.narrow(perm)
        zone = self.narrow(tall_zone)
        self.zone[l] = zone
        lame, shear = lookup(zone, tables[1:])
        self.heft[l] = lame + shear
        self.shear[l] = shear
        self.fixed[l] = fixed_term(zone, lame, shear)
        self.press[l] = self.narrow(self.tall[PRESS, l])
        for c in range(3):
            self.motion[c, l] = self.narrow(self.tall[MOTION + c, l])


def brick_kernel(peers, *refs):
    table, fields, below, above = refs[:4]
    rows = [Rows(*refs[i : i + 2], peers) for i in (4, 6, 8)]
    outs, acc, scratch = refs[10 : 10 + len(KEPT)], refs[10 + len(KEPT)], refs[11 + len(KEPT) :]
    inner = len(ARRAYS) - len(KEPT)
    names = [name for name, _ in ARRAYS if name not in KEPT]
    domain = Brick(dict(zip(names, scratch[:inner])))
    domain.__dict__.update(zip(KEPT, outs))
    domain.tall, domain.perm_tall, domain.ty_tall = scratch[inner:]
    tables = [(table, i) for i in range(3)]
    _, nx, ny, nz = fields.shape
    domain.nx, domain.ny = nx, ny
    at = lax.axis_index("gx")
    domain.has_below = (at > 0).astype(jnp.int32)
    domain.has_above = (at < peers[0] - 1).astype(jnp.int32)
    domain.pair = peers[0] == 2

    empty = jnp.zeros((ny + TILE, nz), jnp.float32)
    for l in (W - 1, W + nx):
        for name in ("perm", "heft", "shear", "press", "z0", "p0"):
            getattr(domain, name)[l] = empty
        for c in range(3):
            domain.motion[c, l] = empty
        for i in range(9):
            domain.zs[i, l] = empty
            domain.ps[i, l] = empty
        domain.perm_tall[l] = jnp.zeros((ny + 2 * TILE, nz), jnp.float32)

    def block(start, count, shift, *source):
        domain.loop(
            start, count, lambda l: domain.assemble(l, l + shift, *source, tables)
        )

    block(W, nx, -W, fields, rows[0])
    if domain.pair:
        start = jnp.where(at > 0, 0, W + nx)
        shift = jnp.where(at > 0, nx - W, -W - nx)
        block(start, W, shift, below, rows[1])
    else:
        block(0, W * domain.has_below, nx - W, below, rows[1])
        block(W + nx, W * domain.has_above, -W - nx, above, rows[2])
    domain.stages()
    acc[...] = jnp.zeros(acc.shape, jnp.float32)
    column = iota((TILE, nz), 1)
    mask = (column >= W) & (column < nz - W)
    domain.loop(W, nx, lambda l: domain.finish(l, acc, mask))


class Ends(Domain):
    def roll(self, v, shift):
        return pltpu.roll(v, shift % LANES, v.ndim - 1)

    def nxt(self, ref, l):
        moved = self.roll(ref[pl.ds(l.start, l.size + 1)], -self.row)
        lane = iota(moved[1:].shape, 2)
        return jnp.where(lane < LANES - self.row, moved[:-1], moved[1:])

    def before(self, v):
        moved = self.roll(v, self.row)
        back = jnp.concatenate([jnp.zeros_like(moved[:1]), moved[:-1]], axis=0)
        return jnp.where(iota(moved.shape, 2) >= self.row, moved, back)

    def prv(self, ref, l):
        return self.before(ref[l])

    def back_x(self, faces, step, ref, l, push=None):
        value = faces[l] * step
        if push:
            value = value + push[1]
        return self.before(value) - value

    def keep_push(self, j, l, value):
        pass

    def yp(self, v):
        return self.roll(v, -1)

    def ym(self, v):
        return self.roll(v, 1)

    def zp(self, v):
        return pltpu.roll(v, ENDS - 1, 1)

    def zm(self, v):
        return pltpu.roll(v, 1, 1)

    def own(self, v):
        return v

    def fold(self, value, mask):
        total = None
        for g in range(value.shape[0]):
            part = jnp.where(mask, value[g], 0.0)
            for start in range(0, value.shape[1], TILE):
                piece = part[start : start + TILE]
                total = piece if total is None else total + piece
        return total

    def run(self, halo, body, before=0):
        body(pl.ds(0, self.groups))

    def lead(self, halo, body):
        pass

    def assemble(self, l, g, keep, ends, left, right, keep_left, keep_right):
        for f in range(NF):
            width, offset = WIDTHS[f], OFFSETS[f]
            self.raw[f, l] = ends[f, g] * keep
            self.raw[f, l, W - width : W, :] = left[g, offset : offset + width, :] * (
                keep_left * keep
            )
            self.raw[f, l, ENDS - W : ENDS - W + width, :] = right[
                g, offset : offset + width, :
            ] * (keep_right * keep)

    def materials(self, tables):
        for g in range(self.groups):
            zone = self.raw[ZONE, g]
            perm, lame, shear = lookup(zone, tables)
            self.perm[g] = perm
            self.heft[g] = lame + shear
            self.shear[g] = shear
            self.fixed[g] = fixed_term(zone, lame, shear)


def own_groups(count, peers):
    return count * lax.axis_index("gx") if peers[0] == 2 else count


def ends_kernel(peers, tall, *refs):
    table, ends, below, above, left, right = refs[:6]
    left_below, right_below, left_above, right_above, added = refs[6:11]
    raw, z0, p0, zs, ps, partial = refs[11:17]
    acc, scratch = refs[17], refs[18:]
    names = [name for name, _ in ARRAYS[6:] if name not in KEPT]
    domain = Ends(dict(zip(names, scratch)))
    domain.raw, domain.z0, domain.p0, domain.zs, domain.ps = raw, z0, p0, zs, ps
    domain.zone, domain.press = raw.at[ZONE], raw.at[PRESS]
    domain.motion = raw.at[MOTION : MOTION + 3]
    domain.load, domain.drain = raw.at[SOURCE], raw.at[DRAIN]
    domain.body = raw.at[BODY : BODY + 3]
    domain.row = tall
    count = ends.shape[1]
    domain.groups = groups = raw.shape[1] - 1
    at = lax.axis_index("gx")
    keep = keeps("gz", peers[2])
    empty = jnp.zeros((ENDS, LANES), jnp.float32)
    for ref in (raw, zs, ps):
        for i in range(ref.shape[0]):
            ref[i, groups] = empty
    for ref in (domain.perm, domain.shear, z0, p0):
        ref[groups] = empty
    mine = own_groups(count, peers)
    if peers[0] == 2:
        blocks = [
            (mine, 1.0, ends, left, right),
            (count * (1 - at), 1.0, below, left_below, right_below),
        ]
    else:
        keep_below, keep_above = keeps("gx", peers[0])
        blocks = [
            (0, keep_below, below, left_below, right_below),
            (mine, 1.0, ends, left, right),
            (mine + count, keep_above, above, left_above, right_above),
        ]
    for start, keep_block, *source in blocks:
        for g in range(count):
            domain.assemble(start + g, g, keep_block, *source, *keep)
    domain.materials([(table, i) for i in range(3)])
    domain.stages()
    acc[...] = added[...]
    shape = (ENDS, LANES)
    column, row = iota(shape, 0), iota(shape, 1) % tall
    at_end = ((column >= W) & (column < 2 * W)) | (
        (column >= ENDS - 2 * W) & (column < ENDS - W)
    )
    mask = at_end & (row >= TILE) & (row < tall - TILE)
    domain.finish(pl.ds(mine, count), acc, mask)

    sums = jnp.concatenate(
        [jnp.sum(acc[i], axis=0, keepdims=True) for i in range(acc.shape[0])], axis=0
    )
    totals = jnp.sum(sums, axis=1, keepdims=True)
    spread = jnp.where(iota(sums.shape, 0) == iota(sums.shape, 1), totals, 0.0)
    line = jnp.sum(spread, axis=0, keepdims=True)
    partial[...] = jnp.broadcast_to(line, partial.shape)


def step_sizes(gamma, delta, cross, energy):
    first = gamma / delta
    gamma_new = gamma - 2.0 * first * delta + first * first * cross
    curved = delta - 2.0 * first * cross + first * first * energy
    ratio = gamma_new / gamma
    second = gamma_new / (curved - ratio * gamma_new / first)
    return first + second * (1.0 + ratio), -first * second


def combine(peers, tall, *refs):
    sums, (old, z0, p0, zs, ps), fields = refs[0], refs[1:6], refs[6]
    raw, ends_z0, ends_p0, ends_zs, ends_ps = refs[7:12]
    pressure, motion, strain, moved, ends_moved, turned = refs[12:]
    line = jnp.sum(sums[...], axis=0, keepdims=True)
    lane = iota(line.shape, 1)

    def value(index):
        return jnp.sum(jnp.where(lane == index, line, 0.0), axis=1, keepdims=True)

    c1, c2 = step_sizes(*[value(i) for i in range(4)])
    weights = (jnp.ones_like(c1), c1, c2)

    def form(start):
        total = 0.0
        for i, (j, k) in enumerate(PAIRS):
            scale = 1.0 if j == k else 2.0
            total = total + scale * weights[j] * weights[k] * value(start + i)
        return total

    d1, d2 = step_sizes(form(4), form(10), form(16), form(22))
    on_z = [d1 * w for w in weights]
    on_p = [d2 * w for w in weights]

    def new_motion(start, z_part, p_part, c, i):
        total = start
        for j in range(3):
            total = total + on_z[j] * z_part[3 * j + c, i]
            total = total + on_p[j] * p_part[3 * j + c, i]
        return total

    nx, ny, nz = pressure.shape
    pack = LANES // tall
    ends = Ends(dict(row=tall))
    groups = raw.shape[1] - 1
    count = groups // (2 if peers[0] == 2 else 3)
    mine = own_groups(count, peers)
    every = pl.ds(0, groups)
    for c in range(3):
        for g in range(groups):
            ends_moved[c, g] = new_motion(raw[MOTION + c, g], ends_zs, ends_ps, c, g)
        ends_moved[c, groups] = jnp.zeros((ENDS, LANES), jnp.float32)
    along_y, along_z = ends_moved[1, every], ends_moved[2, every]
    first = ends_moved.at[0]
    ends_moved[3, every] = 0.5 * (
        (ends.nxt(first, every) - ends.prv(first, every))
        + (ends.yp(along_y) - ends.ym(along_y))
        + (ends.zp(along_z) - ends.zm(along_z))
    )
    for c in range(3):
        around = 1 if c == 0 else 0
        for l in range(W - around, W + nx + around):
            moved[c, l] = new_motion(old[c, l], zs, ps, c, l)
    brick = Brick({})
    outs = [pressure] + [motion.at[c] for c in range(3)] + [strain]
    for g in range(count):
        at = mine + g
        edges = [raw[PRESS, at] + c1 * ends_z0[at] + c2 * ends_p0[at]]
        edges = edges + [ends_moved[c, at] for c in range(4)]
        flipped = []
        for o, edge in enumerate(edges):
            slot = g * len(outs) + o
            turned[slot, :W, :] = edge[W : 2 * W]
            turned[slot, LANES - W :, :] = edge[ENDS - 2 * W : ENDS - W]
            flipped.append(turned[slot].T)
        for i in range(pack):
            x = g * pack + i
            l = W + x
            top = i * tall + TILE
            column = iota((ny, LANES), 1)
            u = [moved[c, l] for c in range(3)]
            change = (
                (moved[0, l + 1] - moved[0, l - 1])
                + (brick.yp(u[1]) - brick.ym(u[1]))
                + (brick.zp(u[2]) - brick.zm(u[2]))
            )
            results = [fields[PRESS, x] + c1 * z0[l, :ny, :] + c2 * p0[l, :ny, :]]
            results = results + [v[:ny] for v in u] + [0.5 * change[:ny]]
            for out, result, edge in zip(outs, results, flipped):
                edge = edge[top : top + ny]
                if nz == LANES:
                    inner = (column >= W) & (column < LANES - W)
                    out[x] = jnp.where(inner, result, edge)
                else:
                    out[x] = result
                    out[x, :, :LANES] = jnp.where(column >= W, result[:, :LANES], edge)
                    out[x, :, nz - LANES :] = jnp.where(
                        column < LANES - W, result[:, nz - LANES :], edge
                    )


def f32(*shape):
    return jax.ShapeDtypeStruct(shape, jnp.float32)


def vmem(*shape):
    return pltpu.VMEM(shape, jnp.float32)


def call(kernel, outs, *args, smem=0, space=pltpu.VMEM, scratch=(), limit=8, cost=None):
    specs = [
        pl.BlockSpec(memory_space=pltpu.SMEM if i < smem else space)
        for i in range(len(args))
    ]
    return pl.pallas_call(
        kernel,
        out_shape=outs,
        in_specs=specs,
        scratch_shapes=scratch,
        cost_estimate=cost,
        compiler_params=pltpu.CompilerParams(vmem_limit_bytes=limit * MIB),
    )(*args)


def ring(value, axis, step):
    peers = lax.axis_size(axis)
    return lax.ppermute(value, axis, [(i, (i + step) % peers) for i in range(peers)])


def pairs(value, axis, start):
    peers = lax.axis_size(axis)
    swaps = [(i, i) for i in range(start)]
    for i in range(start, peers - 1, 2):
        swaps += [(i, i + 1), (i + 1, i)]
    swaps += [(i, i) for i in range(len(swaps), peers)]
    return lax.ppermute(value, axis, swaps)


def x_neighbours(value):
    peers = lax.axis_size("gx")
    above = ring(value, "gx", -1)
    below = above if peers == 2 else ring(value, "gx", 1)
    return below, above


def shards(
    source,
    pressure_old,
    strain_prev,
    motion_old,
    body_force,
    zone_ids,
    drained,
    perm_table,
    lame_table,
    shear_table,
):
    nx, ny, nz = source.shape
    peers = [lax.axis_size(a) for a in AXES]
    total = peers[0] * peers[1] * peers[2]
    table = jnp.stack([perm_table, lame_table, shear_table])
    tall = ny + 2 * TILE
    groups = nx * tall // LANES

    def with_peers(kernel, *more):
        return lambda *refs: kernel(peers, *more, *refs)

    raw = (
        source,
        pressure_old,
        strain_prev,
        motion_old,
        body_force,
        zone_ids,
        drained,
    )
    fields, first, second = call(
        pack_rows,
        [f32(NF, nx, ny, nz), f32(nx, MSG_ROWS, nz), f32(nx, MSG_ROWS, nz)],
        *raw,
        space=pltpu.HBM,
        scratch=[pltpu.VMEM(a.shape, a.dtype) for a in raw]
        + [pltpu.SemaphoreType.DMA((len(raw),))],
        limit=PACK_LIMIT,
    )
    fields_below, fields_above = x_neighbours(fields)
    first = pairs(first, "gy", 0)
    second = pairs(second, "gy", 1)
    first_below, first_above = x_neighbours(first)
    second_below, second_above = x_neighbours(second)
    ends, rightward, leftward = call(
        with_peers(pack_ends),
        [
            f32(NF, groups, ENDS, LANES),
            f32(groups, MSG_ROWS, LANES),
            f32(groups, MSG_ROWS, LANES),
        ],
        fields,
        first,
        second,
        scratch=[vmem(NF * groups, LANES, nz)],
    )
    left = ring(rightward, "gz", 1)
    right = ring(leftward, "gz", -1)
    ends_below, ends_above = x_neighbours(ends)
    depth = nx + 2 * W
    cells = depth * ny * nz

    def shaped(lead, *shape):
        return (lead,) * (lead > 0) + shape

    leads = dict(ARRAYS)
    sums_shape = (up_to(SUMS, TILE), TILE, LANES)
    *kept, added = call(
        with_peers(brick_kernel),
        [f32(*shaped(leads[name], depth, ny + TILE, nz)) for name in KEPT]
        + [f32(*sums_shape)],
        table,
        fields,
        fields_below,
        fields_above,
        first,
        second,
        first_below,
        second_below,
        first_above,
        second_above,
        smem=1,
        scratch=[
            vmem(*shaped(lead, depth, ny + TILE, nz))
            for name, lead in ARRAYS
            if name not in KEPT
        ]
        + [vmem(WIDE, depth, tall, nz), vmem(depth, tall, nz), vmem(depth, tall, nz)],
        limit=24,
        cost=pl.CostEstimate(
            flops=2000 * cells, transcendentals=0, bytes_accessed=400 * cells
        ),
    )
    left, right, added = lax.optimization_barrier((left, right, added))
    left_below, left_above = x_neighbours(left)
    right_below, right_above = x_neighbours(right)
    span = (2 if peers[0] == 2 else 3) * groups + 1
    *ends_kept, partial = call(
        with_peers(ends_kernel, tall),
        [f32(NF, span, ENDS, LANES)]
        + [f32(*shaped(leads[name], span, ENDS, LANES)) for name in KEPT[1:]]
        + [f32(total, LANES)],
        table,
        ends,
        ends_below,
        ends_above,
        left,
        right,
        left_below,
        right_below,
        left_above,
        right_above,
        added,
        smem=1,
        scratch=[vmem(*sums_shape)]
        + [
            vmem(*shaped(lead, span, ENDS, LANES))
            for name, lead in ARRAYS[6:]
            if name not in KEPT
        ],
        limit=16,
    )
    sums = lax.all_to_all(partial, AXES, 0, 0, tiled=True)
    return tuple(
        call(
            with_peers(combine, tall),
            [f32(nx, ny, nz), f32(3, nx, ny, nz), f32(nx, ny, nz)],
            sums,
            *kept,
            fields,
            *ends_kept,
            scratch=[
                vmem(3, depth, ny + TILE, nz),
                vmem(4, span, ENDS, LANES),
                vmem(5 * groups, LANES, LANES),
            ],
            limit=16,
        )
    )


def solution(mesh):
    placed = (
        P("gx", "gy", "gz"),
        P("gx", "gy", "gz"),
        P("gx", "gy", "gz"),
        P(None, "gx", "gy", "gz"),
        P(None, "gx", "gy", "gz"),
        P("gx", "gy", "gz"),
        P("gx", "gy", "gz"),
        P(),
        P(),
        P(),
    )
    return jax.shard_map(
        shards,
        mesh=mesh,
        in_specs=placed,
        out_specs=(P("gx", "gy", "gz"), P(None, "gx", "gy", "gz"), P("gx", "gy", "gz")),
        check_vma=False,
    )
```

time: 356 us -> 45 us (0.13)
  blocking collectives: 161 us -> 13.3 us
  waiting for transfers between devices: 62.5 us -> 4.33 us
  starting transfers between devices: 66 us -> 9.86 us
  other arithmetic: 39.3 us -> 0.7 us
  Pallas kernels: 0 us -> 13.7 us
  between operations: 13.4 us -> 0.71 us
  local copies, waits for them, and re-layouts: 11.4 us -> 2.17 us
    psum x4 -> x0, blocking collectives: 161 us -> none  [products(): lax.psum((jnp.sum(residual * precond), jnp.sum(precond * image)), ('gx',...]
    ppermute x30 -> x10, waiting for transfers between devices: 62.5 us -> 4.33 us  [the longest x2 3.44 us: pairs(): return lax.ppermute(value, axis, swaps)]
    ppermute x30 -> x10, starting transfers between devices: 66 us -> 9.86 us  [the longest x8 5.66 us: ring(): lax.ppermute(value, axis, [(i, (i + step) % peers) for i in range(peers)])]
    unnamed x2 -> x0, other arithmetic: 17.4 us -> none
    pallas_call x0 -> x5, Pallas kernels: none -> 13.7 us  [call(): pl.pallas_call(kernel, out_shape=outs, in_specs=specs, scratch_shapes=scr...]
    all_to_all x0 -> x1, blocking collectives: none -> 13.3 us  [shards(): sums = lax.all_to_all(partial, AXES, 0, 0, tiled=True)]
    add x4 -> x0, other arithmetic: 6.41 us -> none  [the longest x2 3.93 us: conjugate(): tracked = tracked + step_len * direction_pad]
    reduce_sum x5 -> x0, other arithmetic: 5.73 us -> none  [the longest x4 4.03 us: products(): jnp.sum(precond * image)]
  transfers between devices with their start and end apart: 30 -> 10, of which waited for: 20 -> 3; matrix products, arithmetic and copies ran while one was open for 2% -> 2% of each run, Pallas kernels for 0% -> 15%
where the time goes in v2:
time: 45 us; the launch traced here: 44.7 us
  Pallas kernels  13.7 us (30%)
  blocking collectives  13.3 us (30%)
  starting transfers between devices  9.86 us (22%)
  waiting for transfers between devices  4.33 us (10%)
  local copies, waits for them, and re-layouts  2.17 us (5%)
  between operations  0.71 us (2%)
  other arithmetic  0.7 us (2%)
    pallas_call x5, Pallas kernels, call(): pl.pallas_call(kernel, out_shape=outs, in_specs=specs, scratch_shapes=scr...  13.7 us
    all_to_all x1, blocking collectives, shards(): sums = lax.all_to_all(partial, AXES, 0, 0, tiled=True)  13.3 us
    ppermute x8, starting transfers between devices, ring(): lax.ppermute(value, axis, [(i, (i + step) % peers) for i in range(peers)])  5.66 us
    ppermute x2, starting transfers between devices, pairs(): return lax.ppermute(value, axis, swaps)  4.2 us
    ppermute x2, waiting for transfers between devices, pairs(): return lax.ppermute(value, axis, swaps)  3.44 us
    unnamed x4, local copies, waits for them, and re-layouts  2.17 us
  transfers between devices with their start and end apart: 10, of which 3 were waited for; matrix products, arithmetic and copies ran while one was open for 2% of the time, Pallas kernels for 15%

profile of v2, /device:TPU:0, one launch (start us, length us, event | category | flops | bytes accessed | tf_op | source)
XLA Modules:
  0.0 44.7 jit_solution(8074309556970243406)
XLA Ops:
  0.6 2.2 %shard_map.121 = (f32[10,8,16,128]{3,2,1,0:T(8,128)}, f32[8,40,128]{2,1,0:T(8,128)}, f32[8,40,128]{2,1,0:T(8,128)}) custom-call(f32[8,16,128]{2,1,0:T(8,128)} %refs_0_.1, f32[8,16,128]{2,1,0:T(8,128)} %refs_1_.1, f32[8,16,128]{2,1,0:T(8,128)} %refs_2_.1, f32[3,8,16,128]{3,2,1,0:T(8,128)} %refs_3_.1, f32[3,8,16,128]{3,2,1,0:T(8,128)} %refs_4_.1, ...), custom_call_target="tpu_custom_call" | custom-call | tf_op jit(solution)/shard_map/pallas_call | solution.py:830
  2.9 0.6 %collective-permute-start.5 = (f32[10,8,16,128]{3,2,1,0:T(8,128)}, f32[10,8,16,128]{3,2,1,0:T(8,128)S(1)}, u32[]{:S(2)}, u32[]{:S(2)}) collective-permute-start(f32[10,8,16,128]{3,2,1,0:T(8,128)} %get-tuple-element.24.refs_0_.refs_1_.refs_6_), channel_id=1, source_target_pairs={{0,16},{16,0},{1,17},{17,1},{2,18},{18,2},{3,19},{19,3},{4,20},{20... | collective-permute-start | bytes 1966088 | tf_op jit(solution)/shard_map/ppermute | solution.py:842
  3.4 2.6 %collective-permute-start = (f32[8,40,128]{2,1,0:T(8,128)}, f32[8,40,128]{2,1,0:T(8,128)S(1)}, u32[]{:S(2)}, u32[]{:S(2)}) collective-permute-start(f32[8,40,128]{2,1,0:T(8,128)} %get-tuple-element.25), channel_id=1, source_target_pairs={{0,4},{4,0},{8,12},{12,8},{1,5},{5,1},{9,13},{13,9},{2,6},{6,2},{1... | collective-permute-start | bytes 491528 | tf_op jit(solution)/shard_map/ppermute | solution.py:851
  6.1 1.6 %collective-permute-start.1 = (f32[8,40,128]{2,1,0:T(8,128)}, f32[8,40,128]{2,1,0:T(8,128)S(1)}, u32[]{:S(2)}, u32[]{:S(2)}) collective-permute-start(f32[8,40,128]{2,1,0:T(8,128)} %get-tuple-element.26), channel_id=1, source_target_pairs={{0,0},{4,8},{8,4},{12,12},{1,1},{5,9},{9,5},{13,13},{2,2},{6,10},{... | collective-permute-start | bytes 491528 | tf_op jit(solution)/shard_map/ppermute | solution.py:851
  7.6 3.4 %collective-permute-done.refs_1_.refs_4_ = f32[8,40,128]{2,1,0:T(8,128)S(1)} collective-permute-done((f32[8,40,128]{2,1,0:T(8,128)}, f32[8,40,128]{2,1,0:T(8,128)S(1)}, u32[]{:S(2)}, u32[]{:S(2)}) %collective-permute-start) | collective-permute-done | bytes 163872 | tf_op jit(solution)/shard_map/ppermute | solution.py:851
  11.1 0.0 collective-permute-done.1.refs_2_.refs_5_
  11.1 0.0 copy-start
  11.1 1.1 %copy-done = f32[10,8,16,128]{3,2,1,0:T(8,128)S(1)} copy-done((f32[10,8,16,128]{3,2,1,0:T(8,128)S(1)}, f32[10,8,16,128]{3,2,1,0:T(8,128)}, u32[]{:S(2)}) %copy-start) | copy-done | bytes 655384
  12.2 0.4 shard_map.122
  12.6 0.1 collective-permute-start.2
  12.7 0.5 %collective-permute-start.6 = (f32[8,40,128]{2,1,0:T(8,128)S(1)}, f32[8,40,128]{2,1,0:T(8,128)S(1)}, u32[]{:S(2)}, u32[]{:S(2)}) collective-permute-start(f32[8,40,128]{2,1,0:T(8,128)S(1)} %collective-permute-done.refs_1_.refs_4_), channel_id=1, source_target_pairs={{0,16},{16,0},{1,17},{17,1},{2,18},{18,2},{3,19},{19,3},{4,20},{20... | collective-permute-start | bytes 491528 | tf_op jit(solution)/shard_map/ppermute | solution.py:842
  13.2 0.1 collective-permute-start.7
  13.3 1.7 %collective-permute-start.3 = (f32[2,40,128]{2,1,0:T(8,128)S(1)}, f32[2,40,128]{2,1,0:T(8,128)S(1)}, u32[]{:S(2)}, u32[]{:S(2)}) collective-permute-start(f32[2,40,128]{2,1,0:T(8,128)S(1)} %get-tuple-element.28), channel_id=1, source_target_pairs={{0,1},{1,2},{2,3},{3,0},{4,5},{5,6},{6,7},{7,4},{8,9},{9,10},{10,1... | collective-permute-start | bytes 122888 | tf_op jit(solution)/shard_map/ppermute | solution.py:842
  14.9 0.0 collective-permute-done.6.refs_6_.refs_8_
  15.0 2.2 %collective-permute-start.4 = (f32[2,40,128]{2,1,0:T(8,128)S(1)}, f32[2,40,128]{2,1,0:T(8,128)S(1)}, u32[]{:S(2)}, u32[]{:S(2)}) collective-permute-start(f32[2,40,128]{2,1,0:T(8,128)S(1)} %get-tuple-element.29), channel_id=1, source_target_pairs={{0,3},{1,0},{2,1},{3,2},{4,7},{5,4},{6,5},{7,6},{8,11},{9,8},{10,9... | collective-permute-start | bytes 122888 | tf_op jit(solution)/shard_map/ppermute | solution.py:842
  17.2 0.7 %pad_maximum_fusion.refs_0_ = f32[3,8]{1,0:T(4,128)S(1)} fusion(f32[1,8]{1,0:T(1,128)} %bitcast.9, f32[1,8]{1,0:T(1,128)} %bitcast.10, f32[1,8]{1,0:T(1,128)} %bitcast.11), kind=kLoop, calls=%fused_computation | loop fusion | flops 48 | bytes 192 | tf_op jit(solution)/shard_map/stack | solution.py:876
  17.9 0.0 collective-permute-done.7.refs_7_.refs_9_
  17.9 0.0 collective-permute-done.5.refs_2_.refs_3_
  17.9 0.0 copy-start.1
  17.9 1.1 %copy-done.1 = f32[10,8,16,128]{3,2,1,0:T(8,128)S(1)} copy-done((f32[10,8,16,128]{3,2,1,0:T(8,128)S(1)}, f32[10,8,16,128]{3,2,1,0:T(8,128)}, u32[]{:S(2)}) %copy-start.1) | copy-done | bytes 655384
  19.0 6.3 %shard_map.123 = (f32[3,18,24,128]{3,2,1,0:T(8,128)S(1)}, f32[18,24,128]{2,1,0:T(8,128)S(1)}, f32[18,24,128]{2,1,0:T(8,128)S(1)}, f32[9,18,24,128]{3,2,1,0:T(8,1...) custom-call(f32[3,8]{1,0:T(4,128)S(1)} %pad_maximum_fusion.refs_0_, f32[10,8,16,128]{3,2,1,0:T(8,128)S(1)} %copy-done.1, ...), custom_call_target="tpu_custom_call" | custom-call | flops 73728000 | bytes 14745600 | tf_op jit(solution)/shard_map/pallas_call | solution.py:830
  25.3 0.0 collective-permute-done.3.refs_4_
  25.3 0.0 collective-permute-done.4.refs_5_
  25.3 0.1 collective-permute-start.8
  25.4 0.5 %collective-permute-start.9 = (f32[2,40,128]{2,1,0:T(8,128)S(1)}, f32[2,40,128]{2,1,0:T(8,128)S(1)}, u32[]{:S(2)}, u32[]{:S(2)}) collective-permute-start(f32[2,40,128]{2,1,0:T(8,128)S(1)} %collective-permute-done.4.refs_5_), channel_id=1, source_target_pairs={{0,16},{16,0},{1,17},{17,1},{2,18},{18,2},{3,19},{19,3},{4,20},{20... | collective-permute-start | bytes 122888 | tf_op jit(solution)/shard_map/ppermute | solution.py:842
  25.9 0.0 collective-permute-done.2.refs_2_.refs_3_
  25.9 0.7 %collective-permute-done.8.refs_6_.refs_8_ = f32[2,40,128]{2,1,0:T(8,128)S(1)} collective-permute-done((f32[2,40,128]{2,1,0:T(8,128)S(1)}, f32[2,40,128]{2,1,0:T(8,128)S(1)}, u32[]{:S(2)}, u32[]{:S(2)}) %collective-permute-start.8) | collective-permute-done | bytes 40992 | tf_op jit(solution)/shard_map/ppermute | solution.py:842
  26.6 0.2 collective-permute-done.9.refs_7_.refs_9_
  26.8 3.4 %shard_map.124 = (f32[10,5,32,128]{3,2,1,0:T(8,128)S(1)}, f32[5,32,128]{2,1,0:T(8,128)S(1)}, f32[5,32,128]{2,1,0:T(8,128)S(1)}, f32[9,5,32,128]{3,2,1,0:T(8,128)...) custom-call(f32[3,8]{1,0:T(4,128)S(1)} %pad_maximum_fusion.refs_0_, ...), custom_call_target="tpu_custom_call" | custom-call | tf_op jit(solution)/shard_map/pallas_call | solution.py:830
  30.2 13.3 %all_to_all.11 = f32[32,1,128]{2,1,0:T(1,128)S(1)} all-to-all(f32[32,1,128]{2,1,0:T(1,128)S(1)} %bitcast.8), channel_id=1, replica_groups=mesh['gx'=2,'gy'=4,'gz'=4] {'gx','gy','gz'}, dimensions={0} | all-to-all | bytes 32768 | tf_op jit(solution)/shard_map/all_to_all | solution.py:984
  43.5 1.3 %shard_map.125 = (f32[8,16,128]{2,1,0:T(8,128)}, f32[3,8,16,128]{3,2,1,0:T(8,128)}, f32[8,16,128]{2,1,0:T(8,128)}) custom-call(f32[32,128]{1,0:T(8,128)S(1)} %bitcast.7, f32[3,18,24,128]{3,2,1,0:T(8,128)S(1)} %get-tuple-element.35.refs_1_, f32[18,24,128]{2,1,0:T(8,128)S(1)} %get-tuple-element.36.refs_2_, f32[18,24,128]{2,1,0:T(8,128)S(1)} %get-tuple-element.37.refs_3_, ...), custom_call_target="tpu_custom_call" | custom-call | tf_op jit(solution)/shard_map/pallas_call | solution.py:830
Async XLA Ops:
  2.9 15.0 %collective-permute-start.5 = (f32[10,8,16,128]{3,2,1,0:T(8,128)}, f32[10,8,16,128]{3,2,1,0:T(8,128)S(1)}, u32[]{:S(2)}, u32[]{:S(2)}) collective-permute-start(f32[10,8,16,128]{3,2,1,0:T(8,128)} %get-tuple-element.24.refs_0_.refs_1_.refs_6_), channel_id=1, source_target_pairs={{0,16},{16,0},{1,17},{17,1},{2,18},{18,2},{3,19},{19,3},{4,20},{20... | collective-permute-start | bytes 1966088 | tf_op jit(solution)/shard_map/ppermute | solution.py:842
  3.4 7.6 %collective-permute-start = (f32[8,40,128]{2,1,0:T(8,128)}, f32[8,40,128]{2,1,0:T(8,128)S(1)}, u32[]{:S(2)}, u32[]{:S(2)}) collective-permute-start(f32[8,40,128]{2,1,0:T(8,128)} %get-tuple-element.25), channel_id=1, source_target_pairs={{0,4},{4,0},{8,12},{12,8},{1,5},{5,1},{9,13},{13,9},{2,6},{6,2},{1... | collective-permute-start | bytes 491528 | tf_op jit(solution)/shard_map/ppermute | solution.py:851
  6.1 5.0 %collective-permute-start.1 = (f32[8,40,128]{2,1,0:T(8,128)}, f32[8,40,128]{2,1,0:T(8,128)S(1)}, u32[]{:S(2)}, u32[]{:S(2)}) collective-permute-start(f32[8,40,128]{2,1,0:T(8,128)} %get-tuple-element.26), channel_id=1, source_target_pairs={{0,0},{4,8},{8,4},{12,12},{1,1},{5,9},{9,5},{13,13},{2,2},{6,10},{... | collective-permute-start | bytes 491528 | tf_op jit(solution)/shard_map/ppermute | solution.py:851
  11.1 1.1 %copy-start = (f32[10,8,16,128]{3,2,1,0:T(8,128)S(1)}, f32[10,8,16,128]{3,2,1,0:T(8,128)}, u32[]{:S(2)}) copy-start(f32[10,8,16,128]{3,2,1,0:T(8,128)} %get-tuple-element.24.refs_0_.refs_1_.refs_6_) | copy-start | bytes 1966084
  12.6 13.3 %collective-permute-start.2 = (f32[10,2,32,128]{3,2,1,0:T(8,128)S(1)}, f32[10,2,32,128]{3,2,1,0:T(8,128)S(1)}, u32[]{:S(2)}, u32[]{:S(2)}) collective-permute-start(f32[10,2,32,128]{3,2,1,0:T(8,128)S(1)} %get-tuple-element.27.refs_1_), channel_id=1, source_target_pairs={{0,16},{16,0},{1,17},{17,1},{2,18},{18,2},{3,19},{19,3},{4,20},{20... | collective-permute-start | bytes 983048 | tf_op jit(solution)/shard_map/ppermute | solution.py:842
  12.7 2.2 %collective-permute-start.6 = (f32[8,40,128]{2,1,0:T(8,128)S(1)}, f32[8,40,128]{2,1,0:T(8,128)S(1)}, u32[]{:S(2)}, u32[]{:S(2)}) collective-permute-start(f32[8,40,128]{2,1,0:T(8,128)S(1)} %collective-permute-done.refs_1_.refs_4_), channel_id=1, source_target_pairs={{0,16},{16,0},{1,17},{17,1},{2,18},{18,2},{3,19},{19,3},{4,20},{20... | collective-permute-start | bytes 491528 | tf_op jit(solution)/shard_map/ppermute | solution.py:842
  13.2 4.7 %collective-permute-start.7 = (f32[8,40,128]{2,1,0:T(8,128)S(1)}, f32[8,40,128]{2,1,0:T(8,128)S(1)}, u32[]{:S(2)}, u32[]{:S(2)}) collective-permute-start(f32[8,40,128]{2,1,0:T(8,128)S(1)} %collective-permute-done.1.refs_2_.refs_5_), channel_id=1, source_target_pairs={{0,16},{16,0},{1,17},{17,1},{2,18},{18,2},{3,19},{19,3},{4,20},{20... | collective-permute-start | bytes 491528 | tf_op jit(solution)/shard_map/ppermute | solution.py:842
  13.3 12.0 %collective-permute-start.3 = (f32[2,40,128]{2,1,0:T(8,128)S(1)}, f32[2,40,128]{2,1,0:T(8,128)S(1)}, u32[]{:S(2)}, u32[]{:S(2)}) collective-permute-start(f32[2,40,128]{2,1,0:T(8,128)S(1)} %get-tuple-element.28), channel_id=1, source_target_pairs={{0,1},{1,2},{2,3},{3,0},{4,5},{5,6},{6,7},{7,4},{8,9},{9,10},{10,1... | collective-permute-start | bytes 122888 | tf_op jit(solution)/shard_map/ppermute | solution.py:842
  15.0 10.4 %collective-permute-start.4 = (f32[2,40,128]{2,1,0:T(8,128)S(1)}, f32[2,40,128]{2,1,0:T(8,128)S(1)}, u32[]{:S(2)}, u32[]{:S(2)}) collective-permute-start(f32[2,40,128]{2,1,0:T(8,128)S(1)} %get-tuple-element.29), channel_id=1, source_target_pairs={{0,3},{1,0},{2,1},{3,2},{4,7},{5,4},{6,5},{7,6},{8,11},{9,8},{10,9... | collective-permute-start | bytes 122888 | tf_op jit(solution)/shard_map/ppermute | solution.py:842
  17.9 1.1 %copy-start.1 = (f32[10,8,16,128]{3,2,1,0:T(8,128)S(1)}, f32[10,8,16,128]{3,2,1,0:T(8,128)}, u32[]{:S(2)}) copy-start(f32[10,8,16,128]{3,2,1,0:T(8,128)} %get-tuple-element.24.refs_0_.refs_1_.refs_6_) | copy-start | bytes 1966084
  25.3 1.3 %collective-permute-start.8 = (f32[2,40,128]{2,1,0:T(8,128)S(1)}, f32[2,40,128]{2,1,0:T(8,128)S(1)}, u32[]{:S(2)}, u32[]{:S(2)}) collective-permute-start(f32[2,40,128]{2,1,0:T(8,128)S(1)} %collective-permute-done.3.refs_4_), channel_id=1, source_target_pairs={{0,16},{16,0},{1,17},{17,1},{2,18},{18,2},{3,19},{19,3},{4,20},{20... | collective-permute-start | bytes 122888 | tf_op jit(solution)/shard_map/ppermute | solution.py:842
  25.4 1.4 %collective-permute-start.9 = (f32[2,40,128]{2,1,0:T(8,128)S(1)}, f32[2,40,128]{2,1,0:T(8,128)S(1)}, u32[]{:S(2)}, u32[]{:S(2)}) collective-permute-start(f32[2,40,128]{2,1,0:T(8,128)S(1)} %collective-permute-done.4.refs_5_), channel_id=1, source_target_pairs={{0,16},{16,0},{1,17},{17,1},{2,18},{18,2},{3,19},{19,3},{4,20},{20... | collective-permute-start | bytes 122888 | tf_op jit(solution)/shard_map/ppermute | solution.py:842

commit v3 on v2

--- a/solution.py
+++ b/solution.py
@@ -4,6 +4,7 @@
 from jax.experimental import pallas as pl
 from jax.experimental.pallas import tpu as pltpu
 from jax.sharding import PartitionSpec as P
+
 
 ZONES = 8
 
@@ -25,11 +26,9 @@
 OFFSETS = tuple(sum(WIDTHS[:f]) for f in range(NF))
 PAIRS = tuple((j, k) for j in range(3) for k in range(j, 3))
 SUMS = 4 + 4 * len(PAIRS)
-BASIS = 27
 SEG = 16
 ENDS = 2 * SEG
 UNROLL = 4
-PACK_LIMIT = 62
 
 
 def up_to(value, multiple):
@@ -43,9 +42,20 @@
     return lax.broadcasted_iota(jnp.int32, shape, dim)
 
 
-def pack_rows(*refs):
-    sources, (fields, first, second), rest = refs[:7], refs[7:10], refs[10:]
-    held, arrived = rest[:7], rest[7]
+def field_of(raw, f, at):
+    source, pressure, strain, motion, body, zones, drained = raw
+    if f == ZONE:
+        return zones[at].astype(jnp.float32) + 1.0
+    if f == PRESS:
+        return pressure[at]
+    if f == SOURCE:
+        return source[at] + biot_coef * strain[at]
+    if f == DRAIN:
+        return drained[at].astype(jnp.float32)
+    return motion[f - MOTION, *at] if f < SOURCE else body[f - BODY, *at]
+
+
+def fetch(sources, held, arrived):
     copies = [
         pltpu.make_async_copy(source, copy, arrived.at[i])
         for i, (source, copy) in enumerate(zip(sources, held))
@@ -54,39 +64,58 @@
         copy.start()
     for copy in copies:
         copy.wait()
-    source, pressure, strain, motion, body, zones, drained = held
-    nx, ny, nz = source.shape
+
+
+def pack_rows(*refs):
+    sources, (first, second, table), held, arrived = refs[:10], refs[10:13], refs[13:23], refs[23]
+    fetch(sources, held, arrived)
+    raw, tables = held[:7], held[7:]
+    nx, ny, nz = raw[0].shape
     spare = MSG_ROWS - sum(WIDTHS)
-    for x in range(nx):
-        values = [
-            zones[x].astype(jnp.float32) + 1.0,
-            pressure[x],
-            motion[0, x],
-            motion[1, x],
-            motion[2, x],
-            source[x] + biot_coef * strain[x],
-            drained[x].astype(jnp.float32),
-            body[0, x],
-            body[1, x],
-            body[2, x],
-        ]
-        for f, value in enumerate(values):
-            fields[f, x] = value
-        if spare:
-            empty = jnp.zeros((spare, nz), jnp.float32)
-            first[x, MSG_ROWS - spare :, :] = empty
-            second[x, MSG_ROWS - spare :, :] = empty
 
     def messages(upward, downward):
         for x in range(nx):
             for f in range(NF):
                 width, offset = WIDTHS[f], OFFSETS[f]
-                upward[x, offset : offset + width, :] = fields[f, x, ny - width :, :]
-                downward[x, offset : offset + width, :] = fields[f, x, :width, :]
+                value = field_of(raw, f, (x, slice(None)))
+                upward[x, offset : offset + width, :] = value[ny - width :]
+                downward[x, offset : offset + width, :] = value[:width]
+            if spare:
+                empty = jnp.zeros((spare, nz), jnp.float32)
+                upward[x, MSG_ROWS - spare :, :] = empty
+                downward[x, MSG_ROWS - spare :, :] = empty
 
     even = lax.axis_index("gy") % 2 == 0
     pl.when(even)(lambda: messages(first, second))
     pl.when(jnp.logical_not(even))(lambda: messages(second, first))
+    shape = (TILE, LANES)
+    tile = jnp.zeros(shape, jnp.float32)
+    for t in range(len(tables)):
+        for zone in range(ZONES):
+            here = (iota(shape, 0) == t) & (iota(shape, 1) == zone + 1)
+            tile = jnp.where(here, tables[t][zone], tile)
+    table[...] = tile
+
+
+def pack_fields(*refs):
+    sources, fields, held, arrived = refs[:7], refs[8], refs[9:16], refs[16]
+    fetch(sources, held, arrived)
+    for x in range(fields.shape[1]):
+        for f in range(NF):
+            fields[f, x] = field_of(held, f, (x, slice(None)))
+
+
+def keeps(axis, peers):
+    at = lax.axis_index(axis)
+    return jnp.where(at > 0, 1.0, 0.0), jnp.where(at < peers - 1, 1.0, 0.0)
+
+
+def blocks_of(peers):
+    at = lax.axis_index("gx")
+    if peers[0] == 2:
+        return [(at, 1.0), (1 - at, 1.0)]
+    keep_below, keep_above = keeps("gx", peers[0])
+    return [(1, 1.0), (0, keep_below), (2, keep_above)]
 
 
 class Rows:
@@ -107,54 +136,64 @@
     return jnp.where(at > 0, 1.0, 0.0), jnp.where(at < peers - 1, 1.0, 0.0)
 
 
-def pack_ends(peers, fields, first, second, ends, rightward, leftward, stage):
-    _, nx, ny, nz = fields.shape
+def pack_ends(peers, *refs):
+    ends, rightward, leftward, stage = refs[-4:]
+    blocks = blocks_of(peers)
+    _, nx, ny, nz = refs[0].shape
     tall = ny + 2 * TILE
     pack = LANES // tall
-    rows = Rows(first, second, peers)
+    count = nx // pack
     gap = jnp.zeros((TILE, nz), jnp.float32)
+    zeros = jnp.zeros((TILE, LANES), jnp.float32)
     inner = SEG - W
     spare = MSG_ROWS - sum(WIDTHS)
-    for g in range(nx // pack):
-        if spare:
-            empty = jnp.zeros((spare, LANES), jnp.float32)
-            rightward[g, MSG_ROWS - spare :, :] = empty
-            leftward[g, MSG_ROWS - spare :, :] = empty
-        for f in range(NF):
-            width, offset = WIDTHS[f], OFFSETS[f]
-            slot = g * NF + f
-            for i in range(pack):
-                x = g * pack + i
-                top = i * tall
-                stage[slot, top : top + TILE, :] = gap
-                stage[slot, top + TILE + ny : top + tall, :] = gap
-                stage[slot, top + TILE : top + TILE + ny, :] = fields[f, x]
-                low, high = rows.read(f, x)
-                stage[slot, top + TILE - width : top + TILE, :] = low
-                stage[slot, top + TILE + ny : top + TILE + ny + width, :] = high
-            begin = stage[slot, :, :LANES].T
-            finish = begin if nz == LANES else stage[slot, :, nz - LANES :].T
-            rightward[g, offset : offset + width, :] = finish[LANES - width :]
-            leftward[g, offset : offset + width, :] = begin[:width]
-            ends[f, g, :TILE, :] = jnp.zeros((TILE, LANES), jnp.float32)
-            ends[f, g, ENDS - TILE :, :] = jnp.zeros((TILE, LANES), jnp.float32)
-            ends[f, g, W:SEG, :] = begin[:inner]
-            ends[f, g, SEG : ENDS - W, :] = finish[LANES - inner :]
+    for b, (start, keep) in enumerate(blocks):
+        fields = refs[b]
+        first, second = refs[len(blocks) + 2 * b : len(blocks) + 2 * b + 2]
+        rows = Rows(first, second, peers)
+        for i in range(count):
+            g = start * count + i
+            if spare:
+                rightward[g, MSG_ROWS - spare :, :] = zeros[:spare]
+                leftward[g, MSG_ROWS - spare :, :] = zeros[:spare]
+            for f in range(NF):
+                width, offset = WIDTHS[f], OFFSETS[f]
+                slot = (b * count + i) * NF + f
+                for p in range(pack):
+                    x = i * pack + p
+                    top = p * tall
+                    stage[slot, top : top + TILE, :] = gap
+                    stage[slot, top + TILE + ny : top + tall, :] = gap
+                    stage[slot, top + TILE : top + TILE + ny, :] = fields[f, x]
+                    low, high = rows.read(f, x)
+                    stage[slot, top + TILE - width : top + TILE, :] = low
+                    stage[slot, top + TILE + ny : top + TILE + ny + width, :] = high
+                begin = stage[slot, :, :LANES].T
+                finish = begin if nz == LANES else stage[slot, :, nz - LANES :].T
+                if len(blocks) > 2:
+                    begin, finish = begin * keep, finish * keep
+                rightward[g, offset : offset + width, :] = finish[LANES - width :]
+                leftward[g, offset : offset + width, :] = begin[:width]
+                ends[f, g, :TILE, :] = zeros
+                ends[f, g, ENDS - TILE :, :] = zeros
+                ends[f, g, W:SEG, :] = begin[:inner]
+                ends[f, g, SEG : ENDS - W, :] = finish[LANES - inner :]
 
 
 def harmonic(a, b):
     return 2.0 * a * b / jnp.maximum(a + b, 1e-30)
 
 
-def lookup(zone, tables):
-    picked = [jnp.zeros(zone.shape, jnp.float32) for _ in tables]
-    for index in range(ZONES):
-        here = zone == float(index + 1)
-        picked = [
-            jnp.where(here, table[row, index], value)
-            for (table, row), value in zip(tables, picked)
-        ]
-    return picked
+def lookup(zone, table, row):
+    entries = jnp.broadcast_to(table[row : row + 1, :], zone.shape[:-1] + (LANES,))
+    index = zone.astype(jnp.int32)
+    picked = [
+        jnp.take_along_axis(
+            entries, index[:, start : start + LANES], axis=1, mode="promise_in_bounds"
+        )
+        for start in range(0, zone.shape[1], LANES)
+    ]
+    return picked[0] if len(picked) == 1 else jnp.concatenate(picked, axis=1)
 
 
 def fixed_term(zone, lame, shear):
@@ -491,7 +530,7 @@
             ),
         )
 
-    def assemble(self, l, x, fields, beside, tables):
+    def assemble(self, l, x, fields, beside, table):
         ny = self.ny
         rows = ny + 2 * TILE
         gap = jnp.zeros((2 * TILE, fields.shape[3]), jnp.float32)
@@ -512,12 +551,12 @@
                 ref[l, ny : ny + width, :] = above
                 ref[l, narrow_rows - width :, :] = below
         tall_zone = self.tall[ZONE, l]
-        (perm,) = lookup(tall_zone, tables[:1])
+        perm = lookup(tall_zone, table, 0)
         self.perm_tall[l] = perm
         self.perm[l] = self.narrow(perm)
         zone = self.narrow(tall_zone)
         self.zone[l] = zone
-        lame, shear = lookup(zone, tables[1:])
+        lame, shear = lookup(zone, table, 1), lookup(zone, table, 2)
         self.heft[l] = lame + shear
         self.shear[l] = shear
         self.fixed[l] = fixed_term(zone, lame, shear)
@@ -535,7 +574,6 @@
     domain = Brick(dict(zip(names, scratch[:inner])))
     domain.__dict__.update(zip(KEPT, outs))
     domain.tall, domain.perm_tall, domain.ty_tall = scratch[inner:]
-    tables = [(table, i) for i in range(3)]
     _, nx, ny, nz = fields.shape
     domain.nx, domain.ny = nx, ny
     at = lax.axis_index("gx")
@@ -556,7 +594,7 @@
 
     def block(start, count, shift, *source):
         domain.loop(
-            start, count, lambda l: domain.assemble(l, l + shift, *source, tables)
+            start, count, lambda l: domain.assemble(l, l + shift, *source, table)
         )
 
     block(W, nx, -W, fields, rows[0])
@@ -630,36 +668,32 @@
     def lead(self, halo, body):
         pass
 
-    def assemble(self, l, g, keep, ends, left, right, keep_left, keep_right):
-        for f in range(NF):
-            width, offset = WIDTHS[f], OFFSETS[f]
-            self.raw[f, l] = ends[f, g] * keep
-            self.raw[f, l, W - width : W, :] = left[g, offset : offset + width, :] * (
-                keep_left * keep
-            )
-            self.raw[f, l, ENDS - W : ENDS - W + width, :] = right[
-                g, offset : offset + width, :
-            ] * (keep_right * keep)
-
-    def materials(self, tables):
+    def assemble(self, ends, left, right, keep_left, keep_right, table):
         for g in range(self.groups):
+            for f in range(NF):
+                width, offset = WIDTHS[f], OFFSETS[f]
+                rows = slice(offset, offset + width)
+                self.raw[f, g] = ends[f, g]
+                self.raw[f, g, W - width : W, :] = left[g, rows, :] * keep_left
+                self.raw[f, g, ENDS - W : ENDS - W + width, :] = (
+                    right[g, rows, :] * keep_right
+                )
             zone = self.raw[ZONE, g]
-            perm, lame, shear = lookup(zone, tables)
-            self.perm[g] = perm
+            lame, shear = lookup(zone, table, 1), lookup(zone, table, 2)
+            self.perm[g] = lookup(zone, table, 0)
             self.heft[g] = lame + shear
             self.shear[g] = shear
             self.fixed[g] = fixed_term(zone, lame, shear)
 
 
 def own_groups(count, peers):
-    return count * lax.axis_index("gx") if peers[0] == 2 else count
+    return count * blocks_of(peers)[0][0]
 
 
 def ends_kernel(peers, tall, *refs):
-    table, ends, below, above, left, right = refs[:6]
-    left_below, right_below, left_above, right_above, added = refs[6:11]
-    raw, z0, p0, zs, ps, partial = refs[11:17]
-    acc, scratch = refs[17], refs[18:]
+    table, ends, left, right, added = refs[:5]
+    raw, z0, p0, zs, ps, partial = refs[5:11]
+    acc, scratch = refs[11], refs[12:]
     names = [name for name, _ in ARRAYS[6:] if name not in KEPT]
     domain = Ends(dict(zip(names, scratch)))
     domain.raw, domain.z0, domain.p0, domain.zs, domain.ps = raw, z0, p0, zs, ps
@@ -668,9 +702,8 @@
     domain.load, domain.drain = raw.at[SOURCE], raw.at[DRAIN]
     domain.body = raw.at[BODY : BODY + 3]
     domain.row = tall
-    count = ends.shape[1]
     domain.groups = groups = raw.shape[1] - 1
-    at = lax.axis_index("gx")
+    count = groups // len(blocks_of(peers))
     keep = keeps("gz", peers[2])
     empty = jnp.zeros((ENDS, LANES), jnp.float32)
     for ref in (raw, zs, ps):
@@ -679,22 +712,7 @@
     for ref in (domain.perm, domain.shear, z0, p0):
         ref[groups] = empty
     mine = own_groups(count, peers)
-    if peers[0] == 2:
-        blocks = [
-            (mine, 1.0, ends, left, right),
-            (count * (1 - at), 1.0, below, left_below, right_below),
-        ]
-    else:
-        keep_below, keep_above = keeps("gx", peers[0])
-        blocks = [
-            (0, keep_below, below, left_below, right_below),
-            (mine, 1.0, ends, left, right),
-            (mine + count, keep_above, above, left_above, right_above),
-        ]
-    for start, keep_block, *source in blocks:
-        for g in range(count):
-            domain.assemble(start + g, g, keep_block, *source, *keep)
-    domain.materials([(table, i) for i in range(3)])
+    domain.assemble(ends, left, right, *keep, table)
     domain.stages()
     acc[...] = added[...]
     shape = (ENDS, LANES)
@@ -758,7 +776,7 @@
     pack = LANES // tall
     ends = Ends(dict(row=tall))
     groups = raw.shape[1] - 1
-    count = groups // (2 if peers[0] == 2 else 3)
+    count = groups // len(blocks_of(peers))
     mine = own_groups(count, peers)
     every = pl.ds(0, groups)
     for c in range(3):
@@ -822,9 +840,9 @@
     return pltpu.VMEM(shape, jnp.float32)
 
 
-def call(kernel, outs, *args, smem=0, space=pltpu.VMEM, scratch=(), limit=8, cost=None):
+def call(kernel, outs, *args, unread=0, space=pltpu.VMEM, scratch=(), limit=8, cost=None):
     specs = [
-        pl.BlockSpec(memory_space=pltpu.SMEM if i < smem else space)
+        pl.BlockSpec(memory_space=space if i < len(args) - unread else pl.ANY)
         for i in range(len(args))
     ]
     return pl.pallas_call(
@@ -873,7 +891,6 @@
     nx, ny, nz = source.shape
     peers = [lax.axis_size(a) for a in AXES]
     total = peers[0] * peers[1] * peers[2]
-    table = jnp.stack([perm_table, lame_table, shear_table])
     tall = ny + 2 * TILE
     groups = nx * tall // LANES
 
@@ -889,35 +906,57 @@
         zone_ids,
         drained,
     )
-    fields, first, second = call(
+    raw = [pltpu.with_memory_space_constraint(a, pltpu.HBM) for a in raw]
+    held = [pltpu.VMEM(a.shape, a.dtype) for a in raw]
+    tables = [
+        pltpu.with_memory_space_constraint(a, pltpu.HBM)
+        for a in (perm_table, lame_table, shear_table)
+    ]
+    message = f32(nx, MSG_ROWS, nz)
+    first, second, table = call(
         pack_rows,
-        [f32(NF, nx, ny, nz), f32(nx, MSG_ROWS, nz), f32(nx, MSG_ROWS, nz)],
+        [message, message, f32(TILE, LANES)],
         *raw,
+        *tables,
         space=pltpu.HBM,
-        scratch=[pltpu.VMEM(a.shape, a.dtype) for a in raw]
-        + [pltpu.SemaphoreType.DMA((len(raw),))],
-        limit=PACK_LIMIT,
+        scratch=held
+        + [pltpu.SMEM(a.shape, a.dtype) for a in tables]
+        + [pltpu.SemaphoreType.DMA((len(raw) + len(tables),))],
+    )
+    (fields,) = call(
+        pack_fields,
+        [f32(NF, nx, ny, nz)],
+        *raw,
+        table,
+        space=pltpu.HBM,
+        unread=1,
+        scratch=held + [pltpu.SemaphoreType.DMA((len(raw),))],
     )
     fields_below, fields_above = x_neighbours(fields)
     first = pairs(first, "gy", 0)
     second = pairs(second, "gy", 1)
     first_below, first_above = x_neighbours(first)
     second_below, second_above = x_neighbours(second)
+    blocks = [
+        (fields, first, second),
+        (fields_below, first_below, second_below),
+        (fields_above, first_above, second_above),
+    ][: 2 if peers[0] == 2 else 3]
+    span = len(blocks) * groups
     ends, rightward, leftward = call(
         with_peers(pack_ends),
         [
-            f32(NF, groups, ENDS, LANES),
-            f32(groups, MSG_ROWS, LANES),
-            f32(groups, MSG_ROWS, LANES),
+            f32(NF, span, ENDS, LANES),
+            f32(span, MSG_ROWS, LANES),
+            f32(span, MSG_ROWS, LANES),
         ],
-        fields,
-        first,
-        second,
-        scratch=[vmem(NF * groups, LANES, nz)],
+        *[block[0] for block in blocks],
+        *[rows for block in blocks for rows in block[1:]],
+        scratch=[vmem(NF * span, LANES, nz)],
+        limit=12,
     )
     left = ring(rightward, "gz", 1)
     right = ring(leftward, "gz", -1)
-    ends_below, ends_above = x_neighbours(ends)
     depth = nx + 2 * W
     cells = depth * ny * nz
 
@@ -940,7 +979,6 @@
         second_below,
         first_above,
         second_above,
-        smem=1,
         scratch=[
             vmem(*shaped(lead, depth, ny + TILE, nz))
             for name, lead in ARRAYS
@@ -953,9 +991,7 @@
         ),
     )
     left, right, added = lax.optimization_barrier((left, right, added))
-    left_below, left_above = x_neighbours(left)
-    right_below, right_above = x_neighbours(right)
-    span = (2 if peers[0] == 2 else 3) * groups + 1
+    span = span + 1
     *ends_kept, partial = call(
         with_peers(ends_kernel, tall),
         [f32(NF, span, ENDS, LANES)]
@@ -963,16 +999,9 @@
         + [f32(total, LANES)],
         table,
         ends,
-        ends_below,
-        ends_above,
         left,
         right,
-        left_below,
-        right_below,
-        left_above,
-        right_above,
         added,
-        smem=1,
         scratch=[vmem(*sums_shape)]
         + [
             vmem(*shaped(lead, span, ENDS, LANES))

time: 45 us -> 41.1 us (0.913)
  starting transfers between devices: 9.86 us -> 7.34 us
  local copies, waits for them, and re-layouts: 2.17 us -> 0 us
  waiting for transfers between devices: 4.33 us -> 5.25 us
  other arithmetic: 0.7 us -> 0 us
  blocking collectives: 13.3 us -> 14 us
    unnamed x4 -> x0, local copies, waits for them, and re-layouts: 2.17 us -> none
    ppermute x8 -> x5, starting transfers between devices: 5.66 us -> 4.05 us  [ring(): lax.ppermute(value, axis, [(i, (i + step) % peers) for i in range(peers)])]
    ppermute x2, starting transfers between devices: 4.2 us -> 3.3 us  [pairs(): return lax.ppermute(value, axis, swaps)]
    all_to_all x1, blocking collectives: 13.3 us -> 14 us  [shards(): sums = lax.all_to_all(partial, AXES, 0, 0, tiled=True)]
    another operation x1 -> x0, other arithmetic: 0.7 us -> none  [shards(): table = jnp.stack([perm_table, lame_table, shear_table])]
    ppermute x2, waiting for transfers between devices: 3.44 us -> 4.13 us  [pairs(): return lax.ppermute(value, axis, swaps)]
    ppermute x8 -> x5, waiting for transfers between devices: 0.88 us -> 1.12 us  [ring(): lax.ppermute(value, axis, [(i, (i + step) % peers) for i in range(peers)])]
    pallas_call x5 -> x6, Pallas kernels: 13.7 us -> 13.6 us  [call(): pl.pallas_call(kernel, out_shape=outs, in_specs=specs, scratch_shapes=scr...]
  transfers between devices with their start and end apart: 10 -> 7, of which waited for: 3 -> 3; matrix products, arithmetic and copies ran while one was open for 2% -> 0% of each run, Pallas kernels for 15% -> 15%
where the time goes in v3:
time: 41.1 us; the launch traced here: 40.9 us
  blocking collectives  14 us (34%)
  Pallas kernels  13.6 us (33%)
  starting transfers between devices  7.34 us (18%)
  waiting for transfers between devices  5.25 us (13%)
  between operations  0.69 us (2%)
    all_to_all x1, blocking collectives, shards(): sums = lax.all_to_all(partial, AXES, 0, 0, tiled=True)  14 us
    pallas_call x6, Pallas kernels, call(): pl.pallas_call(kernel, out_shape=outs, in_specs=specs, scratch_shapes=scr...  13.6 us
    ppermute x2, waiting for transfers between devices, pairs(): return lax.ppermute(value, axis, swaps)  4.13 us
    ppermute x5, starting transfers between devices, ring(): lax.ppermute(value, axis, [(i, (i + step) % peers) for i in range(peers)])  4.05 us
    ppermute x2, starting transfers between devices, pairs(): return lax.ppermute(value, axis, swaps)  3.3 us
    ppermute x5, waiting for transfers between devices, ring(): lax.ppermute(value, axis, [(i, (i + step) % peers) for i in range(peers)])  1.12 us
  transfers between devices with their start and end apart: 7, of which 3 were waited for; matrix products, arithmetic and copies ran while one was open for 0% of the time, Pallas kernels for 15%

profile of v3, /device:TPU:0, one launch (start us, length us, event | category | flops | bytes accessed | tf_op | source)
XLA Modules:
  0.0 40.9 jit_solution(9735895814693410070)
XLA Ops:
  0.6 1.4 %shard_map.121 = (f32[8,40,128]{2,1,0:T(8,128)S(1)}, f32[8,40,128]{2,1,0:T(8,128)S(1)}, f32[8,128]{1,0:T(8,128)S(1)}) custom-call(f32[8,16,128]{2,1,0:T(8,128)} %refs_0_.3, f32[8,16,128]{2,1,0:T(8,128)} %refs_1_.3, f32[8,16,128]{2,1,0:T(8,128)} %refs_2_.3, f32[3,8,16,128]{3,2,1,0:T(8,128)} %refs_3_.3, f32[3,8,16,128]{3,2,1,0:T(8,128)} %refs_4_.3, ...), custom_call_target="tpu_custom_call" | custom-call | tf_op jit(solution)/shard_map/pallas_call | solution.py:848
  2.0 1.3 %shard_map.122.refs_0_.refs_1_.refs_6_ = f32[10,8,16,128]{3,2,1,0:T(8,128)S(1)} custom-call(f32[8,16,128]{2,1,0:T(8,128)} %refs_0_.3, f32[8,16,128]{2,1,0:T(8,128)} %refs_1_.3, f32[8,16,128]{2,1,0:T(8,128)} %refs_2_.3, f32[3,8,16,128]{3,2,1,0:T(8,128)} %refs_3_.3, f32[3,8,16,128]{3,2,1,0:T(8,128)} %refs_4_.3, s32[8,16,128]{2,1,0:T(8,128)} %refs_5_.3, ...), custom_call_target="tpu_custom_call" | custom-call | tf_op jit(solution)/shard_map/pallas_call | solution.py:848
  3.3 0.6 %collective-permute-start = (f32[10,8,16,128]{3,2,1,0:T(8,128)S(1)}, f32[10,8,16,128]{3,2,1,0:T(8,128)S(1)}, u32[]{:S(2)}, u32[]{:S(2)}) collective-permute-start(f32[10,8,16,128]{3,2,1,0:T(8,128)S(1)} %shard_map.122.refs_0_.refs_1_.refs_6_), channel_id=1, source_target_pairs={{0,16},{16,0},{1,17},{17,1},{2,18},{18,2},{3,19},{19,3},{4,20},{20... | collective-permute-start | bytes 1966088 | tf_op jit(solution)/shard_map/ppermute | solution.py:860
  3.8 2.6 %collective-permute-start.1 = (f32[8,40,128]{2,1,0:T(8,128)S(1)}, f32[8,40,128]{2,1,0:T(8,128)S(1)}, u32[]{:S(2)}, u32[]{:S(2)}) collective-permute-start(f32[8,40,128]{2,1,0:T(8,128)S(1)} %get-tuple-element.25), channel_id=1, source_target_pairs={{0,4},{4,0},{8,12},{12,8},{1,5},{5,1},{9,13},{13,9},{2,6},{6,2},{1... | collective-permute-start | bytes 491528 | tf_op jit(solution)/shard_map/ppermute | solution.py:869
  6.5 0.7 %collective-permute-start.2 = (f32[8,40,128]{2,1,0:T(8,128)S(1)}, f32[8,40,128]{2,1,0:T(8,128)S(1)}, u32[]{:S(2)}, u32[]{:S(2)}) collective-permute-start(f32[8,40,128]{2,1,0:T(8,128)S(1)} %get-tuple-element.26), channel_id=1, source_target_pairs={{0,0},{4,8},{8,4},{12,12},{1,1},{5,9},{9,5},{13,13},{2,2},{6,10},{... | collective-permute-start | bytes 491528 | tf_op jit(solution)/shard_map/ppermute | solution.py:869
  7.1 4.1 %collective-permute-done.1.refs_2_.refs_4_ = f32[8,40,128]{2,1,0:T(8,128)S(1)} collective-permute-done((f32[8,40,128]{2,1,0:T(8,128)S(1)}, f32[8,40,128]{2,1,0:T(8,128)S(1)}, u32[]{:S(2)}, u32[]{:S(2)}) %collective-permute-start.1) | collective-permute-done | bytes 163872 | tf_op jit(solution)/shard_map/ppermute | solution.py:869
  11.3 0.0 collective-permute-start.3
  11.3 0.0 collective-permute-done.2.refs_3_.refs_5_
  11.3 0.5 %collective-permute-start.4 = (f32[8,40,128]{2,1,0:T(8,128)S(1)}, f32[8,40,128]{2,1,0:T(8,128)S(1)}, u32[]{:S(2)}, u32[]{:S(2)}) collective-permute-start(f32[8,40,128]{2,1,0:T(8,128)S(1)} %collective-permute-done.2.refs_3_.refs_5_), channel_id=1, source_target_pairs={{0,16},{16,0},{1,17},{17,1},{2,18},{18,2},{3,19},{19,3},{4,20},{20... | collective-permute-start | bytes 491528 | tf_op jit(solution)/shard_map/ppermute | solution.py:860
  11.8 0.9 %collective-permute-done.3.refs_4_.refs_6_.refs_8_ = f32[8,40,128]{2,1,0:T(8,128)S(1)} collective-permute-done((f32[8,40,128]{2,1,0:T(8,128)S(1)}, f32[8,40,128]{2,1,0:T(8,128)S(1)}, u32[]{:S(2)}, u32[]{:S(2)}) %collective-permute-start.3) | collective-permute-done | bytes 163872 | tf_op jit(solution)/shard_map/ppermute | solution.py:860
  12.7 0.2 collective-permute-done.4.refs_5_.refs_7_.refs_9_
  12.9 0.0 collective-permute-done.refs_1_.refs_2_.refs_3_
  12.9 0.8 %shard_map.123 = (f32[10,4,32,128]{3,2,1,0:T(8,128)S(1)}, f32[4,40,128]{2,1,0:T(8,128)S(1)}, f32[4,40,128]{2,1,0:T(8,128)S(1)}) custom-call(f32[10,8,16,128]{3,2,1,0:T(8,128)S(1)} %shard_map.122.refs_0_.refs_1_.refs_6_, f32[10,8,16,128]{3,2,1,0:T(8,128)S(1)} %collective-permute-done.refs_1_.refs_2_.refs_3_, ...), custom_call_target="tpu_custom_call" | custom-call | tf_op jit(solution)/shard_map/pallas_call | solution.py:848
  13.7 1.7 %collective-permute-start.5 = (f32[4,40,128]{2,1,0:T(8,128)S(1)}, f32[4,40,128]{2,1,0:T(8,128)S(1)}, u32[]{:S(2)}, u32[]{:S(2)}) collective-permute-start(f32[4,40,128]{2,1,0:T(8,128)S(1)} %get-tuple-element.28), channel_id=1, source_target_pairs={{0,1},{1,2},{2,3},{3,0},{4,5},{5,6},{6,7},{7,4},{8,9},{9,10},{10,1... | collective-permute-start | bytes 245768 | tf_op jit(solution)/shard_map/ppermute | solution.py:860
  15.5 1.3 %collective-permute-start.6 = (f32[4,40,128]{2,1,0:T(8,128)S(1)}, f32[4,40,128]{2,1,0:T(8,128)S(1)}, u32[]{:S(2)}, u32[]{:S(2)}) collective-permute-start(f32[4,40,128]{2,1,0:T(8,128)S(1)} %get-tuple-element.29), channel_id=1, source_target_pairs={{0,3},{1,0},{2,1},{3,2},{4,7},{5,4},{6,5},{7,6},{8,11},{9,8},{10,9... | collective-permute-start | bytes 245768 | tf_op jit(solution)/shard_map/ppermute | solution.py:860
  16.7 6.0 %shard_map.124 = (f32[3,18,24,128]{3,2,1,0:T(8,128)S(1)}, f32[18,24,128]{2,1,0:T(8,128)S(1)}, f32[18,24,128]{2,1,0:T(8,128)S(1)}, f32[9,18,24,128]{3,2,1,0:T(8,1...) custom-call(f32[8,128]{1,0:T(8,128)S(1)} %get-tuple-element.24.refs_7_.refs_0_, ...), custom_call_target="tpu_custom_call" | custom-call | flops 73728000 | bytes 14745600 | tf_op jit(solution)/shard_map/pallas_call | solution.py:848
  22.8 0.0 collective-permute-done.5.refs_2_
  22.8 0.0 collective-permute-done.6.refs_3_
  22.8 2.9 %shard_map.125 = (f32[10,5,32,128]{3,2,1,0:T(8,128)S(1)}, f32[5,32,128]{2,1,0:T(8,128)S(1)}, f32[5,32,128]{2,1,0:T(8,128)S(1)}, f32[9,5,32,128]{3,2,1,0:T(8,128)...) custom-call(f32[8,128]{1,0:T(8,128)S(1)} %get-tuple-element.24.refs_7_.refs_0_, ...), custom_call_target="tpu_custom_call" | custom-call | tf_op jit(solution)/shard_map/pallas_call | solution.py:848
  25.6 14.0 %all_to_all.11 = f32[32,1,128]{2,1,0:T(1,128)S(1)} all-to-all(f32[32,1,128]{2,1,0:T(1,128)S(1)} %bitcast.5), channel_id=1, replica_groups=mesh['gx'=2,'gy'=4,'gz'=4] {'gx','gy','gz'}, dimensions={0} | all-to-all | bytes 32768 | tf_op jit(solution)/shard_map/all_to_all | solution.py:1013
  39.7 1.3 %shard_map.126 = (f32[8,16,128]{2,1,0:T(8,128)}, f32[3,8,16,128]{3,2,1,0:T(8,128)}, f32[8,16,128]{2,1,0:T(8,128)}) custom-call(f32[32,128]{1,0:T(8,128)S(1)} %bitcast.4, f32[3,18,24,128]{3,2,1,0:T(8,128)S(1)} %get-tuple-element.35.refs_1_, f32[18,24,128]{2,1,0:T(8,128)S(1)} %get-tuple-element.36.refs_2_, f32[18,24,128]{2,1,0:T(8,128)S(1)} %get-tuple-element.37.refs_3_, ...), custom_call_target="tpu_custom_call" | custom-call | tf_op jit(solution)/shard_map/pallas_call | solution.py:848
Async XLA Ops:
  3.3 9.6 %collective-permute-start = (f32[10,8,16,128]{3,2,1,0:T(8,128)S(1)}, f32[10,8,16,128]{3,2,1,0:T(8,128)S(1)}, u32[]{:S(2)}, u32[]{:S(2)}) collective-permute-start(f32[10,8,16,128]{3,2,1,0:T(8,128)S(1)} %shard_map.122.refs_0_.refs_1_.refs_6_), channel_id=1, source_target_pairs={{0,16},{16,0},{1,17},{17,1},{2,18},{18,2},{3,19},{19,3},{4,20},{20... | collective-permute-start | bytes 1966088 | tf_op jit(solution)/shard_map/ppermute | solution.py:860
  3.8 7.4 %collective-permute-start.1 = (f32[8,40,128]{2,1,0:T(8,128)S(1)}, f32[8,40,128]{2,1,0:T(8,128)S(1)}, u32[]{:S(2)}, u32[]{:S(2)}) collective-permute-start(f32[8,40,128]{2,1,0:T(8,128)S(1)} %get-tuple-element.25), channel_id=1, source_target_pairs={{0,4},{4,0},{8,12},{12,8},{1,5},{5,1},{9,13},{13,9},{2,6},{6,2},{1... | collective-permute-start | bytes 491528 | tf_op jit(solution)/shard_map/ppermute | solution.py:869
  6.5 4.8 %collective-permute-start.2 = (f32[8,40,128]{2,1,0:T(8,128)S(1)}, f32[8,40,128]{2,1,0:T(8,128)S(1)}, u32[]{:S(2)}, u32[]{:S(2)}) collective-permute-start(f32[8,40,128]{2,1,0:T(8,128)S(1)} %get-tuple-element.26), channel_id=1, source_target_pairs={{0,0},{4,8},{8,4},{12,12},{1,1},{5,9},{9,5},{13,13},{2,2},{6,10},{... | collective-permute-start | bytes 491528 | tf_op jit(solution)/shard_map/ppermute | solution.py:869
  11.3 1.4 %collective-permute-start.3 = (f32[8,40,128]{2,1,0:T(8,128)S(1)}, f32[8,40,128]{2,1,0:T(8,128)S(1)}, u32[]{:S(2)}, u32[]{:S(2)}) collective-permute-start(f32[8,40,128]{2,1,0:T(8,128)S(1)} %collective-permute-done.1.refs_2_.refs_4_), channel_id=1, source_target_pairs={{0,16},{16,0},{1,17},{17,1},{2,18},{18,2},{3,19},{19,3},{4,20},{20... | collective-permute-start | bytes 491528 | tf_op jit(solution)/shard_map/ppermute | solution.py:860
  11.3 1.6 %collective-permute-start.4 = (f32[8,40,128]{2,1,0:T(8,128)S(1)}, f32[8,40,128]{2,1,0:T(8,128)S(1)}, u32[]{:S(2)}, u32[]{:S(2)}) collective-permute-start(f32[8,40,128]{2,1,0:T(8,128)S(1)} %collective-permute-done.2.refs_3_.refs_5_), channel_id=1, source_target_pairs={{0,16},{16,0},{1,17},{17,1},{2,18},{18,2},{3,19},{19,3},{4,20},{20... | collective-permute-start | bytes 491528 | tf_op jit(solution)/shard_map/ppermute | solution.py:860
  13.7 9.0 %collective-permute-start.5 = (f32[4,40,128]{2,1,0:T(8,128)S(1)}, f32[4,40,128]{2,1,0:T(8,128)S(1)}, u32[]{:S(2)}, u32[]{:S(2)}) collective-permute-start(f32[4,40,128]{2,1,0:T(8,128)S(1)} %get-tuple-element.28), channel_id=1, source_target_pairs={{0,1},{1,2},{2,3},{3,0},{4,5},{5,6},{6,7},{7,4},{8,9},{9,10},{10,1... | collective-permute-start | bytes 245768 | tf_op jit(solution)/shard_map/ppermute | solution.py:860
  15.5 7.3 %collective-permute-start.6 = (f32[4,40,128]{2,1,0:T(8,128)S(1)}, f32[4,40,128]{2,1,0:T(8,128)S(1)}, u32[]{:S(2)}, u32[]{:S(2)}) collective-permute-start(f32[4,40,128]{2,1,0:T(8,128)S(1)} %get-tuple-element.29), channel_id=1, source_target_pairs={{0,3},{1,0},{2,1},{3,2},{4,7},{5,4},{6,5},{7,6},{8,11},{9,8},{10,9... | collective-permute-start | bytes 245768 | tf_op jit(solution)/shard_map/ppermute | solution.py:860

commit v4 on v3

--- a/solution.py
+++ b/solution.py
@@ -28,7 +28,7 @@
 SUMS = 4 + 4 * len(PAIRS)
 SEG = 16
 ENDS = 2 * SEG
-UNROLL = 4
+UNROLL = dict(assemble=8, faces=8, start=8, next=8, shear=8, motion=8, image=8, finish=8)
 
 
 def up_to(value, multiple):
@@ -55,39 +55,49 @@
     return motion[f - MOTION, *at] if f < SOURCE else body[f - BODY, *at]
 
 
-def fetch(sources, held, arrived):
-    copies = [
-        pltpu.make_async_copy(source, copy, arrived.at[i])
-        for i, (source, copy) in enumerate(zip(sources, held))
-    ]
-    for copy in copies:
-        copy.start()
-    for copy in copies:
-        copy.wait()
+class Fetch:
+    def __init__(self, sources, held, arrived):
+        self.held = held
+        self.copies = [
+            pltpu.make_async_copy(source, copy, arrived.at[i])
+            for i, (source, copy) in enumerate(zip(sources, held))
+        ]
+        self.waiting = set(range(len(held)))
+        for i in sorted(self.waiting, key=lambda i: FETCH_ORDER.index(i)):
+            self.copies[i].start()
+
+    def need(self, *which):
+        for i in which:
+            if i in self.waiting:
+                self.waiting.remove(i)
+                self.copies[i].wait()
+
+
+FETCH_ORDER = (5, 1, 3, 0, 2, 6, 4, 7, 8, 9)
+NEEDS = ((5,), (1,), (3,), (3,), (3,), (0, 2), (6,), (4,), (4,), (4,))
 
 
 def pack_rows(*refs):
     sources, (first, second, table), held, arrived = refs[:10], refs[10:13], refs[13:23], refs[23]
-    fetch(sources, held, arrived)
+    fetch = Fetch(sources, held, arrived)
     raw, tables = held[:7], held[7:]
     nx, ny, nz = raw[0].shape
     spare = MSG_ROWS - sum(WIDTHS)
-
-    def messages(upward, downward):
+    even = lax.axis_index("gy") % 2 == 0
+    for f in range(NF):
+        width, offset = WIDTHS[f], OFFSETS[f]
+        rows = slice(offset, offset + width)
+        fetch.need(*NEEDS[f])
         for x in range(nx):
-            for f in range(NF):
-                width, offset = WIDTHS[f], OFFSETS[f]
-                value = field_of(raw, f, (x, slice(None)))
-                upward[x, offset : offset + width, :] = value[ny - width :]
-                downward[x, offset : offset + width, :] = value[:width]
-            if spare:
-                empty = jnp.zeros((spare, nz), jnp.float32)
-                upward[x, MSG_ROWS - spare :, :] = empty
-                downward[x, MSG_ROWS - spare :, :] = empty
-
-    even = lax.axis_index("gy") % 2 == 0
-    pl.when(even)(lambda: messages(first, second))
-    pl.when(jnp.logical_not(even))(lambda: messages(second, first))
+            value = field_of(raw, f, (x, slice(None)))
+            upward, downward = value[ny - width :], value[:width]
+            first[x, rows, :] = jnp.where(even, upward, downward)
+            second[x, rows, :] = jnp.where(even, downward, upward)
+    if spare:
+        for x in range(nx):
+            for ref in (first, second):
+                ref[x, MSG_ROWS - spare :, :] = jnp.zeros((spare, nz), jnp.float32)
+    fetch.need(7, 8, 9)
     shape = (TILE, LANES)
     tile = jnp.zeros(shape, jnp.float32)
     for t in range(len(tables)):
@@ -99,9 +109,10 @@
 
 def pack_fields(*refs):
     sources, fields, held, arrived = refs[:7], refs[8], refs[9:16], refs[16]
-    fetch(sources, held, arrived)
-    for x in range(fields.shape[1]):
-        for f in range(NF):
+    fetch = Fetch(sources, held, arrived)
+    for f in range(NF):
+        fetch.need(*NEEDS[f])
+        for x in range(fields.shape[1]):
             fields[f, x] = field_of(held, f, (x, slice(None)))
 
 
@@ -136,48 +147,96 @@
     return jnp.where(at > 0, 1.0, 0.0), jnp.where(at < peers - 1, 1.0, 0.0)
 
 
-def pack_ends(peers, *refs):
-    ends, rightward, leftward, stage = refs[-4:]
-    blocks = blocks_of(peers)
-    _, nx, ny, nz = refs[0].shape
+def block_ends(peers, keep, fields, first, second, stage, put):
+    _, nx, ny, nz = fields.shape
     tall = ny + 2 * TILE
     pack = LANES // tall
     count = nx // pack
     gap = jnp.zeros((TILE, nz), jnp.float32)
+    rows = Rows(first, second, peers)
+    for g in range(count):
+        for f in range(NF):
+            width = WIDTHS[f]
+            slot = g * NF + f
+            for p in range(pack):
+                x = g * pack + p
+                top = p * tall
+                stage[slot, top : top + TILE, :] = gap
+                stage[slot, top + TILE + ny : top + tall, :] = gap
+                stage[slot, top + TILE : top + TILE + ny, :] = fields[f, x]
+                low, high = rows.read(f, x)
+                stage[slot, top + TILE - width : top + TILE, :] = low
+                stage[slot, top + TILE + ny : top + TILE + ny + width, :] = high
+            begin = stage[slot, :, :LANES].T
+            finish = begin if nz == LANES else stage[slot, :, nz - LANES :].T
+            if not isinstance(keep, float):
+                begin, finish = begin * keep, finish * keep
+            put(f, g, begin, finish)
+
+
+def put_ends(ends, f, g, begin, finish):
     zeros = jnp.zeros((TILE, LANES), jnp.float32)
     inner = SEG - W
-    spare = MSG_ROWS - sum(WIDTHS)
-    for b, (start, keep) in enumerate(blocks):
-        fields = refs[b]
-        first, second = refs[len(blocks) + 2 * b : len(blocks) + 2 * b + 2]
-        rows = Rows(first, second, peers)
-        for i in range(count):
-            g = start * count + i
-            if spare:
-                rightward[g, MSG_ROWS - spare :, :] = zeros[:spare]
-                leftward[g, MSG_ROWS - spare :, :] = zeros[:spare]
-            for f in range(NF):
-                width, offset = WIDTHS[f], OFFSETS[f]
-                slot = (b * count + i) * NF + f
-                for p in range(pack):
-                    x = i * pack + p
-                    top = p * tall
-                    stage[slot, top : top + TILE, :] = gap
-                    stage[slot, top + TILE + ny : top + tall, :] = gap
-                    stage[slot, top + TILE : top + TILE + ny, :] = fields[f, x]
-                    low, high = rows.read(f, x)
-                    stage[slot, top + TILE - width : top + TILE, :] = low
-                    stage[slot, top + TILE + ny : top + TILE + ny + width, :] = high
-                begin = stage[slot, :, :LANES].T
-                finish = begin if nz == LANES else stage[slot, :, nz - LANES :].T
-                if len(blocks) > 2:
-                    begin, finish = begin * keep, finish * keep
-                rightward[g, offset : offset + width, :] = finish[LANES - width :]
-                leftward[g, offset : offset + width, :] = begin[:width]
-                ends[f, g, :TILE, :] = zeros
-                ends[f, g, ENDS - TILE :, :] = zeros
-                ends[f, g, W:SEG, :] = begin[:inner]
-                ends[f, g, SEG : ENDS - W, :] = finish[LANES - inner :]
+    ends[f, g, :TILE, :] = zeros
+    ends[f, g, ENDS - TILE :, :] = zeros
+    ends[f, g, W:SEG, :] = begin[:inner]
+    ends[f, g, SEG : ENDS - W, :] = finish[LANES - inner :]
+
+
+def put_message(peers, messages, f, g, begin, finish):
+    rows = slice(OFFSETS[f], OFFSETS[f] + WIDTHS[f])
+    rightward, leftward = finish[LANES - WIDTHS[f] :], begin[: WIDTHS[f]]
+    if peers[0] == 2:
+        first = lax.axis_index("gx") == 0
+        messages[0][g, rows, :] = jnp.where(first, rightward, leftward)
+    else:
+        messages[0][g, rows, :] = rightward
+        messages[1][g, rows, :] = leftward
+
+
+def pack_own(peers, fields, first, second, ends, *refs):
+    *messages, stage = refs
+
+    def put(f, g, begin, finish):
+        put_ends(ends, f, g, begin, finish)
+        put_message(peers, messages, f, g, begin, finish)
+
+    for message in messages:
+        message[:, MSG_ROWS - TILE :, :] = jnp.zeros(
+            (message.shape[0], TILE, LANES), jnp.float32
+        )
+    block_ends(peers, 1.0, fields, first, second, stage, put)
+
+
+def pack_others(peers, *refs):
+    blocks = blocks_of(peers)
+    sides = 1 if peers[0] == 2 else 2
+    own_ends, own = refs[0], refs[1 : 1 + sides]
+    others = refs[1 + sides : 1 + sides + 3 * (len(blocks) - 1)]
+    ends, *messages, stage = refs[1 + sides + 3 * (len(blocks) - 1) :]
+    count = own_ends.shape[1]
+    mine = blocks[0][0] * count
+    for g in range(count):
+        for f in range(NF):
+            ends[f, mine + g] = own_ends[f, g]
+        for message, part in zip(messages, own):
+            message[mine + g] = part[g]
+    for b, (start, keep) in enumerate(blocks[1:]):
+
+        def put(f, g, begin, finish, start=start):
+            put_ends(ends, f, start * count + g, begin, finish)
+            put_message(peers, messages, f, start * count + g, begin, finish)
+
+        for message in messages:
+            for g in range(count):
+                message[start * count + g, MSG_ROWS - TILE :, :] = jnp.zeros(
+                    (TILE, LANES), jnp.float32
+                )
+        block_ends(peers, keep, *others[3 * b : 3 * b + 3], stage, put)
+
+
+def times(value, factor):
+    return value if factor == 1.0 else factor * value
 
 
 def harmonic(a, b):
@@ -201,7 +260,9 @@
     return jnp.where(zone > 0.0, biot_coef * biot_coef / scale, 0.0)
 
 
+FIRST_IMAGES, SECOND_IMAGES = (0, 1), (2,)
 KEPT = ("motion", "z0", "p0", "zs", "ps")
+PASSED = ("heft", "mx", "my", "mz", "react", "tx", "ty", "tz", "pdiag", "ediag", "einv")
 ARRAYS = (
     ("zone", 0),
     ("press", 0),
@@ -226,7 +287,6 @@
     ("p0", 0),
     ("ediag", 3),
     ("einv", 3),
-    ("push", 3),
     ("zs", 9),
     ("ps", 9),
 )
@@ -309,10 +369,11 @@
     def parts(ref, j):
         return [ref.at[3 * j + c] for c in range(3)]
 
-    def elastic(self, refs, l, j):
+    def elastic(self, refs, l):
         steps = [self.steps(ref, l) for ref in refs]
         pushed = self.heft[l] * (steps[0][0] + steps[1][1] + steps[2][2])
-        self.keep_push(j, l, pushed)
+        before = self.push_before(refs, l)
+        self.carried = pushed
         out = []
         for c in range(3):
             dx, dy, dz = steps[c]
@@ -321,9 +382,9 @@
                 step_y = step_y + pushed
             if c == 2:
                 step_z = step_z + pushed
-            push = (j, pushed) if c == 0 else None
+            push = (before, pushed) if c == 0 else None
             out.append(
-                support * refs[c][l]
+                times(refs[c][l], support)
                 + self.back_x(self.mx, dx, refs[c], l, push)
                 + self.back_y(step_y)
                 + self.back_z(step_z)
@@ -351,7 +412,7 @@
         )
         inside = self.zone[l] > 0.0
         beside = (self.prv(self.heft, l), self.ym(weight), self.zm(weight))
-        image = self.elastic(self.parts(self.motion, 0), l, 0)
+        image = self.elastic(self.parts(self.motion, 0), l)
         grads = [self.gradient(ref, l) for ref in (self.press, self.z0, self.p0)]
         for c in range(3):
             diag = base + beside[c]
@@ -365,20 +426,29 @@
             self.zs[6 + c, l] = grads[2][c] * scale
 
     def motion_next(self, l, j):
-        image = self.elastic(self.parts(self.zs, j), l, j)
+        image = self.elastic(self.parts(self.zs, j), l)
         for c in range(3):
             self.ps[3 * j + c, l] = image[c] * self.einv[c, l]
 
     def stages(self):
-        self.run(4, self.press_faces, 1)
-        self.run(4, self.press_start)
-        self.run(3, self.press_next)
-        self.run(2, self.motion_faces, 1)
-        self.lead(2, lambda l: self.first_push(self.parts(self.motion, 0), l, 0))
-        self.run(2, self.motion_start)
-        for j in range(3):
-            self.lead(1, lambda l: self.first_push(self.parts(self.zs, j), l, j))
-            self.run(1, lambda l: self.motion_next(l, j))
+        self.first_half()
+        self.second_half()
+
+    def first_half(self):
+        self.run(4, self.press_faces, "faces", 1)
+        self.run(4, self.press_start, "start")
+        self.run(3, self.press_next, "next")
+        self.run(2, self.motion_faces, "shear", 1)
+        self.run(2, self.motion_start, "motion")
+        for j in FIRST_IMAGES:
+            self.images(j)
+
+    def second_half(self):
+        for j in SECOND_IMAGES:
+            self.images(j)
+
+    def images(self, j):
+        self.run(1, lambda l: self.motion_next(l, j), "image")
 
     def finish(self, l, acc, mask):
         own = self.own
@@ -418,20 +488,21 @@
             flat = [(faces[d], moved[c][d]) for c in range(3) for d in range(3)]
             steps.append([v for _, v in flat] + [div] + pa[j])
             heavy.append([f * v for f, v in flat] + [weight * div])
-            heavy[j] = heavy[j] + [support * v for v in pa[j]]
+            heavy[j] = heavy[j] + [times(v, support) for v in pa[j]]
         for i, (j, k) in enumerate(PAIRS):
             add(4 + i, total(zip(dz[j], za[k])))
             add(10 + i, total(zip(dp[k], za[j])))
             add(16 + i, total(zip(dp[j], pa[k])))
             add(22 + i, total(zip(heavy[j], steps[k])))
 
-    @staticmethod
-    def loop(start, count, body, unroll=UNROLL):
-        if not isinstance(count, int):
-            unroll = 1
+    def loop(self, start, count, body, stage):
+        unroll = 1
+        if isinstance(count, int):
+            unroll = -(-count // -(-count // UNROLL[stage]))
         chunks = count // unroll
 
         def step(i, carry):
+            self.carried = None
             for u in range(unroll):
                 body(start + i * unroll + u)
             return carry
@@ -440,6 +511,7 @@
             step(0, 0)
         else:
             lax.fori_loop(0, chunks, step, 0)
+            self.carried = None
         if isinstance(count, int):
             for u in range(chunks * unroll, count):
                 body(start + u)
@@ -467,15 +539,16 @@
     def back_x(self, faces, step, ref, l, push=None):
         out = faces[l - 1] * (ref[l] - ref[l - 1]) - faces[l] * step
         if push:
-            out = out + (self.push[push[0], l - 1] - push[1])
+            out = out + (push[0] - push[1])
         return out
 
-    def keep_push(self, j, l, value):
-        self.push[j, l] = value
-
-    def first_push(self, refs, l, j):
-        dx, dy, dz = [self.steps(ref, l)[i] for i, ref in enumerate(refs)]
-        self.push[j, l] = self.heft[l] * (dx + dy + dz)
+    def push_before(self, refs, l):
+        if self.carried is not None:
+            return self.carried
+        a, b, c = refs
+        own_b, own_c = b[l - 1], c[l - 1]
+        change = (a[l] - a[l - 1]) + (self.yp(own_b) - own_b) + (self.zp(own_c) - own_c)
+        return self.heft[l - 1] * change
 
     def own(self, v):
         return v[: self.ny]
@@ -498,11 +571,9 @@
             return halo
         return halo * (self.has_below + self.has_above)
 
-    def run(self, halo, body, before=0):
-        self.loop(self.first(halo) - before, self.nx + self.reach(halo) + before, body)
-
-    def lead(self, halo, body):
-        body(self.first(halo) - 1)
+    def run(self, halo, body, stage, before=0):
+        count = self.nx + self.reach(halo) + before
+        self.loop(self.first(halo) - before, count, body, stage)
 
     def narrow(self, v):
         ny = self.ny
@@ -565,21 +636,45 @@
             self.motion[c, l] = self.narrow(self.tall[MOTION + c, l])
 
 
-def brick_kernel(peers, *refs):
-    table, fields, below, above = refs[:4]
-    rows = [Rows(*refs[i : i + 2], peers) for i in (4, 6, 8)]
-    outs, acc, scratch = refs[10 : 10 + len(KEPT)], refs[10 + len(KEPT)], refs[11 + len(KEPT) :]
-    inner = len(ARRAYS) - len(KEPT)
-    names = [name for name, _ in ARRAYS if name not in KEPT]
-    domain = Brick(dict(zip(names, scratch[:inner])))
-    domain.__dict__.update(zip(KEPT, outs))
-    domain.tall, domain.perm_tall, domain.ty_tall = scratch[inner:]
-    _, nx, ny, nz = fields.shape
-    domain.nx, domain.ny = nx, ny
+def new_brick(peers, nx, ny):
+    domain = Brick(dict(nx=nx, ny=ny, pair=peers[0] == 2))
     at = lax.axis_index("gx")
     domain.has_below = (at > 0).astype(jnp.int32)
     domain.has_above = (at < peers[0] - 1).astype(jnp.int32)
-    domain.pair = peers[0] == 2
+    return domain
+
+
+FIRST_OUTS = ("motion", "z0", "p0", "zs") + PASSED
+FIRST_SCRATCH = tuple(n for n, _ in ARRAYS if n not in FIRST_OUTS + ("ps",))
+
+
+class Joined:
+    def __init__(self, *refs):
+        self.refs = refs
+        self.at = self
+
+    def __getitem__(self, index):
+        first, *rest = index if isinstance(index, tuple) else (index,)
+        for ref in self.refs:
+            if first < ref.shape[0]:
+                return ref[first, *rest] if rest else ref.at[first]
+            first -= ref.shape[0]
+
+    def __setitem__(self, index, value):
+        self[index[0]][index[1:]] = value
+
+
+def brick_first(peers, *refs):
+    table, fields, below, above = refs[:4]
+    rows = [Rows(*refs[i : i + 2], peers) for i in (4, 6, 8)]
+    outs = refs[10 : 10 + len(FIRST_OUTS)]
+    ps, *scratch = refs[10 + len(FIRST_OUTS) :]
+    _, nx, ny, nz = fields.shape
+    domain = new_brick(peers, nx, ny)
+    domain.__dict__.update(zip(FIRST_OUTS, outs))
+    domain.__dict__.update(zip(FIRST_SCRATCH, scratch))
+    domain.tall, domain.perm_tall, domain.ty_tall = scratch[len(FIRST_SCRATCH) :]
+    domain.ps = Joined(ps)
 
     empty = jnp.zeros((ny + TILE, nz), jnp.float32)
     for l in (W - 1, W + nx):
@@ -589,27 +684,48 @@
             domain.motion[c, l] = empty
         for i in range(9):
             domain.zs[i, l] = empty
-            domain.ps[i, l] = empty
+        for i in range(ps.shape[0]):
+            ps[i, l] = empty
         domain.perm_tall[l] = jnp.zeros((ny + 2 * TILE, nz), jnp.float32)
 
     def block(start, count, shift, *source):
         domain.loop(
-            start, count, lambda l: domain.assemble(l, l + shift, *source, table)
+            start,
+            count,
+            lambda l: domain.assemble(l, l + shift, *source, table),
+            "assemble",
         )
 
     block(W, nx, -W, fields, rows[0])
     if domain.pair:
+        at = lax.axis_index("gx")
         start = jnp.where(at > 0, 0, W + nx)
         shift = jnp.where(at > 0, nx - W, -W - nx)
         block(start, W, shift, below, rows[1])
     else:
         block(0, W * domain.has_below, nx - W, below, rows[1])
         block(W + nx, W * domain.has_above, -W - nx, above, rows[2])
-    domain.stages()
+    domain.first_half()
+
+
+SECOND_INS = ("z0", "p0", "zs") + PASSED
+
+
+def brick_second(peers, nx, ny, *refs):
+    domain = new_brick(peers, nx, ny)
+    domain.__dict__.update(zip(SECOND_INS, refs))
+    ready, ps, acc = refs[len(SECOND_INS) :]
+    domain.ps = Joined(ready, ps)
+    nz = ps.shape[3]
+    empty = jnp.zeros((ny + TILE, nz), jnp.float32)
+    for l in (W - 1, W + nx):
+        for i in range(ps.shape[0]):
+            ps[i, l] = empty
+    domain.second_half()
     acc[...] = jnp.zeros(acc.shape, jnp.float32)
     column = iota((TILE, nz), 1)
     mask = (column >= W) & (column < nz - W)
-    domain.loop(W, nx, lambda l: domain.finish(l, acc, mask))
+    domain.loop(W, nx, lambda l: domain.finish(l, acc, mask), "finish")
 
 
 class Ends(Domain):
@@ -635,8 +751,8 @@
             value = value + push[1]
         return self.before(value) - value
 
-    def keep_push(self, j, l, value):
-        pass
+    def push_before(self, refs, l):
+        return None
 
     def yp(self, v):
         return self.roll(v, -1)
@@ -662,11 +778,8 @@
                 total = piece if total is None else total + piece
         return total
 
-    def run(self, halo, body, before=0):
-        body(pl.ds(0, self.groups))
-
-    def lead(self, halo, body):
-        pass
+    def run(self, halo, body, stage, before=0):
+        body(pl.ds(0, self.groups) if halo > 3 else self.near)
 
     def assemble(self, ends, left, right, keep_left, keep_right, table):
         for g in range(self.groups):
@@ -686,12 +799,24 @@
             self.fixed[g] = fixed_term(zone, lame, shear)
 
 
+class Either:
+    def __init__(self, condition, yes, no):
+        self.condition, self.refs = condition, (yes, no)
+
+    def __getitem__(self, index):
+        return jnp.where(self.condition, *[ref[index] for ref in self.refs])
+
+
 def own_groups(count, peers):
     return count * blocks_of(peers)[0][0]
 
 
 def ends_kernel(peers, tall, *refs):
-    table, ends, left, right, added = refs[:5]
+    table, ends, got, passed, added = refs[:5]
+    left, right = got, passed
+    if peers[0] == 2:
+        first = lax.axis_index("gx") == 0
+        left, right = Either(first, got, passed), Either(first, passed, got)
     raw, z0, p0, zs, ps, partial = refs[5:11]
     acc, scratch = refs[11], refs[12:]
     names = [name for name, _ in ARRAYS[6:] if name not in KEPT]
@@ -704,13 +829,19 @@
     domain.row = tall
     domain.groups = groups = raw.shape[1] - 1
     count = groups // len(blocks_of(peers))
+    domain.near = pl.ds(0, groups)
+    if peers[0] == 2 and LANES // tall > 3:
+        domain.near = pl.ds(lax.axis_index("gx") * (count - 1), count + 1)
     keep = keeps("gz", peers[2])
     empty = jnp.zeros((ENDS, LANES), jnp.float32)
     for ref in (raw, zs, ps):
         for i in range(ref.shape[0]):
             ref[i, groups] = empty
+            if ref is not raw:
+                ref[i, groups - 1] = empty
     for ref in (domain.perm, domain.shear, z0, p0):
         ref[groups] = empty
+    p0[groups - 1] = empty
     mine = own_groups(count, peers)
     domain.assemble(ends, left, right, *keep, table)
     domain.stages()
@@ -742,9 +873,9 @@
 
 
 def combine(peers, tall, *refs):
-    sums, (old, z0, p0, zs, ps), fields = refs[0], refs[1:6], refs[6]
-    raw, ends_z0, ends_p0, ends_zs, ends_ps = refs[7:12]
-    pressure, motion, strain, moved, ends_moved, turned = refs[12:]
+    sums, (old, z0, p0, zs), ps, fields = refs[0], refs[1:5], Joined(*refs[5:7]), refs[7]
+    raw, ends_z0, ends_p0, ends_zs, ends_ps = refs[8:13]
+    pressure, motion, strain, moved, ends_moved, turned = refs[13:]
     line = jnp.sum(sums[...], axis=0, keepdims=True)
     lane = iota(line.shape, 1)
 
@@ -779,10 +910,13 @@
     count = groups // len(blocks_of(peers))
     mine = own_groups(count, peers)
     every = pl.ds(0, groups)
+    if peers[0] == 2 and pack > 3:
+        every = pl.ds(lax.axis_index("gx") * (count - 1), count + 1)
     for c in range(3):
-        for g in range(groups):
+        for i in range(every.size):
+            g = every.start + i
             ends_moved[c, g] = new_motion(raw[MOTION + c, g], ends_zs, ends_ps, c, g)
-        ends_moved[c, groups] = jnp.zeros((ENDS, LANES), jnp.float32)
+        ends_moved[c, every.start + every.size] = jnp.zeros((ENDS, LANES), jnp.float32)
     along_y, along_z = ends_moved[1, every], ends_moved[2, every]
     first = ends_moved.at[0]
     ends_moved[3, every] = 0.5 * (
@@ -891,6 +1025,7 @@
     nx, ny, nz = source.shape
     peers = [lax.axis_size(a) for a in AXES]
     total = peers[0] * peers[1] * peers[2]
+    pair = peers[0] == 2
     tall = ny + 2 * TILE
     groups = nx * tall // LANES
 
@@ -937,26 +1072,36 @@
     second = pairs(second, "gy", 1)
     first_below, first_above = x_neighbours(first)
     second_below, second_above = x_neighbours(second)
-    blocks = [
-        (fields, first, second),
+    others = [
         (fields_below, first_below, second_below),
         (fields_above, first_above, second_above),
-    ][: 2 if peers[0] == 2 else 3]
-    span = len(blocks) * groups
-    ends, rightward, leftward = call(
-        with_peers(pack_ends),
-        [
-            f32(NF, span, ENDS, LANES),
-            f32(span, MSG_ROWS, LANES),
-            f32(span, MSG_ROWS, LANES),
-        ],
-        *[block[0] for block in blocks],
-        *[rows for block in blocks for rows in block[1:]],
-        scratch=[vmem(NF * span, LANES, nz)],
+    ][: 1 if pair else 2]
+    sides = 1 if pair else 2
+    own_ends, *own_messages = call(
+        with_peers(pack_own),
+        [f32(NF, groups, ENDS, LANES)] + [f32(groups, MSG_ROWS, LANES)] * sides,
+        fields,
+        first,
+        second,
+        scratch=[vmem(NF * groups, LANES, nz)],
+    )
+    span = (1 + len(others)) * groups
+    ends, *messages = call(
+        with_peers(pack_others),
+        [f32(NF, span, ENDS, LANES)] + [f32(span, MSG_ROWS, LANES)] * sides,
+        own_ends,
+        *own_messages,
+        *[array for block in others for array in block],
+        scratch=[vmem(NF * groups, LANES, nz)],
         limit=12,
     )
-    left = ring(rightward, "gz", 1)
-    right = ring(leftward, "gz", -1)
+    if pair:
+        n = peers[2]
+        hops = [(i, (i + 1) % n) for i in range(n)]
+        hops += [(n + i, n + (i - 1) % n) for i in range(n)]
+        got = lax.ppermute(messages[0], ("gx", "gz"), hops)
+    else:
+        got, passed = ring(messages[0], "gz", 1), ring(messages[1], "gz", -1)
     depth = nx + 2 * W
     cells = depth * ny * nz
 
@@ -965,10 +1110,14 @@
 
     leads = dict(ARRAYS)
     sums_shape = (up_to(SUMS, TILE), TILE, LANES)
-    *kept, added = call(
-        with_peers(brick_kernel),
-        [f32(*shaped(leads[name], depth, ny + TILE, nz)) for name in KEPT]
-        + [f32(*sums_shape)],
+
+    def layers_of(name):
+        return shaped(leads[name], depth, ny + TILE, nz)
+
+    *halves, ps = call(
+        with_peers(brick_first),
+        [f32(*layers_of(name)) for name in FIRST_OUTS]
+        + [f32(3 * len(FIRST_IMAGES), depth, ny + TILE, nz)],
         table,
         fields,
         fields_below,
@@ -979,18 +1128,20 @@
         second_below,
         first_above,
         second_above,
-        scratch=[
-            vmem(*shaped(lead, depth, ny + TILE, nz))
-            for name, lead in ARRAYS
-            if name not in KEPT
-        ]
+        scratch=[vmem(*layers_of(name)) for name in FIRST_SCRATCH]
         + [vmem(WIDE, depth, tall, nz), vmem(depth, tall, nz), vmem(depth, tall, nz)],
-        limit=24,
-        cost=pl.CostEstimate(
-            flops=2000 * cells, transcendentals=0, bytes_accessed=400 * cells
-        ),
-    )
-    left, right, added = lax.optimization_barrier((left, right, added))
+        limit=16,
+    )
+    half = dict(zip(FIRST_OUTS, halves))
+    if pair:
+        passed = ring(got, "gx", -1)
+    last, added = call(
+        with_peers(brick_second, nx, ny),
+        [f32(3 * len(SECOND_IMAGES), depth, ny + TILE, nz), f32(*sums_shape)],
+        *[half[name] for name in SECOND_INS],
+        ps,
+    )
+    kept = [half[name] for name in KEPT[:-1]] + [ps, last]
     span = span + 1
     *ends_kept, partial = call(
         with_peers(ends_kernel, tall),
@@ -999,8 +1150,8 @@
         + [f32(total, LANES)],
         table,
         ends,
-        left,
-        right,
+        got,
+        passed,
         added,
         scratch=[vmem(*sums_shape)]
         + [

time: 41.1 us -> 42.5 us (1.034)
  waiting for transfers between devices: 5.25 us -> 8.87 us
  starting transfers between devices: 7.34 us -> 6.08 us
  Pallas kernels: 13.6 us -> 12.4 us
    ppermute x0 -> x1, waiting for transfers between devices: none -> 4.09 us  [shards(): got = lax.ppermute(messages[0], ('gx', 'gz'), hops)]
    ppermute x5 -> x4, starting transfers between devices: 4.05 us -> 1.07 us  [ring(): lax.ppermute(value, axis, [(i, (i + step) % peers) for i in range(peers)])]
    ppermute x0 -> x1, starting transfers between devices: none -> 1.71 us  [shards(): got = lax.ppermute(messages[0], ('gx', 'gz'), hops)]
    pallas_call x6 -> x8, Pallas kernels: 13.6 us -> 12.4 us  [call(): pl.pallas_call(kernel, out_shape=outs, in_specs=specs, scratch_shapes=scr...]
    ppermute x5 -> x4, waiting for transfers between devices: 1.12 us -> 0.65 us  [ring(): lax.ppermute(value, axis, [(i, (i + step) % peers) for i in range(peers)])]
  transfers between devices with their start and end apart: 7 -> 7, of which waited for: 3 -> 4; matrix products, arithmetic and copies ran while one was open for 0% -> 0% of each run, Pallas kernels for 15% -> 13%
where the time goes in v4:
time: 42.5 us; the launch traced here: 42.3 us
  blocking collectives  14.2 us (33%)
  Pallas kernels  12.4 us (29%)
  waiting for transfers between devices  8.87 us (21%)
  starting transfers between devices  6.08 us (14%)
  between operations  0.7 us (2%)
    all_to_all x1, blocking collectives, shards(): sums = lax.all_to_all(partial, AXES, 0, 0, tiled=True)  14.2 us
    pallas_call x8, Pallas kernels, call(): pl.pallas_call(kernel, out_shape=outs, in_specs=specs, scratch_shapes=scr...  12.4 us
    ppermute x2, waiting for transfers between devices, pairs(): return lax.ppermute(value, axis, swaps)  4.13 us
    ppermute x1, waiting for transfers between devices, shards(): got = lax.ppermute(messages[0], ('gx', 'gz'), hops)  4.09 us
    ppermute x2, starting transfers between devices, pairs(): return lax.ppermute(value, axis, swaps)  3.3 us
    ppermute x1, starting transfers between devices, shards(): got = lax.ppermute(messages[0], ('gx', 'gz'), hops)  1.71 us
    ppermute x4, starting transfers between devices, ring(): lax.ppermute(value, axis, [(i, (i + step) % peers) for i in range(peers)])  1.07 us
  transfers between devices with their start and end apart: 7, of which 4 were waited for; matrix products, arithmetic and copies ran while one was open for 0% of the time, Pallas kernels for 13%

profile of v4, /device:TPU:0, one launch (start us, length us, event | category | flops | bytes accessed | tf_op | source)
XLA Modules:
  0.0 42.3 jit_solution(2757846201110171901)
XLA Ops:
  0.6 1.4 %shard_map.121 = (f32[8,40,128]{2,1,0:T(8,128)S(1)}, f32[8,40,128]{2,1,0:T(8,128)S(1)}, f32[8,128]{1,0:T(8,128)S(1)}) custom-call(f32[8,16,128]{2,1,0:T(8,128)} %refs_0_.3, f32[8,16,128]{2,1,0:T(8,128)} %refs_1_.3, f32[8,16,128]{2,1,0:T(8,128)} %refs_2_.3, f32[3,8,16,128]{3,2,1,0:T(8,128)} %refs_3_.3, f32[3,8,16,128]{3,2,1,0:T(8,128)} %refs_4_.3, ...), custom_call_target="tpu_custom_call" | custom-call | tf_op jit(solution)/shard_map/pallas_call | solution.py:982
  2.0 1.3 %shard_map.122.refs_0_.refs_1_.refs_7_ = f32[10,8,16,128]{3,2,1,0:T(8,128)S(1)} custom-call(f32[8,16,128]{2,1,0:T(8,128)} %refs_0_.3, f32[8,16,128]{2,1,0:T(8,128)} %refs_1_.3, f32[8,16,128]{2,1,0:T(8,128)} %refs_2_.3, f32[3,8,16,128]{3,2,1,0:T(8,128)} %refs_3_.3, f32[3,8,16,128]{3,2,1,0:T(8,128)} %refs_4_.3, s32[8,16,128]{2,1,0:T(8,128)} %refs_5_.3, ...), custom_call_target="tpu_custom_call" | custom-call | tf_op jit(solution)/shard_map/pallas_call | solution.py:982
  3.3 0.6 %collective-permute-start.2 = (f32[10,8,16,128]{3,2,1,0:T(8,128)S(1)}, f32[10,8,16,128]{3,2,1,0:T(8,128)S(1)}, u32[]{:S(2)}, u32[]{:S(2)}) collective-permute-start(f32[10,8,16,128]{3,2,1,0:T(8,128)S(1)} %shard_map.122.refs_0_.refs_1_.refs_7_), channel_id=1, source_target_pairs={{0,16},{16,0},{1,17},{17,1},{2,18},{18,2},{3,19},{19,3},{4,20},{20... | collective-permute-start | bytes 1966088 | tf_op jit(solution)/shard_map/ppermute | solution.py:994
  3.8 2.6 %collective-permute-start = (f32[8,40,128]{2,1,0:T(8,128)S(1)}, f32[8,40,128]{2,1,0:T(8,128)S(1)}, u32[]{:S(2)}, u32[]{:S(2)}) collective-permute-start(f32[8,40,128]{2,1,0:T(8,128)S(1)} %get-tuple-element.35), channel_id=1, source_target_pairs={{0,4},{4,0},{8,12},{12,8},{1,5},{5,1},{9,13},{13,9},{2,6},{6,2},{1... | collective-permute-start | bytes 491528 | tf_op jit(solution)/shard_map/ppermute | solution.py:1003
  6.5 0.7 %collective-permute-start.1 = (f32[8,40,128]{2,1,0:T(8,128)S(1)}, f32[8,40,128]{2,1,0:T(8,128)S(1)}, u32[]{:S(2)}, u32[]{:S(2)}) collective-permute-start(f32[8,40,128]{2,1,0:T(8,128)S(1)} %get-tuple-element.36), channel_id=1, source_target_pairs={{0,0},{4,8},{8,4},{12,12},{1,1},{5,9},{9,5},{13,13},{2,2},{6,10},{... | collective-permute-start | bytes 491528 | tf_op jit(solution)/shard_map/ppermute | solution.py:1003
  7.1 4.1 %collective-permute-done.refs_1_.refs_4_ = f32[8,40,128]{2,1,0:T(8,128)S(1)} collective-permute-done((f32[8,40,128]{2,1,0:T(8,128)S(1)}, f32[8,40,128]{2,1,0:T(8,128)S(1)}, u32[]{:S(2)}, u32[]{:S(2)}) %collective-permute-start) | collective-permute-done | bytes 163872 | tf_op jit(solution)/shard_map/ppermute | solution.py:1003
  11.3 0.0 collective-permute-start.3
  11.3 0.0 collective-permute-done.1.refs_2_.refs_5_
  11.3 0.5 %collective-permute-start.4 = (f32[8,40,128]{2,1,0:T(8,128)S(1)}, f32[8,40,128]{2,1,0:T(8,128)S(1)}, u32[]{:S(2)}, u32[]{:S(2)}) collective-permute-start(f32[8,40,128]{2,1,0:T(8,128)S(1)} %collective-permute-done.1.refs_2_.refs_5_), channel_id=1, source_target_pairs={{0,16},{16,0},{1,17},{17,1},{2,18},{18,2},{3,19},{19,3},{4,20},{20... | collective-permute-start | bytes 491528 | tf_op jit(solution)/shard_map/ppermute | solution.py:994
  11.8 0.5 %shard_map.123 = (f32[10,2,32,128]{3,2,1,0:T(8,128)S(1)}, f32[2,40,128]{2,1,0:T(8,128)S(1)}) custom-call(f32[10,8,16,128]{3,2,1,0:T(8,128)S(1)} %shard_map.122.refs_0_.refs_1_.refs_7_, f32[8,40,128]{2,1,0:T(8,128)S(1)} %collective-permute-done.refs_1_.refs_4_, f32[8,40,128]{2,1,0:T(8,128)S(1)} %collective-permute-done.1.refs_2_.refs_5_), custom_call_target="tpu_custom_call" | custom-call | tf_op jit(solution)/shard_map/pallas_call | solution.py:982
  12.3 0.4 collective-permute-done.3.refs_3_.refs_6_.refs_8_
  12.7 0.2 collective-permute-done.4.refs_4_.refs_7_.refs_9_
  12.9 0.0 collective-permute-done.2.refs_2_.refs_3_
  12.9 0.5 %shard_map.124 = (f32[10,4,32,128]{3,2,1,0:T(8,128)S(1)}, f32[4,40,128]{2,1,0:T(8,128)S(1)}) custom-call(f32[10,2,32,128]{3,2,1,0:T(8,128)S(1)} %get-tuple-element.37.refs_0_, f32[2,40,128]{2,1,0:T(8,128)S(1)} %get-tuple-element.38.refs_1_, f32[10,8,16,128]{3,2,1,0:T(8,128)S(1)} %collective-permute-done.2.refs_2_.refs_3_, ...), custom_call_target="tpu_custom_call" | custom-call | tf_op jit(solution)/shard_map/pallas_call | solution.py:982
  13.4 1.7 %collective-permute-start.5 = (f32[4,40,128]{2,1,0:T(8,128)S(1)}, f32[4,40,128]{2,1,0:T(8,128)S(1)}, u32[]{:S(2)}, u32[]{:S(2)}) collective-permute-start(f32[4,40,128]{2,1,0:T(8,128)S(1)} %get-tuple-element.40), channel_id=1, source_target_pairs={{0,1},{1,2},{2,3},{3,0},{16,19},{17,16},{18,17},{19,18},{4,5},{5,6... | collective-permute-start | bytes 245768 | tf_op jit(solution)/shard_map/ppermute | solution.py:1102
  15.1 4.1 %collective-permute-done.5.refs_2_ = f32[4,40,128]{2,1,0:T(8,128)S(1)} collective-permute-done((f32[4,40,128]{2,1,0:T(8,128)S(1)}, f32[4,40,128]{2,1,0:T(8,128)S(1)}, u32[]{:S(2)}, u32[]{:S(2)}) %collective-permute-start.5) | collective-permute-done | bytes 81952 | tf_op jit(solution)/shard_map/ppermute | solution.py:1102
  19.2 0.0 collective-permute-start.6
  19.2 3.6 %shard_map.125 = (f32[3,18,24,128]{3,2,1,0:T(8,128)S(1)}, f32[18,24,128]{2,1,0:T(8,128)S(1)}, f32[18,24,128]{2,1,0:T(8,128)S(1)}, f32[9,18,24,128]{3,2,1,0:T(8,1...) custom-call(f32[8,128]{1,0:T(8,128)S(1)} %get-tuple-element.34.refs_, ...), custom_call_target="tpu_custom_call" | custom-call | tf_op jit(solution)/shard_map/pallas_call | solution.py:982
  22.7 1.5 %shard_map.126 = (f32[3,18,24,128]{3,2,1,0:T(8,128)S(1)}, f32[32,8,128]{2,1,0:T(8,128)S(1)}) custom-call(f32[18,24,128]{2,1,0:T(8,128)S(1)} %get-tuple-element.41.refs_0_.refs_2_, f32[18,24,128]{2,1,0:T(8,128)S(1)} %get-tuple-element.42.refs_1_.refs_3_, f32[9,18,24,128]{3,2,1,0:T(8,128)S(1)} %get-tuple-element.43.refs_2_.refs_4_, ...), custom_call_target="tpu_custom_call" | custom-call | tf_op jit(solution)/shard_map/pallas_call | solution.py:982
  24.2 0.0 collective-permute-done.6.refs_3_
  24.2 2.6 %shard_map.127 = (f32[10,5,32,128]{3,2,1,0:T(8,128)S(1)}, f32[5,32,128]{2,1,0:T(8,128)S(1)}, f32[5,32,128]{2,1,0:T(8,128)S(1)}, f32[9,5,32,128]{3,2,1,0:T(8,128)...) custom-call(f32[8,128]{1,0:T(8,128)S(1)} %get-tuple-element.34.refs_7_.refs_0_, ...), custom_call_target="tpu_custom_call" | custom-call | tf_op jit(solution)/shard_map/pallas_call | solution.py:982
  26.8 14.2 %all_to_all.11 = f32[32,1,128]{2,1,0:T(1,128)S(1)} all-to-all(f32[32,1,128]{2,1,0:T(1,128)S(1)} %bitcast.5), channel_id=1, replica_groups=mesh['gx'=2,'gy'=4,'gz'=4] {'gx','gy','gz'}, dimensions={0} | all-to-all | bytes 32768 | tf_op jit(solution)/shard_map/all_to_all | solution.py:1164
  41.1 1.2 %shard_map.128 = (f32[8,16,128]{2,1,0:T(8,128)}, f32[3,8,16,128]{3,2,1,0:T(8,128)}, f32[8,16,128]{2,1,0:T(8,128)}) custom-call(f32[32,128]{1,0:T(8,128)S(1)} %bitcast.4, f32[3,18,24,128]{3,2,1,0:T(8,128)S(1)} %get-tuple-element.58.refs_1_, f32[18,24,128]{2,1,0:T(8,128)S(1)} %get-tuple-element.41.refs_0_.refs_2_, ...), custom_call_target="tpu_custom_call" | custom-call | tf_op jit(solution)/shard_map/pallas_call | solution.py:982
Async XLA Ops:
  3.3 9.6 %collective-permute-start.2 = (f32[10,8,16,128]{3,2,1,0:T(8,128)S(1)}, f32[10,8,16,128]{3,2,1,0:T(8,128)S(1)}, u32[]{:S(2)}, u32[]{:S(2)}) collective-permute-start(f32[10,8,16,128]{3,2,1,0:T(8,128)S(1)} %shard_map.122.refs_0_.refs_1_.refs_7_), channel_id=1, source_target_pairs={{0,16},{16,0},{1,17},{17,1},{2,18},{18,2},{3,19},{19,3},{4,20},{20... | collective-permute-start | bytes 1966088 | tf_op jit(solution)/shard_map/ppermute | solution.py:994
  3.8 7.4 %collective-permute-start = (f32[8,40,128]{2,1,0:T(8,128)S(1)}, f32[8,40,128]{2,1,0:T(8,128)S(1)}, u32[]{:S(2)}, u32[]{:S(2)}) collective-permute-start(f32[8,40,128]{2,1,0:T(8,128)S(1)} %get-tuple-element.35), channel_id=1, source_target_pairs={{0,4},{4,0},{8,12},{12,8},{1,5},{5,1},{9,13},{13,9},{2,6},{6,2},{1... | collective-permute-start | bytes 491528 | tf_op jit(solution)/shard_map/ppermute | solution.py:1003
  6.5 4.8 %collective-permute-start.1 = (f32[8,40,128]{2,1,0:T(8,128)S(1)}, f32[8,40,128]{2,1,0:T(8,128)S(1)}, u32[]{:S(2)}, u32[]{:S(2)}) collective-permute-start(f32[8,40,128]{2,1,0:T(8,128)S(1)} %get-tuple-element.36), channel_id=1, source_target_pairs={{0,0},{4,8},{8,4},{12,12},{1,1},{5,9},{9,5},{13,13},{2,2},{6,10},{... | collective-permute-start | bytes 491528 | tf_op jit(solution)/shard_map/ppermute | solution.py:1003
  11.3 1.4 %collective-permute-start.3 = (f32[8,40,128]{2,1,0:T(8,128)S(1)}, f32[8,40,128]{2,1,0:T(8,128)S(1)}, u32[]{:S(2)}, u32[]{:S(2)}) collective-permute-start(f32[8,40,128]{2,1,0:T(8,128)S(1)} %collective-permute-done.refs_1_.refs_4_), channel_id=1, source_target_pairs={{0,16},{16,0},{1,17},{17,1},{2,18},{18,2},{3,19},{19,3},{4,20},{20... | collective-permute-start | bytes 491528 | tf_op jit(solution)/shard_map/ppermute | solution.py:994
  11.3 1.6 %collective-permute-start.4 = (f32[8,40,128]{2,1,0:T(8,128)S(1)}, f32[8,40,128]{2,1,0:T(8,128)S(1)}, u32[]{:S(2)}, u32[]{:S(2)}) collective-permute-start(f32[8,40,128]{2,1,0:T(8,128)S(1)} %collective-permute-done.1.refs_2_.refs_5_), channel_id=1, source_target_pairs={{0,16},{16,0},{1,17},{17,1},{2,18},{18,2},{3,19},{19,3},{4,20},{20... | collective-permute-start | bytes 491528 | tf_op jit(solution)/shard_map/ppermute | solution.py:994
  13.4 5.8 %collective-permute-start.5 = (f32[4,40,128]{2,1,0:T(8,128)S(1)}, f32[4,40,128]{2,1,0:T(8,128)S(1)}, u32[]{:S(2)}, u32[]{:S(2)}) collective-permute-start(f32[4,40,128]{2,1,0:T(8,128)S(1)} %get-tuple-element.40), channel_id=1, source_target_pairs={{0,1},{1,2},{2,3},{3,0},{16,19},{17,16},{18,17},{19,18},{4,5},{5,6... | collective-permute-start | bytes 245768 | tf_op jit(solution)/shard_map/ppermute | solution.py:1102
  19.2 5.0 %collective-permute-start.6 = (f32[4,40,128]{2,1,0:T(8,128)S(1)}, f32[4,40,128]{2,1,0:T(8,128)S(1)}, u32[]{:S(2)}, u32[]{:S(2)}) collective-permute-start(f32[4,40,128]{2,1,0:T(8,128)S(1)} %collective-permute-done.5.refs_2_), channel_id=1, source_target_pairs={{0,16},{16,0},{1,17},{17,1},{2,18},{18,2},{3,19},{19,3},{4,20},{20... | collective-permute-start | bytes 245768 | tf_op jit(solution)/shard_map/ppermute | solution.py:994

commit v5 on v4

--- a/solution.py
+++ b/solution.py
@@ -21,14 +21,16 @@
 ZONE, PRESS, MOTION, SOURCE, DRAIN, BODY = 0, 1, 2, 5, 6, 7
 WIDTHS = (5, 5, 5, 5, 5, 4, 4, 2, 2, 2)
 NF = len(WIDTHS)
-WIDE = 5
 W = max(WIDTHS)
 OFFSETS = tuple(sum(WIDTHS[:f]) for f in range(NF))
+ROW_WIDTHS = (5, 4, 4, 3, 4, 4, 4, 2, 2, 2)
+ROW_OFFSETS = tuple(sum(ROW_WIDTHS[:f]) for f in range(NF))
+ROWS_EACH = sum(ROW_WIDTHS)
 PAIRS = tuple((j, k) for j in range(3) for k in range(j, 3))
 SUMS = 4 + 4 * len(PAIRS)
 SEG = 16
 ENDS = 2 * SEG
-UNROLL = dict(assemble=8, faces=8, start=8, next=8, shear=8, motion=8, image=8, finish=8)
+UNROLL = dict(faces=8, start=8, next=8, shear=8, motion=8, image=8, finish=8)
 
 
 def up_to(value, multiple):
@@ -82,21 +84,7 @@
     fetch = Fetch(sources, held, arrived)
     raw, tables = held[:7], held[7:]
     nx, ny, nz = raw[0].shape
-    spare = MSG_ROWS - sum(WIDTHS)
     even = lax.axis_index("gy") % 2 == 0
-    for f in range(NF):
-        width, offset = WIDTHS[f], OFFSETS[f]
-        rows = slice(offset, offset + width)
-        fetch.need(*NEEDS[f])
-        for x in range(nx):
-            value = field_of(raw, f, (x, slice(None)))
-            upward, downward = value[ny - width :], value[:width]
-            first[x, rows, :] = jnp.where(even, upward, downward)
-            second[x, rows, :] = jnp.where(even, downward, upward)
-    if spare:
-        for x in range(nx):
-            for ref in (first, second):
-                ref[x, MSG_ROWS - spare :, :] = jnp.zeros((spare, nz), jnp.float32)
     fetch.need(7, 8, 9)
     shape = (TILE, LANES)
     tile = jnp.zeros(shape, jnp.float32)
@@ -105,6 +93,40 @@
             here = (iota(shape, 0) == t) & (iota(shape, 1) == zone + 1)
             tile = jnp.where(here, tables[t][zone], tile)
     table[...] = tile
+    inner = iota((ny, nz), 0) < ny - 1
+    for f in range(NF):
+        width = ROW_WIDTHS[f]
+        fetch.need(*NEEDS[f])
+        for x in range(nx):
+            at = (x, slice(None))
+            value = field_of(raw, f, at)
+            if f == SOURCE:
+                zone, press, middle = [field_of(raw, g, at) for g in (ZONE, PRESS, MOTION + 1)]
+                perm = lookup(zone, tile, 0)
+                face = jnp.where(inner, harmonic(perm, rows_up(perm)), 0.0)
+                value = value - y_part(face, press, middle, inner)
+            upward, downward = value[ny - width :], value[:width]
+            start = x * ROWS_EACH + ROW_OFFSETS[f]
+            first[start : start + width, :] = jnp.where(even, upward, downward)
+            second[start : start + width, :] = jnp.where(even, downward, upward)
+    used = nx * ROWS_EACH
+    for ref in (first, second):
+        if ref.shape[0] > used:
+            ref[used:, :] = jnp.zeros((ref.shape[0] - used, nz), jnp.float32)
+
+
+def rows_up(v):
+    return pltpu.roll(v, v.shape[0] - 1, 0)
+
+
+def rows_down(v):
+    return pltpu.roll(v, 1, 0)
+
+
+def y_part(face, press, middle, marked, up=rows_up, down=rows_down):
+    step = jnp.where(marked, face * (up(press) - press), 0.0)
+    change = jnp.where(marked, up(middle), 0.0) - down(jnp.where(marked, middle, 0.0))
+    return (down(step) - step) + (0.5 * biot_coef) * change
 
 
 def pack_fields(*refs):
@@ -136,8 +158,8 @@
         self.keep = keeps("gy", peers[1])
 
     def read(self, f, x):
-        width, offset = WIDTHS[f], OFFSETS[f]
-        a, b = [ref[x, offset : offset + width, :] for ref in self.refs]
+        start = x * ROWS_EACH + ROW_OFFSETS[f]
+        a, b = [ref[start : start + ROW_WIDTHS[f], :] for ref in self.refs]
         low, high = jnp.where(self.even, b, a), jnp.where(self.even, a, b)
         return low * self.keep[0], high * self.keep[1]
 
@@ -156,7 +178,7 @@
     rows = Rows(first, second, peers)
     for g in range(count):
         for f in range(NF):
-            width = WIDTHS[f]
+            width = ROW_WIDTHS[f]
             slot = g * NF + f
             for p in range(pack):
                 x = g * pack + p
@@ -325,12 +347,9 @@
 
     def y_terms(self, l):
         face = self.ty[l]
-        own, middle = self.press[l], self.motion[1, l]
-        return (
-            face + self.ym(face),
-            self.back_y(face * (self.yp(own) - own))
-            + (0.5 * biot_coef) * (self.yp(middle) - self.ym(middle)),
-        )
+        marked = self.near_faces(face.shape)
+        part = y_part(face, self.press[l], self.motion[1, l], marked, self.yp, self.ym)
+        return self.y_sum(l), part
 
     def press_start(self, l):
         face_sum, y_part = self.y_terms(l)
@@ -586,42 +605,33 @@
         self.tx[l] = harmonic(own, self.nxt(self.perm, l))
         tall = self.perm_tall[l]
         face = harmonic(tall, self.yp(tall))
-        self.ty_tall[l] = face
         self.ty[l] = self.narrow(face)
+        self.face_sum[l] = self.narrow(face + self.ym(face))
         self.tz[l] = harmonic(own, self.zp(own))
 
-    def y_terms(self, l):
-        face = self.ty_tall[l]
-        own, middle = self.tall[PRESS, l], self.tall[MOTION + 1, l]
-        return (
-            self.narrow(face + self.ym(face)),
-            self.narrow(
-                self.back_y(face * (self.yp(own) - own))
-                + (0.5 * biot_coef) * (self.yp(middle) - self.ym(middle))
-            ),
-        )
-
-    def assemble(self, l, x, fields, beside, table):
+    def y_sum(self, l):
+        return self.face_sum[l]
+
+    def near_faces(self, shape):
+        row = iota(shape, 0)
+        return (row < self.ny) | (row == shape[0] - 1)
+
+    def assemble(self, l, x, fields, beside, table, keep=None):
         ny = self.ny
-        rows = ny + 2 * TILE
         gap = jnp.zeros((2 * TILE, fields.shape[3]), jnp.float32)
-        narrow_rows = ny + TILE
-        slim = (self.load, self.drain) + tuple(self.body.at[c] for c in range(3))
-        for f in range(NF):
-            width = WIDTHS[f]
-            below, above = beside.read(f, x)
-            if f < WIDE:
-                self.tall[f, l, :ny, :] = fields[f, x]
-                self.tall[f, l, ny:, :] = gap
-                self.tall[f, l, ny : ny + width, :] = above
-                self.tall[f, l, rows - width :, :] = below
-            else:
-                ref = slim[f - WIDE]
-                ref[l, :ny, :] = fields[f, x]
-                ref[l, ny:, :] = gap[:TILE]
-                ref[l, ny : ny + width, :] = above
-                ref[l, narrow_rows - width :, :] = below
-        tall_zone = self.tall[ZONE, l]
+        refs = [self.zone_tall, self.press] + [self.motion.at[c] for c in range(3)]
+        refs += [self.load, self.drain] + [self.body.at[c] for c in range(3)]
+        for f, ref in enumerate(refs):
+            width, rows = ROW_WIDTHS[f], ref.shape[1]
+            below, above = beside(f)
+            middle = fields[f, x]
+            if keep is not None:
+                below, above, middle = below * keep, above * keep, middle * keep
+            ref[l, :ny, :] = middle
+            ref[l, ny:, :] = gap[: rows - ny]
+            ref[l, ny : ny + width, :] = above
+            ref[l, rows - width :, :] = below
+        tall_zone = self.zone_tall[l]
         perm = lookup(tall_zone, table, 0)
         self.perm_tall[l] = perm
         self.perm[l] = self.narrow(perm)
@@ -631,9 +641,6 @@
         self.heft[l] = lame + shear
         self.shear[l] = shear
         self.fixed[l] = fixed_term(zone, lame, shear)
-        self.press[l] = self.narrow(self.tall[PRESS, l])
-        for c in range(3):
-            self.motion[c, l] = self.narrow(self.tall[MOTION + c, l])
 
 
 def new_brick(peers, nx, ny):
@@ -673,7 +680,7 @@
     domain = new_brick(peers, nx, ny)
     domain.__dict__.update(zip(FIRST_OUTS, outs))
     domain.__dict__.update(zip(FIRST_SCRATCH, scratch))
-    domain.tall, domain.perm_tall, domain.ty_tall = scratch[len(FIRST_SCRATCH) :]
+    domain.zone_tall, domain.perm_tall, domain.face_sum = scratch[len(FIRST_SCRATCH) :]
     domain.ps = Joined(ps)
 
     empty = jnp.zeros((ny + TILE, nz), jnp.float32)
@@ -688,23 +695,26 @@
             ps[i, l] = empty
         domain.perm_tall[l] = jnp.zeros((ny + 2 * TILE, nz), jnp.float32)
 
-    def block(start, count, shift, *source):
-        domain.loop(
-            start,
-            count,
-            lambda l: domain.assemble(l, l + shift, *source, table),
-            "assemble",
-        )
-
-    block(W, nx, -W, fields, rows[0])
+    for x in range(nx):
+        domain.assemble(W + x, x, fields, lambda f, x=x: rows[0].read(f, x), table)
     if domain.pair:
-        at = lax.axis_index("gx")
-        start = jnp.where(at > 0, 0, W + nx)
-        shift = jnp.where(at > 0, nx - W, -W - nx)
-        block(start, W, shift, below, rows[1])
+        upper = lax.axis_index("gx") > 0
+        for u in range(W):
+
+            def beside(f, u=u):
+                ending, starting = rows[1].read(f, nx - W + u), rows[1].read(f, u)
+                return [jnp.where(upper, a, b) for a, b in zip(ending, starting)]
+
+            l = jnp.where(upper, u, W + nx + u)
+            x = jnp.where(upper, nx - W + u, u)
+            domain.assemble(l, x, below, beside, table)
     else:
-        block(0, W * domain.has_below, nx - W, below, rows[1])
-        block(W + nx, W * domain.has_above, -W - nx, above, rows[2])
+        keep_below, keep_above = keeps("gx", peers[0])
+        for u in range(W):
+            x = nx - W + u
+            domain.assemble(u, x, below, lambda f, x=x: rows[1].read(f, x), table, keep_below)
+            l = W + nx + u
+            domain.assemble(l, u, above, lambda f, u=u: rows[2].read(f, u), table, keep_above)
     domain.first_half()
 
 
@@ -765,6 +775,14 @@
 
     def zm(self, v):
         return pltpu.roll(v, 1, 1)
+
+    def y_sum(self, l):
+        face = self.ty[l]
+        return face + self.ym(face)
+
+    def near_faces(self, shape):
+        row = iota(shape, len(shape) - 1) % self.row
+        return (row >= TILE - 1) & (row < self.row - TILE)
 
     def own(self, v):
         return v
@@ -1047,7 +1065,7 @@
         pltpu.with_memory_space_constraint(a, pltpu.HBM)
         for a in (perm_table, lame_table, shear_table)
     ]
-    message = f32(nx, MSG_ROWS, nz)
+    message = f32(up_to(nx * ROWS_EACH, TILE), nz)
     first, second, table = call(
         pack_rows,
         [message, message, f32(TILE, LANES)],
@@ -1129,7 +1147,7 @@
         first_above,
         second_above,
         scratch=[vmem(*layers_of(name)) for name in FIRST_SCRATCH]
-        + [vmem(WIDE, depth, tall, nz), vmem(depth, tall, nz), vmem(depth, tall, nz)],
+        + [vmem(depth, tall, nz), vmem(depth, tall, nz), vmem(depth, ny + TILE, nz)],
         limit=16,
     )
     half = dict(zip(FIRST_OUTS, halves))

time: 42.5 us -> 41.8 us (0.984)
  waiting for transfers between devices: 8.87 us -> 8.31 us
    ppermute x2, waiting for transfers between devices: 4.13 us -> 3.6 us  [pairs(): return lax.ppermute(value, axis, swaps)]
where the time goes in v5:
time: 41.8 us; the launch traced here: 41.6 us
  blocking collectives  14.2 us (34%)
  Pallas kernels  12.3 us (29%)
  waiting for transfers between devices  8.31 us (20%)
  starting transfers between devices  6.08 us (15%)
  between operations  0.7 us (2%)
    all_to_all x1, blocking collectives, shards(): sums = lax.all_to_all(partial, AXES, 0, 0, tiled=True)  14.2 us
    pallas_call x8, Pallas kernels, call(): pl.pallas_call(kernel, out_shape=outs, in_specs=specs, scratch_shapes=scr...  12.3 us
    ppermute x1, waiting for transfers between devices, shards(): got = lax.ppermute(messages[0], ('gx', 'gz'), hops)  4.13 us
    ppermute x2, waiting for transfers between devices, pairs(): return lax.ppermute(value, axis, swaps)  3.6 us
    ppermute x2, starting transfers between devices, pairs(): return lax.ppermute(value, axis, swaps)  3.3 us
    ppermute x1, starting transfers between devices, shards(): got = lax.ppermute(messages[0], ('gx', 'gz'), hops)  1.71 us
    ppermute x4, starting transfers between devices, ring(): lax.ppermute(value, axis, [(i, (i + step) % peers) for i in range(peers)])  1.07 us
  transfers between devices with their start and end apart: 7, of which 4 were waited for; matrix products, arithmetic and copies ran while one was open for 0% of the time, Pallas kernels for 13%

profile of v5, /device:TPU:0, one launch (start us, length us, event | category | flops | bytes accessed | tf_op | source)
XLA Modules:
  0.0 41.6 jit_solution(3057595917815568456)
XLA Ops:
  0.6 1.3 %shard_map.121 = (f32[272,128]{1,0:T(8,128)S(1)}, f32[272,128]{1,0:T(8,128)S(1)}, f32[8,128]{1,0:T(8,128)S(1)}) custom-call(f32[8,16,128]{2,1,0:T(8,128)} %refs_0_.3, f32[8,16,128]{2,1,0:T(8,128)} %refs_1_.3, f32[8,16,128]{2,1,0:T(8,128)} %refs_2_.3, f32[3,8,16,128]{3,2,1,0:T(8,128)} %refs_3_.3, f32[3,8,16,128]{3,2,1,0:T(8,128)} %refs_4_.3, ...), custom_call_target="tpu_custom_call" | custom-call | tf_op jit(solution)/shard_map/pallas_call | solution.py:1000
  1.9 1.3 %shard_map.122.refs_0_.refs_1_.refs_7_ = f32[10,8,16,128]{3,2,1,0:T(8,128)S(1)} custom-call(f32[8,16,128]{2,1,0:T(8,128)} %refs_0_.3, f32[8,16,128]{2,1,0:T(8,128)} %refs_1_.3, f32[8,16,128]{2,1,0:T(8,128)} %refs_2_.3, f32[3,8,16,128]{3,2,1,0:T(8,128)} %refs_3_.3, f32[3,8,16,128]{3,2,1,0:T(8,128)} %refs_4_.3, s32[8,16,128]{2,1,0:T(8,128)} %refs_5_.3, ...), custom_call_target="tpu_custom_call" | custom-call | tf_op jit(solution)/shard_map/pallas_call | solution.py:1000
  3.2 0.6 %collective-permute-start.2 = (f32[10,8,16,128]{3,2,1,0:T(8,128)S(1)}, f32[10,8,16,128]{3,2,1,0:T(8,128)S(1)}, u32[]{:S(2)}, u32[]{:S(2)}) collective-permute-start(f32[10,8,16,128]{3,2,1,0:T(8,128)S(1)} %shard_map.122.refs_0_.refs_1_.refs_7_), channel_id=1, source_target_pairs={{0,16},{16,0},{1,17},{17,1},{2,18},{18,2},{3,19},{19,3},{4,20},{20... | collective-permute-start | bytes 1966088 | tf_op jit(solution)/shard_map/ppermute | solution.py:1012
  3.8 2.6 %collective-permute-start = (f32[272,128]{1,0:T(8,128)S(1)}, f32[272,128]{1,0:T(8,128)S(1)}, u32[]{:S(2)}, u32[]{:S(2)}) collective-permute-start(f32[272,128]{1,0:T(8,128)S(1)} %get-tuple-element.35), channel_id=1, source_target_pairs={{0,4},{4,0},{8,12},{12,8},{1,5},{5,1},{9,13},{13,9},{2,6},{6,2},{1... | collective-permute-start | bytes 417800 | tf_op jit(solution)/shard_map/ppermute | solution.py:1021
  6.4 0.7 %collective-permute-start.1 = (f32[272,128]{1,0:T(8,128)S(1)}, f32[272,128]{1,0:T(8,128)S(1)}, u32[]{:S(2)}, u32[]{:S(2)}) collective-permute-start(f32[272,128]{1,0:T(8,128)S(1)} %get-tuple-element.36), channel_id=1, source_target_pairs={{0,0},{4,8},{8,4},{12,12},{1,1},{5,9},{9,5},{13,13},{2,2},{6,10},{... | collective-permute-start | bytes 417800 | tf_op jit(solution)/shard_map/ppermute | solution.py:1021
  7.1 3.6 %collective-permute-done.refs_1_.refs_4_ = f32[272,128]{1,0:T(8,128)S(1)} collective-permute-done((f32[272,128]{1,0:T(8,128)S(1)}, f32[272,128]{1,0:T(8,128)S(1)}, u32[]{:S(2)}, u32[]{:S(2)}) %collective-permute-start) | collective-permute-done | bytes 139296 | tf_op jit(solution)/shard_map/ppermute | solution.py:1021
  10.7 0.0 collective-permute-start.3
  10.7 0.0 collective-permute-done.1.refs_2_.refs_5_
  10.7 0.5 %collective-permute-start.4 = (f32[272,128]{1,0:T(8,128)S(1)}, f32[272,128]{1,0:T(8,128)S(1)}, u32[]{:S(2)}, u32[]{:S(2)}) collective-permute-start(f32[272,128]{1,0:T(8,128)S(1)} %collective-permute-done.1.refs_2_.refs_5_), channel_id=1, source_target_pairs={{0,16},{16,0},{1,17},{17,1},{2,18},{18,2},{3,19},{19,3},{4,20},{20... | collective-permute-start | bytes 417800 | tf_op jit(solution)/shard_map/ppermute | solution.py:1012
  11.2 0.5 %shard_map.123 = (f32[10,2,32,128]{3,2,1,0:T(8,128)S(1)}, f32[2,40,128]{2,1,0:T(8,128)S(1)}) custom-call(f32[10,8,16,128]{3,2,1,0:T(8,128)S(1)} %shard_map.122.refs_0_.refs_1_.refs_7_, f32[272,128]{1,0:T(8,128)S(1)} %collective-permute-done.refs_1_.refs_4_, f32[272,128]{1,0:T(8,128)S(1)} %collective-permute-done.1.refs_2_.refs_5_), custom_call_target="tpu_custom_call" | custom-call | tf_op jit(solution)/shard_map/pallas_call | solution.py:1000
  11.7 0.4 collective-permute-done.3.refs_3_.refs_6_.refs_8_
  12.0 0.2 collective-permute-done.4.refs_4_.refs_7_.refs_9_
  12.2 0.0 collective-permute-done.2.refs_2_.refs_3_
  12.2 0.5 %shard_map.124 = (f32[10,4,32,128]{3,2,1,0:T(8,128)S(1)}, f32[4,40,128]{2,1,0:T(8,128)S(1)}) custom-call(f32[10,2,32,128]{3,2,1,0:T(8,128)S(1)} %get-tuple-element.37.refs_0_, f32[2,40,128]{2,1,0:T(8,128)S(1)} %get-tuple-element.38.refs_1_, f32[10,8,16,128]{3,2,1,0:T(8,128)S(1)} %collective-permute-done.2.refs_2_.refs_3_, ...), custom_call_target="tpu_custom_call" | custom-call | tf_op jit(solution)/shard_map/pallas_call | solution.py:1000
  12.7 1.7 %collective-permute-start.5 = (f32[4,40,128]{2,1,0:T(8,128)S(1)}, f32[4,40,128]{2,1,0:T(8,128)S(1)}, u32[]{:S(2)}, u32[]{:S(2)}) collective-permute-start(f32[4,40,128]{2,1,0:T(8,128)S(1)} %get-tuple-element.40), channel_id=1, source_target_pairs={{0,1},{1,2},{2,3},{3,0},{16,19},{17,16},{18,17},{19,18},{4,5},{5,6... | collective-permute-start | bytes 245768 | tf_op jit(solution)/shard_map/ppermute | solution.py:1120
  14.4 4.1 %collective-permute-done.5.refs_2_ = f32[4,40,128]{2,1,0:T(8,128)S(1)} collective-permute-done((f32[4,40,128]{2,1,0:T(8,128)S(1)}, f32[4,40,128]{2,1,0:T(8,128)S(1)}, u32[]{:S(2)}, u32[]{:S(2)}) %collective-permute-start.5) | collective-permute-done | bytes 81952 | tf_op jit(solution)/shard_map/ppermute | solution.py:1120
  18.6 0.0 collective-permute-start.6
  18.6 3.5 %shard_map.125 = (f32[3,18,24,128]{3,2,1,0:T(8,128)S(1)}, f32[18,24,128]{2,1,0:T(8,128)S(1)}, f32[18,24,128]{2,1,0:T(8,128)S(1)}, f32[9,18,24,128]{3,2,1,0:T(8,1...) custom-call(f32[8,128]{1,0:T(8,128)S(1)} %get-tuple-element.34.refs_, ...), custom_call_target="tpu_custom_call" | custom-call | tf_op jit(solution)/shard_map/pallas_call | solution.py:1000
  22.0 1.5 %shard_map.126 = (f32[3,18,24,128]{3,2,1,0:T(8,128)S(1)}, f32[32,8,128]{2,1,0:T(8,128)S(1)}) custom-call(f32[18,24,128]{2,1,0:T(8,128)S(1)} %get-tuple-element.41.refs_0_.refs_2_, f32[18,24,128]{2,1,0:T(8,128)S(1)} %get-tuple-element.42.refs_1_.refs_3_, f32[9,18,24,128]{3,2,1,0:T(8,128)S(1)} %get-tuple-element.43.refs_2_.refs_4_, ...), custom_call_target="tpu_custom_call" | custom-call | tf_op jit(solution)/shard_map/pallas_call | solution.py:1000
  23.5 0.0 collective-permute-done.6.refs_3_
  23.5 2.6 %shard_map.127 = (f32[10,5,32,128]{3,2,1,0:T(8,128)S(1)}, f32[5,32,128]{2,1,0:T(8,128)S(1)}, f32[5,32,128]{2,1,0:T(8,128)S(1)}, f32[9,5,32,128]{3,2,1,0:T(8,128)...) custom-call(f32[8,128]{1,0:T(8,128)S(1)} %get-tuple-element.34.refs_7_.refs_0_, ...), custom_call_target="tpu_custom_call" | custom-call | tf_op jit(solution)/shard_map/pallas_call | solution.py:1000
  26.1 14.2 %all_to_all.11 = f32[32,1,128]{2,1,0:T(1,128)S(1)} all-to-all(f32[32,1,128]{2,1,0:T(1,128)S(1)} %bitcast.5), channel_id=1, replica_groups=mesh['gx'=2,'gy'=4,'gz'=4] {'gx','gy','gz'}, dimensions={0} | all-to-all | bytes 32768 | tf_op jit(solution)/shard_map/all_to_all | solution.py:1182
  40.4 1.2 %shard_map.128 = (f32[8,16,128]{2,1,0:T(8,128)}, f32[3,8,16,128]{3,2,1,0:T(8,128)}, f32[8,16,128]{2,1,0:T(8,128)}) custom-call(f32[32,128]{1,0:T(8,128)S(1)} %bitcast.4, f32[3,18,24,128]{3,2,1,0:T(8,128)S(1)} %get-tuple-element.58.refs_1_, f32[18,24,128]{2,1,0:T(8,128)S(1)} %get-tuple-element.41.refs_0_.refs_2_, ...), custom_call_target="tpu_custom_call" | custom-call | tf_op jit(solution)/shard_map/pallas_call | solution.py:1000
Async XLA Ops:
  3.2 9.0 %collective-permute-start.2 = (f32[10,8,16,128]{3,2,1,0:T(8,128)S(1)}, f32[10,8,16,128]{3,2,1,0:T(8,128)S(1)}, u32[]{:S(2)}, u32[]{:S(2)}) collective-permute-start(f32[10,8,16,128]{3,2,1,0:T(8,128)S(1)} %shard_map.122.refs_0_.refs_1_.refs_7_), channel_id=1, source_target_pairs={{0,16},{16,0},{1,17},{17,1},{2,18},{18,2},{3,19},{19,3},{4,20},{20... | collective-permute-start | bytes 1966088 | tf_op jit(solution)/shard_map/ppermute | solution.py:1012
  3.8 6.9 %collective-permute-start = (f32[272,128]{1,0:T(8,128)S(1)}, f32[272,128]{1,0:T(8,128)S(1)}, u32[]{:S(2)}, u32[]{:S(2)}) collective-permute-start(f32[272,128]{1,0:T(8,128)S(1)} %get-tuple-element.35), channel_id=1, source_target_pairs={{0,4},{4,0},{8,12},{12,8},{1,5},{5,1},{9,13},{13,9},{2,6},{6,2},{1... | collective-permute-start | bytes 417800 | tf_op jit(solution)/shard_map/ppermute | solution.py:1021
  6.4 4.3 %collective-permute-start.1 = (f32[272,128]{1,0:T(8,128)S(1)}, f32[272,128]{1,0:T(8,128)S(1)}, u32[]{:S(2)}, u32[]{:S(2)}) collective-permute-start(f32[272,128]{1,0:T(8,128)S(1)} %get-tuple-element.36), channel_id=1, source_target_pairs={{0,0},{4,8},{8,4},{12,12},{1,1},{5,9},{9,5},{13,13},{2,2},{6,10},{... | collective-permute-start | bytes 417800 | tf_op jit(solution)/shard_map/ppermute | solution.py:1021
  10.7 1.4 %collective-permute-start.3 = (f32[272,128]{1,0:T(8,128)S(1)}, f32[272,128]{1,0:T(8,128)S(1)}, u32[]{:S(2)}, u32[]{:S(2)}) collective-permute-start(f32[272,128]{1,0:T(8,128)S(1)} %collective-permute-done.refs_1_.refs_4_), channel_id=1, source_target_pairs={{0,16},{16,0},{1,17},{17,1},{2,18},{18,2},{3,19},{19,3},{4,20},{20... | collective-permute-start | bytes 417800 | tf_op jit(solution)/shard_map/ppermute | solution.py:1012
  10.7 1.6 %collective-permute-start.4 = (f32[272,128]{1,0:T(8,128)S(1)}, f32[272,128]{1,0:T(8,128)S(1)}, u32[]{:S(2)}, u32[]{:S(2)}) collective-permute-start(f32[272,128]{1,0:T(8,128)S(1)} %collective-permute-done.1.refs_2_.refs_5_), channel_id=1, source_target_pairs={{0,16},{16,0},{1,17},{17,1},{2,18},{18,2},{3,19},{19,3},{4,20},{20... | collective-permute-start | bytes 417800 | tf_op jit(solution)/shard_map/ppermute | solution.py:1012
  12.7 5.8 %collective-permute-start.5 = (f32[4,40,128]{2,1,0:T(8,128)S(1)}, f32[4,40,128]{2,1,0:T(8,128)S(1)}, u32[]{:S(2)}, u32[]{:S(2)}) collective-permute-start(f32[4,40,128]{2,1,0:T(8,128)S(1)} %get-tuple-element.40), channel_id=1, source_target_pairs={{0,1},{1,2},{2,3},{3,0},{16,19},{17,16},{18,17},{19,18},{4,5},{5,6... | collective-permute-start | bytes 245768 | tf_op jit(solution)/shard_map/ppermute | solution.py:1120
  18.6 5.0 %collective-permute-start.6 = (f32[4,40,128]{2,1,0:T(8,128)S(1)}, f32[4,40,128]{2,1,0:T(8,128)S(1)}, u32[]{:S(2)}, u32[]{:S(2)}) collective-permute-start(f32[4,40,128]{2,1,0:T(8,128)S(1)} %collective-permute-done.5.refs_2_), channel_id=1, source_target_pairs={{0,16},{16,0},{1,17},{17,1},{2,18},{18,2},{3,19},{19,3},{4,20},{20... | collective-permute-start | bytes 245768 | tf_op jit(solution)/shard_map/ppermute | solution.py:1012

commit v6 on v5

--- a/solution.py
+++ b/solution.py
@@ -30,7 +30,7 @@
 SUMS = 4 + 4 * len(PAIRS)
 SEG = 16
 ENDS = 2 * SEG
-UNROLL = dict(faces=8, start=8, next=8, shear=8, motion=8, image=8, finish=8)
+UNROLL = dict(faces=8, start=8, next=8, shear=8, motion=8, image=3, finish=8)
 
 
 def up_to(value, multiple):
@@ -282,7 +282,7 @@
     return jnp.where(zone > 0.0, biot_coef * biot_coef / scale, 0.0)
 
 
-FIRST_IMAGES, SECOND_IMAGES = (0, 1), (2,)
+FIRST_IMAGES, SECOND_IMAGES = (0, 1, 2), ()
 KEPT = ("motion", "z0", "p0", "zs", "ps")
 PASSED = ("heft", "mx", "my", "mz", "react", "tx", "ty", "tz", "pdiag", "ediag", "einv")
 ARRAYS = (
@@ -342,7 +342,11 @@
 
     def press_flux(self, ref, l, along_y=True):
         dx, dy, dz = self.steps(ref, l)
-        total = self.back_x(self.tx, dx, ref, l) + self.back_z(self.tz[l] * dz)
+        (part,) = self.back_x(
+            [self.tx[l] * dx],
+            lambda: [self.tx[l - 1] * (ref[l] - ref[l - 1])],
+        )
+        total = part + self.back_z(self.tz[l] * dz)
         return total + self.back_y(self.ty[l] * dy) if along_y else total
 
     def y_terms(self, l):
@@ -391,31 +395,39 @@
     def elastic(self, refs, l):
         steps = [self.steps(ref, l) for ref in refs]
         pushed = self.heft[l] * (steps[0][0] + steps[1][1] + steps[2][2])
-        before = self.push_before(refs, l)
-        self.carried = pushed
+        face = self.mx[l]
+        along_x = [face * steps[c][0] for c in range(3)]
+        along_x[0] = along_x[0] + pushed
+        parts_x = self.back_x(along_x, lambda: self.motion_fluxes(refs, l - 1))
         out = []
         for c in range(3):
-            dx, dy, dz = steps[c]
+            _, dy, dz = steps[c]
             step_y, step_z = self.my[l] * dy, self.mz[l] * dz
             if c == 1:
                 step_y = step_y + pushed
             if c == 2:
                 step_z = step_z + pushed
-            push = (before, pushed) if c == 0 else None
             out.append(
                 times(refs[c][l], support)
-                + self.back_x(self.mx, dx, refs[c], l, push)
+                + parts_x[c]
                 + self.back_y(step_y)
                 + self.back_z(step_z)
             )
         return out
 
+    def motion_fluxes(self, refs, l):
+        a, b, c = [ref[l] for ref in refs]
+        steps = [self.nxt(ref, l) - own for ref, own in zip(refs, (a, b, c))]
+        face = self.mx[l]
+        pushed = self.heft[l] * (steps[0] + (self.yp(b) - b) + (self.zp(c) - c))
+        return [face * steps[0] + pushed, face * steps[1], face * steps[2]]
+
     def gradient(self, ref, l):
         own = ref[l]
         return (
-            0.5 * (self.nxt(ref, l) - self.prv(ref, l)),
-            0.5 * (self.yp(own) - self.ym(own)),
-            0.5 * (self.zp(own) - self.zm(own)),
+            self.nxt(ref, l) - self.prv(ref, l),
+            self.yp(own) - self.ym(own),
+            self.zp(own) - self.zm(own),
         )
 
     def motion_start(self, l):
@@ -438,9 +450,9 @@
             inverse = jnp.where(inside, 1.0 / diag, 0.0)
             self.ediag[c, l] = diag
             self.einv[c, l] = inverse
-            start = self.body[c, l] - biot_coef * grads[0][c] - image[c]
+            start = self.body[c, l] - (0.5 * biot_coef) * grads[0][c] - image[c]
             self.zs[c, l] = start * inverse
-            scale = -biot_coef * inverse
+            scale = (-0.5 * biot_coef) * inverse
             self.zs[3 + c, l] = grads[1][c] * scale
             self.zs[6 + c, l] = grads[2][c] * scale
 
@@ -555,19 +567,10 @@
     def zm(self, v):
         return pltpu.roll(v, 1, 1)
 
-    def back_x(self, faces, step, ref, l, push=None):
-        out = faces[l - 1] * (ref[l] - ref[l - 1]) - faces[l] * step
-        if push:
-            out = out + (push[0] - push[1])
-        return out
-
-    def push_before(self, refs, l):
-        if self.carried is not None:
-            return self.carried
-        a, b, c = refs
-        own_b, own_c = b[l - 1], c[l - 1]
-        change = (a[l] - a[l - 1]) + (self.yp(own_b) - own_b) + (self.zp(own_c) - own_c)
-        return self.heft[l - 1] * change
+    def back_x(self, values, again):
+        before = again() if self.carried is None else self.carried
+        self.carried = values
+        return [a - b for a, b in zip(before, values)]
 
     def own(self, v):
         return v[: self.ny]
@@ -576,9 +579,12 @@
         total = value[:TILE]
         for start in range(TILE, value.shape[0], TILE):
             total = total + value[start : start + TILE]
-        total = jnp.where(mask, total, 0.0)
+        nz = value.shape[1]
+        if nz > LANES:
+            column = iota(total.shape, 1)
+            total = jnp.where((column >= W) & (column < nz - W), total, 0.0)
         folded = total[:, :LANES]
-        for start in range(LANES, value.shape[1], LANES):
+        for start in range(LANES, nz, LANES):
             folded = folded + total[:, start : start + LANES]
         return folded
 
@@ -724,18 +730,22 @@
 def brick_second(peers, nx, ny, *refs):
     domain = new_brick(peers, nx, ny)
     domain.__dict__.update(zip(SECOND_INS, refs))
-    ready, ps, acc = refs[len(SECOND_INS) :]
-    domain.ps = Joined(ready, ps)
-    nz = ps.shape[3]
+    ready, *made, acc = refs[len(SECOND_INS) :]
+    domain.ps = Joined(ready, *made)
+    nz = ready.shape[3]
     empty = jnp.zeros((ny + TILE, nz), jnp.float32)
-    for l in (W - 1, W + nx):
-        for i in range(ps.shape[0]):
-            ps[i, l] = empty
+    for ps in made:
+        for l in (W - 1, W + nx):
+            for i in range(ps.shape[0]):
+                ps[i, l] = empty
     domain.second_half()
     acc[...] = jnp.zeros(acc.shape, jnp.float32)
-    column = iota((TILE, nz), 1)
-    mask = (column >= W) & (column < nz - W)
-    domain.loop(W, nx, lambda l: domain.finish(l, acc, mask), "finish")
+    domain.loop(W, nx, lambda l: domain.finish(l, acc, None), "finish")
+    if nz == LANES:
+        column = iota((TILE, LANES), 1)
+        mask = (column >= W) & (column < nz - W)
+        for i in range(SUMS):
+            acc[i] = jnp.where(mask, acc[i], 0.0)
 
 
 class Ends(Domain):
@@ -755,14 +765,8 @@
     def prv(self, ref, l):
         return self.before(ref[l])
 
-    def back_x(self, faces, step, ref, l, push=None):
-        value = faces[l] * step
-        if push:
-            value = value + push[1]
-        return self.before(value) - value
-
-    def push_before(self, refs, l):
-        return None
+    def back_x(self, values, again):
+        return [self.before(value) - value for value in values]
 
     def yp(self, v):
         return self.roll(v, -1)
@@ -891,9 +895,10 @@
 
 
 def combine(peers, tall, *refs):
-    sums, (old, z0, p0, zs), ps, fields = refs[0], refs[1:5], Joined(*refs[5:7]), refs[7]
-    raw, ends_z0, ends_p0, ends_zs, ends_ps = refs[8:13]
-    pressure, motion, strain, moved, ends_moved, turned = refs[13:]
+    sums, (old, z0, p0, zs) = refs[0], refs[1:5]
+    *ps, fields, raw, ends_z0, ends_p0, ends_zs, ends_ps = refs[5:-6]
+    ps = Joined(*ps)
+    pressure, motion, strain, moved, ends_moved, turned = refs[-6:]
     line = jnp.sum(sums[...], axis=0, keepdims=True)
     lane = iota(line.shape, 1)
 
@@ -1153,13 +1158,14 @@
     half = dict(zip(FIRST_OUTS, halves))
     if pair:
         passed = ring(got, "gx", -1)
-    last, added = call(
+    late = [f32(3 * len(SECOND_IMAGES), depth, ny + TILE, nz)] * bool(SECOND_IMAGES)
+    *last, added = call(
         with_peers(brick_second, nx, ny),
-        [f32(3 * len(SECOND_IMAGES), depth, ny + TILE, nz), f32(*sums_shape)],
+        late + [f32(*sums_shape)],
         *[half[name] for name in SECOND_INS],
         ps,
     )
-    kept = [half[name] for name in KEPT[:-1]] + [ps, last]
+    kept = [half[name] for name in KEPT[:-1]] + [ps, *last]
     span = span + 1
     *ends_kept, partial = call(
         with_peers(ends_kernel, tall),

time: 41.8 us -> 41.8 us (level)
  no operation moved by 1% of the time
where the time goes in v6:
time: 41.8 us; the launch traced here: 41.6 us
  blocking collectives  14.2 us (34%)
  Pallas kernels  12.2 us (29%)
  waiting for transfers between devices  8.32 us (20%)
  starting transfers between devices  6.08 us (15%)
  between operations  0.7 us (2%)
    all_to_all x1, blocking collectives, shards(): sums = lax.all_to_all(partial, AXES, 0, 0, tiled=True)  14.2 us
    pallas_call x8, Pallas kernels, call(): pl.pallas_call(kernel, out_shape=outs, in_specs=specs, scratch_shapes=scr...  12.2 us
    ppermute x1, waiting for transfers between devices, shards(): got = lax.ppermute(messages[0], ('gx', 'gz'), hops)  4.13 us
    ppermute x2, waiting for transfers between devices, pairs(): return lax.ppermute(value, axis, swaps)  3.6 us
    ppermute x2, starting transfers between devices, pairs(): return lax.ppermute(value, axis, swaps)  3.3 us
    ppermute x1, starting transfers between devices, shards(): got = lax.ppermute(messages[0], ('gx', 'gz'), hops)  1.71 us
    ppermute x4, starting transfers between devices, ring(): lax.ppermute(value, axis, [(i, (i + step) % peers) for i in range(peers)])  1.07 us
  transfers between devices with their start and end apart: 7, of which 4 were waited for; matrix products, arithmetic and copies ran while one was open for 0% of the time, Pallas kernels for 13%

profile of v6, /device:TPU:0, one launch (start us, length us, event | category | flops | bytes accessed | tf_op | source)
XLA Modules:
  0.0 41.6 jit_solution(17959247672825778856)
XLA Ops:
  0.6 1.3 %shard_map.121 = (f32[272,128]{1,0:T(8,128)S(1)}, f32[272,128]{1,0:T(8,128)S(1)}, f32[8,128]{1,0:T(8,128)S(1)}) custom-call(f32[8,16,128]{2,1,0:T(8,128)} %refs_0_.3, f32[8,16,128]{2,1,0:T(8,128)} %refs_1_.3, f32[8,16,128]{2,1,0:T(8,128)} %refs_2_.3, f32[3,8,16,128]{3,2,1,0:T(8,128)} %refs_3_.3, f32[3,8,16,128]{3,2,1,0:T(8,128)} %refs_4_.3, ...), custom_call_target="tpu_custom_call" | custom-call | tf_op jit(solution)/shard_map/pallas_call | solution.py:1005
  1.9 1.3 %shard_map.122.refs_0_.refs_1_.refs_6_ = f32[10,8,16,128]{3,2,1,0:T(8,128)S(1)} custom-call(f32[8,16,128]{2,1,0:T(8,128)} %refs_0_.3, f32[8,16,128]{2,1,0:T(8,128)} %refs_1_.3, f32[8,16,128]{2,1,0:T(8,128)} %refs_2_.3, f32[3,8,16,128]{3,2,1,0:T(8,128)} %refs_3_.3, f32[3,8,16,128]{3,2,1,0:T(8,128)} %refs_4_.3, s32[8,16,128]{2,1,0:T(8,128)} %refs_5_.3, ...), custom_call_target="tpu_custom_call" | custom-call | tf_op jit(solution)/shard_map/pallas_call | solution.py:1005
  3.2 0.6 %collective-permute-start.2 = (f32[10,8,16,128]{3,2,1,0:T(8,128)S(1)}, f32[10,8,16,128]{3,2,1,0:T(8,128)S(1)}, u32[]{:S(2)}, u32[]{:S(2)}) collective-permute-start(f32[10,8,16,128]{3,2,1,0:T(8,128)S(1)} %shard_map.122.refs_0_.refs_1_.refs_6_), channel_id=1, source_target_pairs={{0,16},{16,0},{1,17},{17,1},{2,18},{18,2},{3,19},{19,3},{4,20},{20... | collective-permute-start | bytes 1966088 | tf_op jit(solution)/shard_map/ppermute | solution.py:1017
  3.8 2.6 %collective-permute-start = (f32[272,128]{1,0:T(8,128)S(1)}, f32[272,128]{1,0:T(8,128)S(1)}, u32[]{:S(2)}, u32[]{:S(2)}) collective-permute-start(f32[272,128]{1,0:T(8,128)S(1)} %get-tuple-element.33), channel_id=1, source_target_pairs={{0,4},{4,0},{8,12},{12,8},{1,5},{5,1},{9,13},{13,9},{2,6},{6,2},{1... | collective-permute-start | bytes 417800 | tf_op jit(solution)/shard_map/ppermute | solution.py:1026
  6.4 0.7 %collective-permute-start.1 = (f32[272,128]{1,0:T(8,128)S(1)}, f32[272,128]{1,0:T(8,128)S(1)}, u32[]{:S(2)}, u32[]{:S(2)}) collective-permute-start(f32[272,128]{1,0:T(8,128)S(1)} %get-tuple-element.34), channel_id=1, source_target_pairs={{0,0},{4,8},{8,4},{12,12},{1,1},{5,9},{9,5},{13,13},{2,2},{6,10},{... | collective-permute-start | bytes 417800 | tf_op jit(solution)/shard_map/ppermute | solution.py:1026
  7.1 3.6 %collective-permute-done.refs_1_.refs_4_ = f32[272,128]{1,0:T(8,128)S(1)} collective-permute-done((f32[272,128]{1,0:T(8,128)S(1)}, f32[272,128]{1,0:T(8,128)S(1)}, u32[]{:S(2)}, u32[]{:S(2)}) %collective-permute-start) | collective-permute-done | bytes 139296 | tf_op jit(solution)/shard_map/ppermute | solution.py:1026
  10.7 0.0 collective-permute-start.3
  10.7 0.0 collective-permute-done.1.refs_2_.refs_5_
  10.7 0.5 %collective-permute-start.4 = (f32[272,128]{1,0:T(8,128)S(1)}, f32[272,128]{1,0:T(8,128)S(1)}, u32[]{:S(2)}, u32[]{:S(2)}) collective-permute-start(f32[272,128]{1,0:T(8,128)S(1)} %collective-permute-done.1.refs_2_.refs_5_), channel_id=1, source_target_pairs={{0,16},{16,0},{1,17},{17,1},{2,18},{18,2},{3,19},{19,3},{4,20},{20... | collective-permute-start | bytes 417800 | tf_op jit(solution)/shard_map/ppermute | solution.py:1017
  11.2 0.5 %shard_map.123 = (f32[10,2,32,128]{3,2,1,0:T(8,128)S(1)}, f32[2,40,128]{2,1,0:T(8,128)S(1)}) custom-call(f32[10,8,16,128]{3,2,1,0:T(8,128)S(1)} %shard_map.122.refs_0_.refs_1_.refs_6_, f32[272,128]{1,0:T(8,128)S(1)} %collective-permute-done.refs_1_.refs_4_, f32[272,128]{1,0:T(8,128)S(1)} %collective-permute-done.1.refs_2_.refs_5_), custom_call_target="tpu_custom_call" | custom-call | tf_op jit(solution)/shard_map/pallas_call | solution.py:1005
  11.7 0.4 collective-permute-done.3.refs_3_.refs_6_.refs_8_
  12.0 0.2 collective-permute-done.4.refs_4_.refs_7_.refs_9_
  12.2 0.0 collective-permute-done.2.refs_2_.refs_3_
  12.2 0.5 %shard_map.124 = (f32[10,4,32,128]{3,2,1,0:T(8,128)S(1)}, f32[4,40,128]{2,1,0:T(8,128)S(1)}) custom-call(f32[10,2,32,128]{3,2,1,0:T(8,128)S(1)} %get-tuple-element.35.refs_0_, f32[2,40,128]{2,1,0:T(8,128)S(1)} %get-tuple-element.36.refs_1_, f32[10,8,16,128]{3,2,1,0:T(8,128)S(1)} %collective-permute-done.2.refs_2_.refs_3_, ...), custom_call_target="tpu_custom_call" | custom-call | tf_op jit(solution)/shard_map/pallas_call | solution.py:1005
  12.7 1.7 %collective-permute-start.5 = (f32[4,40,128]{2,1,0:T(8,128)S(1)}, f32[4,40,128]{2,1,0:T(8,128)S(1)}, u32[]{:S(2)}, u32[]{:S(2)}) collective-permute-start(f32[4,40,128]{2,1,0:T(8,128)S(1)} %get-tuple-element.38), channel_id=1, source_target_pairs={{0,1},{1,2},{2,3},{3,0},{16,19},{17,16},{18,17},{19,18},{4,5},{5,6... | collective-permute-start | bytes 245768 | tf_op jit(solution)/shard_map/ppermute | solution.py:1125
  14.4 4.1 %collective-permute-done.5.refs_2_ = f32[4,40,128]{2,1,0:T(8,128)S(1)} collective-permute-done((f32[4,40,128]{2,1,0:T(8,128)S(1)}, f32[4,40,128]{2,1,0:T(8,128)S(1)}, u32[]{:S(2)}, u32[]{:S(2)}) %collective-permute-start.5) | collective-permute-done | bytes 81952 | tf_op jit(solution)/shard_map/ppermute | solution.py:1125
  18.6 0.0 collective-permute-start.6
  18.6 3.9 %shard_map.125 = (f32[3,18,24,128]{3,2,1,0:T(8,128)S(1)}, f32[18,24,128]{2,1,0:T(8,128)S(1)}, f32[18,24,128]{2,1,0:T(8,128)S(1)}, f32[9,18,24,128]{3,2,1,0:T(8,1...) custom-call(f32[8,128]{1,0:T(8,128)S(1)} %get-tuple-element.32.refs_, ...), custom_call_target="tpu_custom_call" | custom-call | tf_op jit(solution)/shard_map/pallas_call | solution.py:1005
  22.5 1.0 %shard_map.126.refs_4_ = f32[32,8,128]{2,1,0:T(8,128)S(1)} custom-call(f32[18,24,128]{2,1,0:T(8,128)S(1)} %get-tuple-element.39.refs_0_.refs_2_, f32[18,24,128]{2,1,0:T(8,128)S(1)} %get-tuple-element.40.refs_1_.refs_3_, f32[9,18,24,128]{3,2,1,0:T(8,128)S(1)} %get-tuple-element.41.refs_2_.refs_4_, f32[18,24,128]{2,1,0:T(8,128)S(1)} %get-tuple-element.42.refs_3_, ...), custom_call_target="tpu_custom_call" | custom-call | tf_op jit(solution)/shard_map/pallas_call | solution.py:1005
  23.5 0.0 collective-permute-done.6.refs_3_
  23.5 2.6 %shard_map.127 = (f32[10,5,32,128]{3,2,1,0:T(8,128)S(1)}, f32[5,32,128]{2,1,0:T(8,128)S(1)}, f32[5,32,128]{2,1,0:T(8,128)S(1)}, f32[9,5,32,128]{3,2,1,0:T(8,128)...) custom-call(f32[8,128]{1,0:T(8,128)S(1)} %get-tuple-element.32.refs_7_.refs_0_, ...), custom_call_target="tpu_custom_call" | custom-call | tf_op jit(solution)/shard_map/pallas_call | solution.py:1005
  26.1 14.2 %all_to_all.11 = f32[32,1,128]{2,1,0:T(1,128)S(1)} all-to-all(f32[32,1,128]{2,1,0:T(1,128)S(1)} %bitcast.5), channel_id=1, replica_groups=mesh['gx'=2,'gy'=4,'gz'=4] {'gx','gy','gz'}, dimensions={0} | all-to-all | bytes 32768 | tf_op jit(solution)/shard_map/all_to_all | solution.py:1188
  40.3 1.2 %shard_map.128 = (f32[8,16,128]{2,1,0:T(8,128)}, f32[3,8,16,128]{3,2,1,0:T(8,128)}, f32[8,16,128]{2,1,0:T(8,128)}) custom-call(f32[32,128]{1,0:T(8,128)S(1)} %bitcast.4, f32[3,18,24,128]{3,2,1,0:T(8,128)S(1)} %get-tuple-element.55.refs_1_, f32[18,24,128]{2,1,0:T(8,128)S(1)} %get-tuple-element.39.refs_0_.refs_2_, ...), custom_call_target="tpu_custom_call" | custom-call | tf_op jit(solution)/shard_map/pallas_call | solution.py:1005
Async XLA Ops:
  3.2 9.0 %collective-permute-start.2 = (f32[10,8,16,128]{3,2,1,0:T(8,128)S(1)}, f32[10,8,16,128]{3,2,1,0:T(8,128)S(1)}, u32[]{:S(2)}, u32[]{:S(2)}) collective-permute-start(f32[10,8,16,128]{3,2,1,0:T(8,128)S(1)} %shard_map.122.refs_0_.refs_1_.refs_6_), channel_id=1, source_target_pairs={{0,16},{16,0},{1,17},{17,1},{2,18},{18,2},{3,19},{19,3},{4,20},{20... | collective-permute-start | bytes 1966088 | tf_op jit(solution)/shard_map/ppermute | solution.py:1017
  3.8 6.9 %collective-permute-start = (f32[272,128]{1,0:T(8,128)S(1)}, f32[272,128]{1,0:T(8,128)S(1)}, u32[]{:S(2)}, u32[]{:S(2)}) collective-permute-start(f32[272,128]{1,0:T(8,128)S(1)} %get-tuple-element.33), channel_id=1, source_target_pairs={{0,4},{4,0},{8,12},{12,8},{1,5},{5,1},{9,13},{13,9},{2,6},{6,2},{1... | collective-permute-start | bytes 417800 | tf_op jit(solution)/shard_map/ppermute | solution.py:1026
  6.4 4.3 %collective-permute-start.1 = (f32[272,128]{1,0:T(8,128)S(1)}, f32[272,128]{1,0:T(8,128)S(1)}, u32[]{:S(2)}, u32[]{:S(2)}) collective-permute-start(f32[272,128]{1,0:T(8,128)S(1)} %get-tuple-element.34), channel_id=1, source_target_pairs={{0,0},{4,8},{8,4},{12,12},{1,1},{5,9},{9,5},{13,13},{2,2},{6,10},{... | collective-permute-start | bytes 417800 | tf_op jit(solution)/shard_map/ppermute | solution.py:1026
  10.7 1.4 %collective-permute-start.3 = (f32[272,128]{1,0:T(8,128)S(1)}, f32[272,128]{1,0:T(8,128)S(1)}, u32[]{:S(2)}, u32[]{:S(2)}) collective-permute-start(f32[272,128]{1,0:T(8,128)S(1)} %collective-permute-done.refs_1_.refs_4_), channel_id=1, source_target_pairs={{0,16},{16,0},{1,17},{17,1},{2,18},{18,2},{3,19},{19,3},{4,20},{20... | collective-permute-start | bytes 417800 | tf_op jit(solution)/shard_map/ppermute | solution.py:1017
  10.7 1.6 %collective-permute-start.4 = (f32[272,128]{1,0:T(8,128)S(1)}, f32[272,128]{1,0:T(8,128)S(1)}, u32[]{:S(2)}, u32[]{:S(2)}) collective-permute-start(f32[272,128]{1,0:T(8,128)S(1)} %collective-permute-done.1.refs_2_.refs_5_), channel_id=1, source_target_pairs={{0,16},{16,0},{1,17},{17,1},{2,18},{18,2},{3,19},{19,3},{4,20},{20... | collective-permute-start | bytes 417800 | tf_op jit(solution)/shard_map/ppermute | solution.py:1017
  12.7 5.8 %collective-permute-start.5 = (f32[4,40,128]{2,1,0:T(8,128)S(1)}, f32[4,40,128]{2,1,0:T(8,128)S(1)}, u32[]{:S(2)}, u32[]{:S(2)}) collective-permute-start(f32[4,40,128]{2,1,0:T(8,128)S(1)} %get-tuple-element.38), channel_id=1, source_target_pairs={{0,1},{1,2},{2,3},{3,0},{16,19},{17,16},{18,17},{19,18},{4,5},{5,6... | collective-permute-start | bytes 245768 | tf_op jit(solution)/shard_map/ppermute | solution.py:1125
  18.6 4.9 %collective-permute-start.6 = (f32[4,40,128]{2,1,0:T(8,128)S(1)}, f32[4,40,128]{2,1,0:T(8,128)S(1)}, u32[]{:S(2)}, u32[]{:S(2)}) collective-permute-start(f32[4,40,128]{2,1,0:T(8,128)S(1)} %collective-permute-done.5.refs_2_), channel_id=1, source_target_pairs={{0,16},{16,0},{1,17},{17,1},{2,18},{18,2},{3,19},{19,3},{4,20},{20... | collective-permute-start | bytes 245768 | tf_op jit(solution)/shard_map/ppermute | solution.py:1017

commit v7 on v6

--- a/solution.py
+++ b/solution.py
@@ -29,7 +29,9 @@
 PAIRS = tuple((j, k) for j in range(3) for k in range(j, 3))
 SUMS = 4 + 4 * len(PAIRS)
 SEG = 16
-ENDS = 2 * SEG
+ENDS_KEPT = (("press", 1), ("motion", 3), ("z0", 1), ("p0", 1), ("zs", 9), ("ps", 9))
+ENDS_ARRAYS = sum(count for _, count in ENDS_KEPT)
+ENDS_START = dict(press=0, motion=1, z0=4, p0=5, zs=6, ps=15)
 UNROLL = dict(faces=8, start=8, next=8, shear=8, motion=8, image=3, finish=8)
 
 
@@ -196,13 +198,21 @@
             put(f, g, begin, finish)
 
 
-def put_ends(ends, f, g, begin, finish):
-    zeros = jnp.zeros((TILE, LANES), jnp.float32)
-    inner = SEG - W
-    ends[f, g, :TILE, :] = zeros
-    ends[f, g, ENDS - TILE :, :] = zeros
-    ends[f, g, W:SEG, :] = begin[:inner]
-    ends[f, g, SEG : ENDS - W, :] = finish[LANES - inner :]
+def sides_of(peers):
+    return 1 if peers[0] == 2 else 2
+
+
+def put_ends(peers, ends, f, g, begin, finish):
+    row = iota((SEG, LANES), 0)
+    left = pltpu.roll(begin[:SEG], W, 0)
+    right = pltpu.roll(finish[LANES - SEG :], SEG - W, 0)
+    left = jnp.where(row >= W, left, 0.0)
+    right = jnp.where(row < SEG - W, right, 0.0)
+    if sides_of(peers) == 1:
+        ends[f, g] = jnp.where(lax.axis_index("gx") == 0, left, right)
+    else:
+        ends[f, g, :SEG, :] = left
+        ends[f, g, SEG:, :] = right
 
 
 def put_message(peers, messages, f, g, begin, finish):
@@ -220,7 +230,7 @@
     *messages, stage = refs
 
     def put(f, g, begin, finish):
-        put_ends(ends, f, g, begin, finish)
+        put_ends(peers, ends, f, g, begin, finish)
         put_message(peers, messages, f, g, begin, finish)
 
     for message in messages:
@@ -246,7 +256,7 @@
     for b, (start, keep) in enumerate(blocks[1:]):
 
         def put(f, g, begin, finish, start=start):
-            put_ends(ends, f, start * count + g, begin, finish)
+            put_ends(peers, ends, f, start * count + g, begin, finish)
             put_message(peers, messages, f, start * count + g, begin, finish)
 
         for message in messages:
@@ -775,7 +785,7 @@
         return self.roll(v, 1)
 
     def zp(self, v):
-        return pltpu.roll(v, ENDS - 1, 1)
+        return pltpu.roll(v, v.shape[1] - 1, 1)
 
     def zm(self, v):
         return pltpu.roll(v, 1, 1)
@@ -801,18 +811,31 @@
         return total
 
     def run(self, halo, body, stage, before=0):
-        body(pl.ds(0, self.groups) if halo > 3 else self.near)
-
-    def assemble(self, ends, left, right, keep_left, keep_right, table):
+        body(pl.ds(0, self.groups))
+
+    def assemble(self, peers, ends, messages, table):
+        keep = keeps("gz", peers[2])
         for g in range(self.groups):
             for f in range(NF):
-                width, offset = WIDTHS[f], OFFSETS[f]
-                rows = slice(offset, offset + width)
                 self.raw[f, g] = ends[f, g]
-                self.raw[f, g, W - width : W, :] = left[g, rows, :] * keep_left
-                self.raw[f, g, ENDS - W : ENDS - W + width, :] = (
-                    right[g, rows, :] * keep_right
-                )
+
+        def halo(message, side, base, keep):
+            for g in range(self.groups):
+                for f in range(NF):
+                    width, offset = WIDTHS[f], OFFSETS[f]
+                    start = base + (SEG - W if side else W - width)
+                    self.raw[f, g, start : start + width, :] = (
+                        message[g, offset : offset + width, :] * keep
+                    )
+
+        if sides_of(peers) == 1:
+            first = lax.axis_index("gx") == 0
+            pl.when(first)(lambda: halo(messages[0], 0, 0, keep[0]))
+            pl.when(jnp.logical_not(first))(lambda: halo(messages[0], 1, 0, keep[1]))
+        else:
+            halo(messages[0], 0, 0, keep[0])
+            halo(messages[1], 1, SEG, keep[1])
+        for g in range(self.groups):
             zone = self.raw[ZONE, g]
             lame, shear = lookup(zone, table, 1), lookup(zone, table, 2)
             self.perm[g] = lookup(zone, table, 0)
@@ -834,47 +857,48 @@
 
 
 def ends_kernel(peers, tall, *refs):
-    table, ends, got, passed, added = refs[:5]
-    left, right = got, passed
-    if peers[0] == 2:
-        first = lax.axis_index("gx") == 0
-        left, right = Either(first, got, passed), Either(first, passed, got)
-    raw, z0, p0, zs, ps, partial = refs[5:11]
-    acc, scratch = refs[11], refs[12:]
+    sides = sides_of(peers)
+    table, ends, *messages = refs[: 2 + sides]
+    added, out, partial, raw, acc, *scratch = refs[2 + sides :]
     names = [name for name, _ in ARRAYS[6:] if name not in KEPT]
     domain = Ends(dict(zip(names, scratch)))
-    domain.raw, domain.z0, domain.p0, domain.zs, domain.ps = raw, z0, p0, zs, ps
+    domain.raw = raw
+    kept = {n: out.at[ENDS_START[n] : ENDS_START[n] + k] for n, k in ENDS_KEPT}
+    domain.z0, domain.p0 = out.at[ENDS_START["z0"]], out.at[ENDS_START["p0"]]
+    domain.zs, domain.ps = kept["zs"], kept["ps"]
     domain.zone, domain.press = raw.at[ZONE], raw.at[PRESS]
     domain.motion = raw.at[MOTION : MOTION + 3]
     domain.load, domain.drain = raw.at[SOURCE], raw.at[DRAIN]
     domain.body = raw.at[BODY : BODY + 3]
     domain.row = tall
     domain.groups = groups = raw.shape[1] - 1
-    count = groups // len(blocks_of(peers))
-    domain.near = pl.ds(0, groups)
-    if peers[0] == 2 and LANES // tall > 3:
-        domain.near = pl.ds(lax.axis_index("gx") * (count - 1), count + 1)
-    keep = keeps("gz", peers[2])
-    empty = jnp.zeros((ENDS, LANES), jnp.float32)
-    for ref in (raw, zs, ps):
+    columns = raw.shape[2]
+    empty = jnp.zeros((columns, LANES), jnp.float32)
+    for ref in (raw, out):
         for i in range(ref.shape[0]):
             ref[i, groups] = empty
-            if ref is not raw:
-                ref[i, groups - 1] = empty
-    for ref in (domain.perm, domain.shear, z0, p0):
+    for ref in (domain.perm, domain.shear):
         ref[groups] = empty
-    p0[groups - 1] = empty
-    mine = own_groups(count, peers)
-    domain.assemble(ends, left, right, *keep, table)
+    domain.assemble(peers, ends, messages, table)
     domain.stages()
+    for g in range(groups):
+        for i in range(4):
+            out[i, g] = raw[PRESS + i, g]
     acc[...] = added[...]
-    shape = (ENDS, LANES)
+    shape = (columns, LANES)
     column, row = iota(shape, 0), iota(shape, 1) % tall
-    at_end = ((column >= W) & (column < 2 * W)) | (
-        (column >= ENDS - 2 * W) & (column < ENDS - W)
-    )
+    if sides == 1:
+        start = jnp.where(lax.axis_index("gx") == 0, W, SEG - 2 * W)
+        at_end = (column >= start) & (column < start + W)
+        mine = pl.ds(0, groups)
+    else:
+        inner = column % SEG
+        start = jnp.where(column < SEG, W, SEG - 2 * W)
+        at_end = (inner >= start) & (inner < start + W)
+        count = groups // len(blocks_of(peers))
+        mine = pl.ds(own_groups(count, peers), count)
     mask = at_end & (row >= TILE) & (row < tall - TILE)
-    domain.finish(pl.ds(mine, count), acc, mask)
+    domain.finish(mine, acc, mask)
 
     sums = jnp.concatenate(
         [jnp.sum(acc[i], axis=0, keepdims=True) for i in range(acc.shape[0])], axis=0
@@ -895,10 +919,20 @@
 
 
 def combine(peers, tall, *refs):
+    pair = sides_of(peers) == 1
     sums, (old, z0, p0, zs) = refs[0], refs[1:5]
-    *ps, fields, raw, ends_z0, ends_p0, ends_zs, ends_ps = refs[5:-6]
+    *ps, fields, own_ends, other_ends = refs[5:-6] if pair else refs[5:-6] + refs[-7:-6]
     ps = Joined(*ps)
     pressure, motion, strain, moved, ends_moved, turned = refs[-6:]
+    if pair:
+        first = lax.axis_index("gx") == 0
+        halves = (Either(first, own_ends, other_ends), Either(first, other_ends, own_ends))
+
+    def end_of(side, i, g):
+        if pair:
+            return halves[side][i, g]
+        return own_ends[i, g, side * SEG : (side + 1) * SEG, :]
+
     line = jnp.sum(sums[...], axis=0, keepdims=True)
     lane = iota(line.shape, 1)
 
@@ -919,49 +953,63 @@
     on_z = [d1 * w for w in weights]
     on_p = [d2 * w for w in weights]
 
-    def new_motion(start, z_part, p_part, c, i):
+    def new_motion(start, z_part, p_part, c):
         total = start
         for j in range(3):
-            total = total + on_z[j] * z_part[3 * j + c, i]
-            total = total + on_p[j] * p_part[3 * j + c, i]
+            total = total + on_z[j] * z_part(3 * j + c)
+            total = total + on_p[j] * p_part(3 * j + c)
         return total
 
     nx, ny, nz = pressure.shape
     pack = LANES // tall
     ends = Ends(dict(row=tall))
-    groups = raw.shape[1] - 1
+    groups = own_ends.shape[1] - 1
     count = groups // len(blocks_of(peers))
     mine = own_groups(count, peers)
     every = pl.ds(0, groups)
-    if peers[0] == 2 and pack > 3:
+    if pair:
         every = pl.ds(lax.axis_index("gx") * (count - 1), count + 1)
-    for c in range(3):
-        for i in range(every.size):
-            g = every.start + i
-            ends_moved[c, g] = new_motion(raw[MOTION + c, g], ends_zs, ends_ps, c, g)
-        ends_moved[c, every.start + every.size] = jnp.zeros((ENDS, LANES), jnp.float32)
-    along_y, along_z = ends_moved[1, every], ends_moved[2, every]
-    first = ends_moved.at[0]
-    ends_moved[3, every] = 0.5 * (
-        (ends.nxt(first, every) - ends.prv(first, every))
-        + (ends.yp(along_y) - ends.ym(along_y))
-        + (ends.zp(along_z) - ends.zm(along_z))
-    )
+    empty = jnp.zeros((SEG, LANES), jnp.float32)
+    start = ENDS_START
+    for side in range(2):
+        for c in range(3):
+            for i in range(every.size):
+                g = every.start + i
+                ends_moved[side, c, g] = new_motion(
+                    end_of(side, start["motion"] + c, g),
+                    lambda k, side=side, g=g: end_of(side, start["zs"] + k, g),
+                    lambda k, side=side, g=g: end_of(side, start["ps"] + k, g),
+                    c,
+                )
+            ends_moved[side, c, every.start + every.size] = empty
+        along_y, along_z = ends_moved[side, 1, every], ends_moved[side, 2, every]
+        along_x = ends_moved.at[side, 0]
+        ends_moved[side, 3, every] = 0.5 * (
+            (ends.nxt(along_x, every) - ends.prv(along_x, every))
+            + (ends.yp(along_y) - ends.ym(along_y))
+            + (ends.zp(along_z) - ends.zm(along_z))
+        )
     for c in range(3):
         around = 1 if c == 0 else 0
         for l in range(W - around, W + nx + around):
-            moved[c, l] = new_motion(old[c, l], zs, ps, c, l)
+            moved[c, l] = new_motion(
+                old[c, l], lambda k, l=l: zs[k, l], lambda k, l=l: ps[k, l], c
+            )
     brick = Brick({})
     outs = [pressure] + [motion.at[c] for c in range(3)] + [strain]
     for g in range(count):
         at = mine + g
-        edges = [raw[PRESS, at] + c1 * ends_z0[at] + c2 * ends_p0[at]]
-        edges = edges + [ends_moved[c, at] for c in range(4)]
         flipped = []
-        for o, edge in enumerate(edges):
+        for o in range(len(outs)):
             slot = g * len(outs) + o
-            turned[slot, :W, :] = edge[W : 2 * W]
-            turned[slot, LANES - W :, :] = edge[ENDS - 2 * W : ENDS - W]
+            for side, (row, first_row) in enumerate(((0, W), (LANES - W, SEG - 2 * W))):
+                if o == 0:
+                    edge = end_of(side, start["press"], at)
+                    edge = edge + c1 * end_of(side, start["z0"], at)
+                    edge = edge + c2 * end_of(side, start["p0"], at)
+                else:
+                    edge = ends_moved[side, o - 1, at]
+                turned[slot, row : row + W, :] = edge[first_row : first_row + W]
             flipped.append(turned[slot].T)
         for i in range(pack):
             x = g * pack + i
@@ -1102,7 +1150,7 @@
     sides = 1 if pair else 2
     own_ends, *own_messages = call(
         with_peers(pack_own),
-        [f32(NF, groups, ENDS, LANES)] + [f32(groups, MSG_ROWS, LANES)] * sides,
+        [f32(NF, groups, sides * SEG, LANES)] + [f32(groups, MSG_ROWS, LANES)] * sides,
         fields,
         first,
         second,
@@ -1111,7 +1159,7 @@
     span = (1 + len(others)) * groups
     ends, *messages = call(
         with_peers(pack_others),
-        [f32(NF, span, ENDS, LANES)] + [f32(span, MSG_ROWS, LANES)] * sides,
+        [f32(NF, span, sides * SEG, LANES)] + [f32(span, MSG_ROWS, LANES)] * sides,
         own_ends,
         *own_messages,
         *[array for block in others for array in block],
@@ -1122,9 +1170,9 @@
         n = peers[2]
         hops = [(i, (i + 1) % n) for i in range(n)]
         hops += [(n + i, n + (i - 1) % n) for i in range(n)]
-        got = lax.ppermute(messages[0], ("gx", "gz"), hops)
+        got = [lax.ppermute(messages[0], ("gx", "gz"), hops)]
     else:
-        got, passed = ring(messages[0], "gz", 1), ring(messages[1], "gz", -1)
+        got = [ring(messages[0], "gz", 1), ring(messages[1], "gz", -1)]
     depth = nx + 2 * W
     cells = depth * ny * nz
 
@@ -1156,8 +1204,6 @@
         limit=16,
     )
     half = dict(zip(FIRST_OUTS, halves))
-    if pair:
-        passed = ring(got, "gx", -1)
     late = [f32(3 * len(SECOND_IMAGES), depth, ny + TILE, nz)] * bool(SECOND_IMAGES)
     *last, added = call(
         with_peers(brick_second, nx, ny),
@@ -1166,25 +1212,25 @@
         ps,
     )
     kept = [half[name] for name in KEPT[:-1]] + [ps, *last]
-    span = span + 1
-    *ends_kept, partial = call(
+    span, columns = span + 1, sides * SEG
+    ends_kept, partial = call(
         with_peers(ends_kernel, tall),
-        [f32(NF, span, ENDS, LANES)]
-        + [f32(*shaped(leads[name], span, ENDS, LANES)) for name in KEPT[1:]]
-        + [f32(total, LANES)],
+        [f32(ENDS_ARRAYS, span, columns, LANES), f32(total, LANES)],
         table,
         ends,
-        got,
-        passed,
+        *got,
         added,
-        scratch=[vmem(*sums_shape)]
+        scratch=[vmem(NF, span, columns, LANES), vmem(*sums_shape)]
         + [
-            vmem(*shaped(lead, span, ENDS, LANES))
+            vmem(*shaped(lead, span, columns, LANES))
             for name, lead in ARRAYS[6:]
             if name not in KEPT
         ],
         limit=16,
     )
+    both = [ends_kept]
+    if pair:
+        both.append(ring(ends_kept, "gx", -1))
     sums = lax.all_to_all(partial, AXES, 0, 0, tiled=True)
     return tuple(
         call(
@@ -1193,10 +1239,10 @@
             sums,
             *kept,
             fields,
-            *ends_kept,
+            *both,
             scratch=[
                 vmem(3, depth, ny + TILE, nz),
-                vmem(4, span, ENDS, LANES),
+                vmem(2, 4, span, SEG, LANES),
                 vmem(5 * groups, LANES, LANES),
             ],
             limit=16,

time: 41.8 us -> 36.6 us (0.88)
  waiting for transfers between devices: 8.32 us -> 4.19 us
  blocking collectives: 14.2 us -> 13 us
  starting transfers between devices: 6.08 us -> 7.08 us
  Pallas kernels: 12.2 us -> 11.5 us
    ppermute x1, waiting for transfers between devices: 4.13 us -> 0.01 us  [shards(): got = [lax.ppermute(messages[0], ('gx', 'gz'), hops)]]
    all_to_all x1, blocking collectives: 14.2 us -> 13 us  [shards(): sums = lax.all_to_all(partial, AXES, 0, 0, tiled=True)]
    ppermute x4, starting transfers between devices: 1.07 us -> 2.08 us  [ring(): lax.ppermute(value, axis, [(i, (i + step) % peers) for i in range(peers)])]
    pallas_call x8, Pallas kernels: 12.2 us -> 11.5 us  [call(): pl.pallas_call(kernel, out_shape=outs, in_specs=specs, scratch_shapes=scr...]
  transfers between devices with their start and end apart: 7 -> 7, of which waited for: 4 -> 3; matrix products, arithmetic and copies ran while one was open for 0% -> 0% of each run, Pallas kernels for 13% -> 15%
where the time goes in v7:
time: 36.6 us; the launch traced here: 36.4 us
  blocking collectives  13 us (36%)
  Pallas kernels  11.5 us (31%)
  starting transfers between devices  7.08 us (19%)
  waiting for transfers between devices  4.19 us (11%)
  between operations  0.7 us (2%)
    all_to_all x1, blocking collectives, shards(): sums = lax.all_to_all(partial, AXES, 0, 0, tiled=True)  13 us
    pallas_call x8, Pallas kernels, call(): pl.pallas_call(kernel, out_shape=outs, in_specs=specs, scratch_shapes=scr...  11.5 us
    ppermute x2, waiting for transfers between devices, pairs(): return lax.ppermute(value, axis, swaps)  3.6 us
    ppermute x2, starting transfers between devices, pairs(): return lax.ppermute(value, axis, swaps)  3.3 us
    ppermute x4, starting transfers between devices, ring(): lax.ppermute(value, axis, [(i, (i + step) % peers) for i in range(peers)])  2.08 us
    ppermute x1, starting transfers between devices, shards(): got = [lax.ppermute(messages[0], ('gx', 'gz'), hops)]  1.71 us
  transfers between devices with their start and end apart: 7, of which 3 were waited for; matrix products, arithmetic and copies ran while one was open for 0% of the time, Pallas kernels for 15%

profile of v7, /device:TPU:0, one launch (start us, length us, event | category | flops | bytes accessed | tf_op | source)
XLA Modules:
  0.0 36.4 jit_solution(12417815447002068264)
XLA Ops:
  0.6 1.3 %shard_map.121 = (f32[272,128]{1,0:T(8,128)S(1)}, f32[272,128]{1,0:T(8,128)S(1)}, f32[8,128]{1,0:T(8,128)S(1)}) custom-call(f32[8,16,128]{2,1,0:T(8,128)} %refs_0_.3, f32[8,16,128]{2,1,0:T(8,128)} %refs_1_.3, f32[8,16,128]{2,1,0:T(8,128)} %refs_2_.3, f32[3,8,16,128]{3,2,1,0:T(8,128)} %refs_3_.3, f32[3,8,16,128]{3,2,1,0:T(8,128)} %refs_4_.3, ...), custom_call_target="tpu_custom_call" | custom-call | tf_op jit(solution)/shard_map/pallas_call | solution.py:1053
  1.9 1.3 %shard_map.122.refs_0_.refs_1_.refs_6_ = f32[10,8,16,128]{3,2,1,0:T(8,128)S(1)} custom-call(f32[8,16,128]{2,1,0:T(8,128)} %refs_0_.3, f32[8,16,128]{2,1,0:T(8,128)} %refs_1_.3, f32[8,16,128]{2,1,0:T(8,128)} %refs_2_.3, f32[3,8,16,128]{3,2,1,0:T(8,128)} %refs_3_.3, f32[3,8,16,128]{3,2,1,0:T(8,128)} %refs_4_.3, s32[8,16,128]{2,1,0:T(8,128)} %refs_5_.3, ...), custom_call_target="tpu_custom_call" | custom-call | tf_op jit(solution)/shard_map/pallas_call | solution.py:1053
  3.2 0.6 %collective-permute-start.2 = (f32[10,8,16,128]{3,2,1,0:T(8,128)S(1)}, f32[10,8,16,128]{3,2,1,0:T(8,128)S(1)}, u32[]{:S(2)}, u32[]{:S(2)}) collective-permute-start(f32[10,8,16,128]{3,2,1,0:T(8,128)S(1)} %shard_map.122.refs_0_.refs_1_.refs_6_), channel_id=1, source_target_pairs={{0,16},{16,0},{1,17},{17,1},{2,18},{18,2},{3,19},{19,3},{4,20},{20... | collective-permute-start | bytes 1966088 | tf_op jit(solution)/shard_map/ppermute | solution.py:1065
  3.8 2.6 %collective-permute-start = (f32[272,128]{1,0:T(8,128)S(1)}, f32[272,128]{1,0:T(8,128)S(1)}, u32[]{:S(2)}, u32[]{:S(2)}) collective-permute-start(f32[272,128]{1,0:T(8,128)S(1)} %get-tuple-element.29), channel_id=1, source_target_pairs={{0,4},{4,0},{8,12},{12,8},{1,5},{5,1},{9,13},{13,9},{2,6},{6,2},{1... | collective-permute-start | bytes 417800 | tf_op jit(solution)/shard_map/ppermute | solution.py:1074
  6.4 0.7 %collective-permute-start.1 = (f32[272,128]{1,0:T(8,128)S(1)}, f32[272,128]{1,0:T(8,128)S(1)}, u32[]{:S(2)}, u32[]{:S(2)}) collective-permute-start(f32[272,128]{1,0:T(8,128)S(1)} %get-tuple-element.30), channel_id=1, source_target_pairs={{0,0},{4,8},{8,4},{12,12},{1,1},{5,9},{9,5},{13,13},{2,2},{6,10},{... | collective-permute-start | bytes 417800 | tf_op jit(solution)/shard_map/ppermute | solution.py:1074
  7.1 3.6 %collective-permute-done.refs_1_.refs_4_ = f32[272,128]{1,0:T(8,128)S(1)} collective-permute-done((f32[272,128]{1,0:T(8,128)S(1)}, f32[272,128]{1,0:T(8,128)S(1)}, u32[]{:S(2)}, u32[]{:S(2)}) %collective-permute-start) | collective-permute-done | bytes 139296 | tf_op jit(solution)/shard_map/ppermute | solution.py:1074
  10.7 0.0 collective-permute-start.3
  10.7 0.0 collective-permute-done.1.refs_2_.refs_5_
  10.7 0.5 %collective-permute-start.4 = (f32[272,128]{1,0:T(8,128)S(1)}, f32[272,128]{1,0:T(8,128)S(1)}, u32[]{:S(2)}, u32[]{:S(2)}) collective-permute-start(f32[272,128]{1,0:T(8,128)S(1)} %collective-permute-done.1.refs_2_.refs_5_), channel_id=1, source_target_pairs={{0,16},{16,0},{1,17},{17,1},{2,18},{18,2},{3,19},{19,3},{4,20},{20... | collective-permute-start | bytes 417800 | tf_op jit(solution)/shard_map/ppermute | solution.py:1065
  11.2 0.5 %shard_map.123 = (f32[10,2,16,128]{3,2,1,0:T(8,128)S(1)}, f32[2,40,128]{2,1,0:T(8,128)S(1)}) custom-call(f32[10,8,16,128]{3,2,1,0:T(8,128)S(1)} %shard_map.122.refs_0_.refs_1_.refs_6_, f32[272,128]{1,0:T(8,128)S(1)} %collective-permute-done.refs_1_.refs_4_, f32[272,128]{1,0:T(8,128)S(1)} %collective-permute-done.1.refs_2_.refs_5_), custom_call_target="tpu_custom_call" | custom-call | tf_op jit(solution)/shard_map/pallas_call | solution.py:1053
  11.7 0.4 %collective-permute-done.3.refs_3_.refs_6_.refs_8_ = f32[272,128]{1,0:T(8,128)S(1)} collective-permute-done((f32[272,128]{1,0:T(8,128)S(1)}, f32[272,128]{1,0:T(8,128)S(1)}, u32[]{:S(2)}, u32[]{:S(2)}) %collective-permute-start.3) | collective-permute-done | bytes 139296 | tf_op jit(solution)/shard_map/ppermute | solution.py:1065
  12.0 0.2 collective-permute-done.4.refs_4_.refs_7_.refs_9_
  12.2 0.0 collective-permute-done.2.refs_2_.refs_3_
  12.2 0.5 %shard_map.124 = (f32[10,4,16,128]{3,2,1,0:T(8,128)S(1)}, f32[4,40,128]{2,1,0:T(8,128)S(1)}) custom-call(f32[10,2,16,128]{3,2,1,0:T(8,128)S(1)} %get-tuple-element.31.refs_0_, f32[2,40,128]{2,1,0:T(8,128)S(1)} %get-tuple-element.32.refs_1_, f32[10,8,16,128]{3,2,1,0:T(8,128)S(1)} %collective-permute-done.2.refs_2_.refs_3_, ...), custom_call_target="tpu_custom_call" | custom-call | tf_op jit(solution)/shard_map/pallas_call | solution.py:1053
  12.7 1.7 %collective-permute-start.5 = (f32[4,40,128]{2,1,0:T(8,128)S(1)}, f32[4,40,128]{2,1,0:T(8,128)S(1)}, u32[]{:S(2)}, u32[]{:S(2)}) collective-permute-start(f32[4,40,128]{2,1,0:T(8,128)S(1)} %get-tuple-element.34), channel_id=1, source_target_pairs={{0,1},{1,2},{2,3},{3,0},{16,19},{17,16},{18,17},{19,18},{4,5},{5,6... | collective-permute-start | bytes 245768 | tf_op jit(solution)/shard_map/ppermute | solution.py:1173
  14.4 3.9 %shard_map.125 = (f32[3,18,24,128]{3,2,1,0:T(8,128)S(1)}, f32[18,24,128]{2,1,0:T(8,128)S(1)}, f32[18,24,128]{2,1,0:T(8,128)S(1)}, f32[9,18,24,128]{3,2,1,0:T(8,1...) custom-call(f32[8,128]{1,0:T(8,128)S(1)} %get-tuple-element.28.refs_, ...), custom_call_target="tpu_custom_call" | custom-call | tf_op jit(solution)/shard_map/pallas_call | solution.py:1053
  18.4 1.0 %shard_map.126.refs_3_ = f32[32,8,128]{2,1,0:T(8,128)S(1)} custom-call(f32[18,24,128]{2,1,0:T(8,128)S(1)} %get-tuple-element.35.refs_0_.refs_2_, f32[18,24,128]{2,1,0:T(8,128)S(1)} %get-tuple-element.36.refs_1_.refs_3_, f32[9,18,24,128]{3,2,1,0:T(8,128)S(1)} %get-tuple-element.37.refs_2_.refs_4_, f32[18,24,128]{2,1,0:T(8,128)S(1)} %get-tuple-element.38.refs_3_, ...), custom_call_target="tpu_custom_call" | custom-call | tf_op jit(solution)/shard_map/pallas_call | solution.py:1053
  19.3 0.0 collective-permute-done.5.refs_2_
  19.4 1.8 %shard_map.127 = (f32[24,5,16,128]{3,2,1,0:T(8,128)S(1)}, f32[32,128]{1,0:T(8,128)S(1)}) custom-call(f32[8,128]{1,0:T(8,128)S(1)} %get-tuple-element.28.refs_7_.refs_0_, f32[10,4,16,128]{3,2,1,0:T(8,128)S(1)} %get-tuple-element.33.refs_1_, f32[4,40,128]{2,1,0:T(8,128)S(1)} %collective-permute-done.5.refs_2_, f32[32,8,128]{2,1,0:T(8,128)S(1)} %shard_map.126.refs_3_), custom_call_target="tpu_custom_call" | custom-call | tf_op jit(solution)/shard_map/pallas_call | solution.py:1053
  21.2 1.0 %collective-permute-start.6 = (f32[24,5,16,128]{3,2,1,0:T(8,128)S(1)}, f32[24,5,16,128]{3,2,1,0:T(8,128)S(1)}, u32[]{:S(2)}, u32[]{:S(2)}) collective-permute-start(f32[24,5,16,128]{3,2,1,0:T(8,128)S(1)} %get-tuple-element.52.refs_7_), channel_id=1, source_target_pairs={{0,16},{16,0},{1,17},{17,1},{2,18},{18,2},{3,19},{19,3},{4,20},{20... | collective-permute-start | bytes 2949128 | tf_op jit(solution)/shard_map/ppermute | solution.py:1065
  22.2 13.0 %all_to_all.11 = f32[32,1,128]{2,1,0:T(1,128)S(1)} all-to-all(f32[32,1,128]{2,1,0:T(1,128)S(1)} %bitcast.5), channel_id=1, replica_groups=mesh['gx'=2,'gy'=4,'gz'=4] {'gx','gy','gz'}, dimensions={0} | all-to-all | bytes 32768 | tf_op jit(solution)/shard_map/all_to_all | solution.py:1234
  35.1 0.0 collective-permute-done.6.refs_8_
  35.2 1.2 %shard_map.128 = (f32[8,16,128]{2,1,0:T(8,128)}, f32[3,8,16,128]{3,2,1,0:T(8,128)}, f32[8,16,128]{2,1,0:T(8,128)}) custom-call(f32[32,128]{1,0:T(8,128)S(1)} %bitcast.4, f32[3,18,24,128]{3,2,1,0:T(8,128)S(1)} %get-tuple-element.51.refs_1_, f32[18,24,128]{2,1,0:T(8,128)S(1)} %get-tuple-element.35.refs_0_.refs_2_, ...), custom_call_target="tpu_custom_call" | custom-call | tf_op jit(solution)/shard_map/pallas_call | solution.py:1053
Async XLA Ops:
  3.2 9.0 %collective-permute-start.2 = (f32[10,8,16,128]{3,2,1,0:T(8,128)S(1)}, f32[10,8,16,128]{3,2,1,0:T(8,128)S(1)}, u32[]{:S(2)}, u32[]{:S(2)}) collective-permute-start(f32[10,8,16,128]{3,2,1,0:T(8,128)S(1)} %shard_map.122.refs_0_.refs_1_.refs_6_), channel_id=1, source_target_pairs={{0,16},{16,0},{1,17},{17,1},{2,18},{18,2},{3,19},{19,3},{4,20},{20... | collective-permute-start | bytes 1966088 | tf_op jit(solution)/shard_map/ppermute | solution.py:1065
  3.8 6.9 %collective-permute-start = (f32[272,128]{1,0:T(8,128)S(1)}, f32[272,128]{1,0:T(8,128)S(1)}, u32[]{:S(2)}, u32[]{:S(2)}) collective-permute-start(f32[272,128]{1,0:T(8,128)S(1)} %get-tuple-element.29), channel_id=1, source_target_pairs={{0,4},{4,0},{8,12},{12,8},{1,5},{5,1},{9,13},{13,9},{2,6},{6,2},{1... | collective-permute-start | bytes 417800 | tf_op jit(solution)/shard_map/ppermute | solution.py:1074
  6.4 4.3 %collective-permute-start.1 = (f32[272,128]{1,0:T(8,128)S(1)}, f32[272,128]{1,0:T(8,128)S(1)}, u32[]{:S(2)}, u32[]{:S(2)}) collective-permute-start(f32[272,128]{1,0:T(8,128)S(1)} %get-tuple-element.30), channel_id=1, source_target_pairs={{0,0},{4,8},{8,4},{12,12},{1,1},{5,9},{9,5},{13,13},{2,2},{6,10},{... | collective-permute-start | bytes 417800 | tf_op jit(solution)/shard_map/ppermute | solution.py:1074
  10.7 1.4 %collective-permute-start.3 = (f32[272,128]{1,0:T(8,128)S(1)}, f32[272,128]{1,0:T(8,128)S(1)}, u32[]{:S(2)}, u32[]{:S(2)}) collective-permute-start(f32[272,128]{1,0:T(8,128)S(1)} %collective-permute-done.refs_1_.refs_4_), channel_id=1, source_target_pairs={{0,16},{16,0},{1,17},{17,1},{2,18},{18,2},{3,19},{19,3},{4,20},{20... | collective-permute-start | bytes 417800 | tf_op jit(solution)/shard_map/ppermute | solution.py:1065
  10.7 1.6 %collective-permute-start.4 = (f32[272,128]{1,0:T(8,128)S(1)}, f32[272,128]{1,0:T(8,128)S(1)}, u32[]{:S(2)}, u32[]{:S(2)}) collective-permute-start(f32[272,128]{1,0:T(8,128)S(1)} %collective-permute-done.1.refs_2_.refs_5_), channel_id=1, source_target_pairs={{0,16},{16,0},{1,17},{17,1},{2,18},{18,2},{3,19},{19,3},{4,20},{20... | collective-permute-start | bytes 417800 | tf_op jit(solution)/shard_map/ppermute | solution.py:1065
  12.7 6.6 %collective-permute-start.5 = (f32[4,40,128]{2,1,0:T(8,128)S(1)}, f32[4,40,128]{2,1,0:T(8,128)S(1)}, u32[]{:S(2)}, u32[]{:S(2)}) collective-permute-start(f32[4,40,128]{2,1,0:T(8,128)S(1)} %get-tuple-element.34), channel_id=1, source_target_pairs={{0,1},{1,2},{2,3},{3,0},{16,19},{17,16},{18,17},{19,18},{4,5},{5,6... | collective-permute-start | bytes 245768 | tf_op jit(solution)/shard_map/ppermute | solution.py:1173
  21.2 14.0 %collective-permute-start.6 = (f32[24,5,16,128]{3,2,1,0:T(8,128)S(1)}, f32[24,5,16,128]{3,2,1,0:T(8,128)S(1)}, u32[]{:S(2)}, u32[]{:S(2)}) collective-permute-start(f32[24,5,16,128]{3,2,1,0:T(8,128)S(1)} %get-tuple-element.52.refs_7_), channel_id=1, source_target_pairs={{0,16},{16,0},{1,17},{17,1},{2,18},{18,2},{3,19},{19,3},{4,20},{20... | collective-permute-start | bytes 2949128 | tf_op jit(solution)/shard_map/ppermute | solution.py:1065

commit v8 on v7

--- a/solution.py
+++ b/solution.py
@@ -292,9 +292,7 @@
     return jnp.where(zone > 0.0, biot_coef * biot_coef / scale, 0.0)
 
 
-FIRST_IMAGES, SECOND_IMAGES = (0, 1, 2), ()
 KEPT = ("motion", "z0", "p0", "zs", "ps")
-PASSED = ("heft", "mx", "my", "mz", "react", "tx", "ty", "tz", "pdiag", "ediag", "einv")
 ARRAYS = (
     ("zone", 0),
     ("press", 0),
@@ -472,24 +470,13 @@
             self.ps[3 * j + c, l] = image[c] * self.einv[c, l]
 
     def stages(self):
-        self.first_half()
-        self.second_half()
-
-    def first_half(self):
         self.run(4, self.press_faces, "faces", 1)
         self.run(4, self.press_start, "start")
         self.run(3, self.press_next, "next")
         self.run(2, self.motion_faces, "shear", 1)
         self.run(2, self.motion_start, "motion")
-        for j in FIRST_IMAGES:
-            self.images(j)
-
-    def second_half(self):
-        for j in SECOND_IMAGES:
-            self.images(j)
-
-    def images(self, j):
-        self.run(1, lambda l: self.motion_next(l, j), "image")
+        for j in range(3):
+            self.run(1, lambda l: self.motion_next(l, j), "image")
 
     def finish(self, l, acc, mask):
         own = self.own
@@ -667,37 +654,18 @@
     return domain
 
 
-FIRST_OUTS = ("motion", "z0", "p0", "zs") + PASSED
-FIRST_SCRATCH = tuple(n for n, _ in ARRAYS if n not in FIRST_OUTS + ("ps",))
-
-
-class Joined:
-    def __init__(self, *refs):
-        self.refs = refs
-        self.at = self
-
-    def __getitem__(self, index):
-        first, *rest = index if isinstance(index, tuple) else (index,)
-        for ref in self.refs:
-            if first < ref.shape[0]:
-                return ref[first, *rest] if rest else ref.at[first]
-            first -= ref.shape[0]
-
-    def __setitem__(self, index, value):
-        self[index[0]][index[1:]] = value
-
-
-def brick_first(peers, *refs):
+BRICK_SCRATCH = tuple(name for name, _ in ARRAYS if name not in KEPT)
+
+
+def brick_kernel(peers, *refs):
     table, fields, below, above = refs[:4]
     rows = [Rows(*refs[i : i + 2], peers) for i in (4, 6, 8)]
-    outs = refs[10 : 10 + len(FIRST_OUTS)]
-    ps, *scratch = refs[10 + len(FIRST_OUTS) :]
+    outs, acc, scratch = refs[10 : 10 + len(KEPT)], refs[10 + len(KEPT)], refs[11 + len(KEPT) :]
     _, nx, ny, nz = fields.shape
     domain = new_brick(peers, nx, ny)
-    domain.__dict__.update(zip(FIRST_OUTS, outs))
-    domain.__dict__.update(zip(FIRST_SCRATCH, scratch))
-    domain.zone_tall, domain.perm_tall, domain.face_sum = scratch[len(FIRST_SCRATCH) :]
-    domain.ps = Joined(ps)
+    domain.__dict__.update(zip(KEPT, outs))
+    domain.__dict__.update(zip(BRICK_SCRATCH, scratch))
+    domain.zone_tall, domain.perm_tall, domain.face_sum = scratch[len(BRICK_SCRATCH) :]
 
     empty = jnp.zeros((ny + TILE, nz), jnp.float32)
     for l in (W - 1, W + nx):
@@ -707,8 +675,7 @@
             domain.motion[c, l] = empty
         for i in range(9):
             domain.zs[i, l] = empty
-        for i in range(ps.shape[0]):
-            ps[i, l] = empty
+            domain.ps[i, l] = empty
         domain.perm_tall[l] = jnp.zeros((ny + 2 * TILE, nz), jnp.float32)
 
     for x in range(nx):
@@ -731,24 +698,7 @@
             domain.assemble(u, x, below, lambda f, x=x: rows[1].read(f, x), table, keep_below)
             l = W + nx + u
             domain.assemble(l, u, above, lambda f, u=u: rows[2].read(f, u), table, keep_above)
-    domain.first_half()
-
-
-SECOND_INS = ("z0", "p0", "zs") + PASSED
-
-
-def brick_second(peers, nx, ny, *refs):
-    domain = new_brick(peers, nx, ny)
-    domain.__dict__.update(zip(SECOND_INS, refs))
-    ready, *made, acc = refs[len(SECOND_INS) :]
-    domain.ps = Joined(ready, *made)
-    nz = ready.shape[3]
-    empty = jnp.zeros((ny + TILE, nz), jnp.float32)
-    for ps in made:
-        for l in (W - 1, W + nx):
-            for i in range(ps.shape[0]):
-                ps[i, l] = empty
-    domain.second_half()
+    domain.stages()
     acc[...] = jnp.zeros(acc.shape, jnp.float32)
     domain.loop(W, nx, lambda l: domain.finish(l, acc, None), "finish")
     if nz == LANES:
@@ -921,8 +871,7 @@
 def combine(peers, tall, *refs):
     pair = sides_of(peers) == 1
     sums, (old, z0, p0, zs) = refs[0], refs[1:5]
-    *ps, fields, own_ends, other_ends = refs[5:-6] if pair else refs[5:-6] + refs[-7:-6]
-    ps = Joined(*ps)
+    ps, fields, own_ends, other_ends = refs[5:-6] if pair else refs[5:-6] + refs[-7:-6]
     pressure, motion, strain, moved, ends_moved, turned = refs[-6:]
     if pair:
         first = lax.axis_index("gx") == 0
@@ -1185,10 +1134,9 @@
     def layers_of(name):
         return shaped(leads[name], depth, ny + TILE, nz)
 
-    *halves, ps = call(
-        with_peers(brick_first),
-        [f32(*layers_of(name)) for name in FIRST_OUTS]
-        + [f32(3 * len(FIRST_IMAGES), depth, ny + TILE, nz)],
+    *kept, added = call(
+        with_peers(brick_kernel),
+        [f32(*layers_of(name)) for name in KEPT] + [f32(*sums_shape)],
         table,
         fields,
         fields_below,
@@ -1199,19 +1147,10 @@
         second_below,
         first_above,
         second_above,
-        scratch=[vmem(*layers_of(name)) for name in FIRST_SCRATCH]
+        scratch=[vmem(*layers_of(name)) for name in BRICK_SCRATCH]
         + [vmem(depth, tall, nz), vmem(depth, tall, nz), vmem(depth, ny + TILE, nz)],
-        limit=16,
+        limit=20,
     )
-    half = dict(zip(FIRST_OUTS, halves))
-    late = [f32(3 * len(SECOND_IMAGES), depth, ny + TILE, nz)] * bool(SECOND_IMAGES)
-    *last, added = call(
-        with_peers(brick_second, nx, ny),
-        late + [f32(*sums_shape)],
-        *[half[name] for name in SECOND_INS],
-        ps,
-    )
-    kept = [half[name] for name in KEPT[:-1]] + [ps, *last]
     span, columns = span + 1, sides * SEG
     ends_kept, partial = call(
         with_peers(ends_kernel, tall),

time: 36.6 us -> 36.5 us (level)
    pallas_call x8 -> x7, Pallas kernels: 11.5 us -> 11.4 us  [call(): pl.pallas_call(kernel, out_shape=outs, in_specs=specs, scratch_shapes=scr...]
where the time goes in v8:
time: 36.5 us; the launch traced here: 36.3 us
  blocking collectives  13 us (36%)
  Pallas kernels  11.4 us (31%)
  starting transfers between devices  7.07 us (19%)
  waiting for transfers between devices  4.19 us (11%)
  between operations  0.69 us (2%)
    all_to_all x1, blocking collectives, shards(): sums = lax.all_to_all(partial, AXES, 0, 0, tiled=True)  13 us
    pallas_call x7, Pallas kernels, call(): pl.pallas_call(kernel, out_shape=outs, in_specs=specs, scratch_shapes=scr...  11.4 us
    ppermute x2, waiting for transfers between devices, pairs(): return lax.ppermute(value, axis, swaps)  3.6 us
    ppermute x2, starting transfers between devices, pairs(): return lax.ppermute(value, axis, swaps)  3.3 us
    ppermute x4, starting transfers between devices, ring(): lax.ppermute(value, axis, [(i, (i + step) % peers) for i in range(peers)])  2.07 us
    ppermute x1, starting transfers between devices, shards(): got = [lax.ppermute(messages[0], ('gx', 'gz'), hops)]  1.71 us
  transfers between devices with their start and end apart: 7, of which 3 were waited for; matrix products, arithmetic and copies ran while one was open for 0% of the time, Pallas kernels for 15%

profile of v8, /device:TPU:0, one launch (start us, length us, event | category | flops | bytes accessed | tf_op | source)
XLA Modules:
  0.0 36.3 jit_solution(9682714528733340046)
XLA Ops:
  0.6 1.3 %shard_map.121 = (f32[272,128]{1,0:T(8,128)S(1)}, f32[272,128]{1,0:T(8,128)S(1)}, f32[8,128]{1,0:T(8,128)S(1)}) custom-call(f32[8,16,128]{2,1,0:T(8,128)} %refs_0_.3, f32[8,16,128]{2,1,0:T(8,128)} %refs_1_.3, f32[8,16,128]{2,1,0:T(8,128)} %refs_2_.3, f32[3,8,16,128]{3,2,1,0:T(8,128)} %refs_3_.3, f32[3,8,16,128]{3,2,1,0:T(8,128)} %refs_4_.3, ...), custom_call_target="tpu_custom_call" | custom-call | tf_op jit(solution)/shard_map/pallas_call | solution.py:1002
  1.9 1.3 %shard_map.122.refs_0_.refs_1_.refs_6_ = f32[10,8,16,128]{3,2,1,0:T(8,128)S(1)} custom-call(f32[8,16,128]{2,1,0:T(8,128)} %refs_0_.3, f32[8,16,128]{2,1,0:T(8,128)} %refs_1_.3, f32[8,16,128]{2,1,0:T(8,128)} %refs_2_.3, f32[3,8,16,128]{3,2,1,0:T(8,128)} %refs_3_.3, f32[3,8,16,128]{3,2,1,0:T(8,128)} %refs_4_.3, s32[8,16,128]{2,1,0:T(8,128)} %refs_5_.3, ...), custom_call_target="tpu_custom_call" | custom-call | tf_op jit(solution)/shard_map/pallas_call | solution.py:1002
  3.2 0.6 %collective-permute-start.2 = (f32[10,8,16,128]{3,2,1,0:T(8,128)S(1)}, f32[10,8,16,128]{3,2,1,0:T(8,128)S(1)}, u32[]{:S(2)}, u32[]{:S(2)}) collective-permute-start(f32[10,8,16,128]{3,2,1,0:T(8,128)S(1)} %shard_map.122.refs_0_.refs_1_.refs_6_), channel_id=1, source_target_pairs={{0,16},{16,0},{1,17},{17,1},{2,18},{18,2},{3,19},{19,3},{4,20},{20... | collective-permute-start | bytes 1966088 | tf_op jit(solution)/shard_map/ppermute | solution.py:1014
  3.8 2.6 %collective-permute-start = (f32[272,128]{1,0:T(8,128)S(1)}, f32[272,128]{1,0:T(8,128)S(1)}, u32[]{:S(2)}, u32[]{:S(2)}) collective-permute-start(f32[272,128]{1,0:T(8,128)S(1)} %get-tuple-element.19), channel_id=1, source_target_pairs={{0,4},{4,0},{8,12},{12,8},{1,5},{5,1},{9,13},{13,9},{2,6},{6,2},{1... | collective-permute-start | bytes 417800 | tf_op jit(solution)/shard_map/ppermute | solution.py:1023
  6.4 0.7 %collective-permute-start.1 = (f32[272,128]{1,0:T(8,128)S(1)}, f32[272,128]{1,0:T(8,128)S(1)}, u32[]{:S(2)}, u32[]{:S(2)}) collective-permute-start(f32[272,128]{1,0:T(8,128)S(1)} %get-tuple-element.20), channel_id=1, source_target_pairs={{0,0},{4,8},{8,4},{12,12},{1,1},{5,9},{9,5},{13,13},{2,2},{6,10},{... | collective-permute-start | bytes 417800 | tf_op jit(solution)/shard_map/ppermute | solution.py:1023
  7.1 3.6 %collective-permute-done.refs_1_.refs_4_ = f32[272,128]{1,0:T(8,128)S(1)} collective-permute-done((f32[272,128]{1,0:T(8,128)S(1)}, f32[272,128]{1,0:T(8,128)S(1)}, u32[]{:S(2)}, u32[]{:S(2)}) %collective-permute-start) | collective-permute-done | bytes 139296 | tf_op jit(solution)/shard_map/ppermute | solution.py:1023
  10.7 0.0 collective-permute-start.3
  10.7 0.0 collective-permute-done.1.refs_2_.refs_5_
  10.7 0.5 %collective-permute-start.4 = (f32[272,128]{1,0:T(8,128)S(1)}, f32[272,128]{1,0:T(8,128)S(1)}, u32[]{:S(2)}, u32[]{:S(2)}) collective-permute-start(f32[272,128]{1,0:T(8,128)S(1)} %collective-permute-done.1.refs_2_.refs_5_), channel_id=1, source_target_pairs={{0,16},{16,0},{1,17},{17,1},{2,18},{18,2},{3,19},{19,3},{4,20},{20... | collective-permute-start | bytes 417800 | tf_op jit(solution)/shard_map/ppermute | solution.py:1014
  11.2 0.5 %shard_map.123 = (f32[10,2,16,128]{3,2,1,0:T(8,128)S(1)}, f32[2,40,128]{2,1,0:T(8,128)S(1)}) custom-call(f32[10,8,16,128]{3,2,1,0:T(8,128)S(1)} %shard_map.122.refs_0_.refs_1_.refs_6_, f32[272,128]{1,0:T(8,128)S(1)} %collective-permute-done.refs_1_.refs_4_, f32[272,128]{1,0:T(8,128)S(1)} %collective-permute-done.1.refs_2_.refs_5_), custom_call_target="tpu_custom_call" | custom-call | tf_op jit(solution)/shard_map/pallas_call | solution.py:1002
  11.7 0.4 %collective-permute-done.3.refs_3_.refs_6_.refs_8_ = f32[272,128]{1,0:T(8,128)S(1)} collective-permute-done((f32[272,128]{1,0:T(8,128)S(1)}, f32[272,128]{1,0:T(8,128)S(1)}, u32[]{:S(2)}, u32[]{:S(2)}) %collective-permute-start.3) | collective-permute-done | bytes 139296 | tf_op jit(solution)/shard_map/ppermute | solution.py:1014
  12.0 0.2 collective-permute-done.4.refs_4_.refs_7_.refs_9_
  12.2 0.0 collective-permute-done.2.refs_2_.refs_3_
  12.2 0.5 %shard_map.124 = (f32[10,4,16,128]{3,2,1,0:T(8,128)S(1)}, f32[4,40,128]{2,1,0:T(8,128)S(1)}) custom-call(f32[10,2,16,128]{3,2,1,0:T(8,128)S(1)} %get-tuple-element.21.refs_0_, f32[2,40,128]{2,1,0:T(8,128)S(1)} %get-tuple-element.22.refs_1_, f32[10,8,16,128]{3,2,1,0:T(8,128)S(1)} %collective-permute-done.2.refs_2_.refs_3_, ...), custom_call_target="tpu_custom_call" | custom-call | tf_op jit(solution)/shard_map/pallas_call | solution.py:1002
  12.7 1.7 %collective-permute-start.5 = (f32[4,40,128]{2,1,0:T(8,128)S(1)}, f32[4,40,128]{2,1,0:T(8,128)S(1)}, u32[]{:S(2)}, u32[]{:S(2)}) collective-permute-start(f32[4,40,128]{2,1,0:T(8,128)S(1)} %get-tuple-element.24), channel_id=1, source_target_pairs={{0,1},{1,2},{2,3},{3,0},{16,19},{17,16},{18,17},{19,18},{4,5},{5,6... | collective-permute-start | bytes 245768 | tf_op jit(solution)/shard_map/ppermute | solution.py:1122
  14.4 4.9 %shard_map.125 = (f32[3,18,24,128]{3,2,1,0:T(8,128)S(1)}, f32[18,24,128]{2,1,0:T(8,128)S(1)}, f32[18,24,128]{2,1,0:T(8,128)S(1)}, f32[9,18,24,128]{3,2,1,0:T(8,1...) custom-call(f32[8,128]{1,0:T(8,128)S(1)} %get-tuple-element.18.refs_7_.refs_0_, ...), custom_call_target="tpu_custom_call" | custom-call | tf_op jit(solution)/shard_map/pallas_call | solution.py:1002
  19.4 0.0 collective-permute-done.5.refs_2_
  19.4 1.7 %shard_map.126 = (f32[24,5,16,128]{3,2,1,0:T(8,128)S(1)}, f32[32,128]{1,0:T(8,128)S(1)}) custom-call(f32[8,128]{1,0:T(8,128)S(1)} %get-tuple-element.18.refs_7_.refs_0_, f32[10,4,16,128]{3,2,1,0:T(8,128)S(1)} %get-tuple-element.23.refs_1_, f32[4,40,128]{2,1,0:T(8,128)S(1)} %collective-permute-done.5.refs_2_, f32[32,8,128]{2,1,0:T(8,128)S(1)} %get-tuple-element.25.refs_3_), custom_call_target="tpu_custom_call" | custom-call | tf_op jit(solution)/shard_map/pallas_call | solution.py:1002
  21.1 1.0 %collective-permute-start.6 = (f32[24,5,16,128]{3,2,1,0:T(8,128)S(1)}, f32[24,5,16,128]{3,2,1,0:T(8,128)S(1)}, u32[]{:S(2)}, u32[]{:S(2)}) collective-permute-start(f32[24,5,16,128]{3,2,1,0:T(8,128)S(1)} %get-tuple-element.32.refs_7_), channel_id=1, source_target_pairs={{0,16},{16,0},{1,17},{17,1},{2,18},{18,2},{3,19},{19,3},{4,20},{20... | collective-permute-start | bytes 2949128 | tf_op jit(solution)/shard_map/ppermute | solution.py:1014
  22.1 13.0 %all_to_all.11 = f32[32,1,128]{2,1,0:T(1,128)S(1)} all-to-all(f32[32,1,128]{2,1,0:T(1,128)S(1)} %bitcast.5), channel_id=1, replica_groups=mesh['gx'=2,'gy'=4,'gz'=4] {'gx','gy','gz'}, dimensions={0} | all-to-all | bytes 32768 | tf_op jit(solution)/shard_map/all_to_all | solution.py:1173
  35.1 0.0 collective-permute-done.6.refs_8_
  35.1 1.3 %shard_map.127 = (f32[8,16,128]{2,1,0:T(8,128)}, f32[3,8,16,128]{3,2,1,0:T(8,128)}, f32[8,16,128]{2,1,0:T(8,128)}) custom-call(f32[32,128]{1,0:T(8,128)S(1)} %bitcast.4, f32[3,18,24,128]{3,2,1,0:T(8,128)S(1)} %get-tuple-element.27.refs_1_, f32[18,24,128]{2,1,0:T(8,128)S(1)} %get-tuple-element.28.refs_2_, f32[18,24,128]{2,1,0:T(8,128)S(1)} %get-tuple-element.29.refs_3_, ...), custom_call_target="tpu_custom_call" | custom-call | tf_op jit(solution)/shard_map/pallas_call | solution.py:1002
Async XLA Ops:
  3.2 9.0 %collective-permute-start.2 = (f32[10,8,16,128]{3,2,1,0:T(8,128)S(1)}, f32[10,8,16,128]{3,2,1,0:T(8,128)S(1)}, u32[]{:S(2)}, u32[]{:S(2)}) collective-permute-start(f32[10,8,16,128]{3,2,1,0:T(8,128)S(1)} %shard_map.122.refs_0_.refs_1_.refs_6_), channel_id=1, source_target_pairs={{0,16},{16,0},{1,17},{17,1},{2,18},{18,2},{3,19},{19,3},{4,20},{20... | collective-permute-start | bytes 1966088 | tf_op jit(solution)/shard_map/ppermute | solution.py:1014
  3.8 6.9 %collective-permute-start = (f32[272,128]{1,0:T(8,128)S(1)}, f32[272,128]{1,0:T(8,128)S(1)}, u32[]{:S(2)}, u32[]{:S(2)}) collective-permute-start(f32[272,128]{1,0:T(8,128)S(1)} %get-tuple-element.19), channel_id=1, source_target_pairs={{0,4},{4,0},{8,12},{12,8},{1,5},{5,1},{9,13},{13,9},{2,6},{6,2},{1... | collective-permute-start | bytes 417800 | tf_op jit(solution)/shard_map/ppermute | solution.py:1023
  6.4 4.3 %collective-permute-start.1 = (f32[272,128]{1,0:T(8,128)S(1)}, f32[272,128]{1,0:T(8,128)S(1)}, u32[]{:S(2)}, u32[]{:S(2)}) collective-permute-start(f32[272,128]{1,0:T(8,128)S(1)} %get-tuple-element.20), channel_id=1, source_target_pairs={{0,0},{4,8},{8,4},{12,12},{1,1},{5,9},{9,5},{13,13},{2,2},{6,10},{... | collective-permute-start | bytes 417800 | tf_op jit(solution)/shard_map/ppermute | solution.py:1023
  10.7 1.4 %collective-permute-start.3 = (f32[272,128]{1,0:T(8,128)S(1)}, f32[272,128]{1,0:T(8,128)S(1)}, u32[]{:S(2)}, u32[]{:S(2)}) collective-permute-start(f32[272,128]{1,0:T(8,128)S(1)} %collective-permute-done.refs_1_.refs_4_), channel_id=1, source_target_pairs={{0,16},{16,0},{1,17},{17,1},{2,18},{18,2},{3,19},{19,3},{4,20},{20... | collective-permute-start | bytes 417800 | tf_op jit(solution)/shard_map/ppermute | solution.py:1014
  10.7 1.6 %collective-permute-start.4 = (f32[272,128]{1,0:T(8,128)S(1)}, f32[272,128]{1,0:T(8,128)S(1)}, u32[]{:S(2)}, u32[]{:S(2)}) collective-permute-start(f32[272,128]{1,0:T(8,128)S(1)} %collective-permute-done.1.refs_2_.refs_5_), channel_id=1, source_target_pairs={{0,16},{16,0},{1,17},{17,1},{2,18},{18,2},{3,19},{19,3},{4,20},{20... | collective-permute-start | bytes 417800 | tf_op jit(solution)/shard_map/ppermute | solution.py:1014
  12.7 6.7 %collective-permute-start.5 = (f32[4,40,128]{2,1,0:T(8,128)S(1)}, f32[4,40,128]{2,1,0:T(8,128)S(1)}, u32[]{:S(2)}, u32[]{:S(2)}) collective-permute-start(f32[4,40,128]{2,1,0:T(8,128)S(1)} %get-tuple-element.24), channel_id=1, source_target_pairs={{0,1},{1,2},{2,3},{3,0},{16,19},{17,16},{18,17},{19,18},{4,5},{5,6... | collective-permute-start | bytes 245768 | tf_op jit(solution)/shard_map/ppermute | solution.py:1122
  21.1 14.0 %collective-permute-start.6 = (f32[24,5,16,128]{3,2,1,0:T(8,128)S(1)}, f32[24,5,16,128]{3,2,1,0:T(8,128)S(1)}, u32[]{:S(2)}, u32[]{:S(2)}) collective-permute-start(f32[24,5,16,128]{3,2,1,0:T(8,128)S(1)} %get-tuple-element.32.refs_7_), channel_id=1, source_target_pairs={{0,16},{16,0},{1,17},{17,1},{2,18},{18,2},{3,19},{19,3},{4,20},{20... | collective-permute-start | bytes 2949128 | tf_op jit(solution)/shard_map/ppermute | solution.py:1014
